TPU v7x, 32 devices: a whole 2x2x4 slice. The times are simulated.
32 devices in a mesh: ctx: 8 (over y, x, core), fsdp: 4 (over z).
Axes of the slice: x: 2, y: 2, z: 4, core: 2. Of those that a mesh axis runs over, the one named last changes fastest.
Arguments:
- hidden: bfloat16 [3, 8, 2, 256, 1024], P(None, 'fsdp', None, 'ctx'), may hold values from -6 to 6
- encoder_out: bfloat16 [8, 512, 1024], P('fsdp', 'ctx'), may hold values from -6 to 6
- out_grad: bfloat16 [3, 8, 2, 256, 1024], P(None, 'fsdp', None, 'ctx'), may hold values from -6 to 6
- slot_len: int32 [8], P('fsdp'), may hold values from 128 to 512, as said below
- enc_len: int32 [8], P('fsdp'), may hold values from 128 to 512, as said below
- rel_bucket: int32 [512], replicated, may hold values from 0 to 31, as said below
- query_weight: bfloat16 [1024, 1024], P('fsdp'), may hold values from -0.1875 to 0.1875
- key_weight: bfloat16 [1024, 1024], P('fsdp'), may hold values from -0.1875 to 0.1875
- value_weight: bfloat16 [1024, 1024], P('fsdp'), may hold values from -0.1875 to 0.1875
- relative_weight: bfloat16 [1024, 512], P('fsdp'), may hold values from -0.1875 to 0.1875
- output_weight: bfloat16 [1024, 1024], P('fsdp'), may hold values from -1 to 1
- self_norm_gain: bfloat16 [1024], P('fsdp'), may hold values from 0.5 to 1.5
- self_norm_shift: bfloat16 [1024], P('fsdp'), may hold values from -3 to 3
- cross_query_weight: bfloat16 [1024, 1024], P('fsdp'), may hold values from -0.1875 to 0.1875
- cross_key_weight: bfloat16 [1024, 1024], P('fsdp'), may hold values from -0.1875 to 0.1875
- cross_value_weight: bfloat16 [1024, 1024], P('fsdp'), may hold values from -0.1875 to 0.1875
- cross_output_weight: bfloat16 [1024, 1024], P('fsdp'), may hold values from -1 to 1
- cross_norm_gain: bfloat16 [1024], P('fsdp'), may hold values from 0.5 to 1.5
- cross_norm_shift: bfloat16 [1024], P('fsdp'), may hold values from -3 to 3
- up_weight: bfloat16 [1024, 4096], P('fsdp'), may hold values from -0.1875 to 0.1875
- down_weight: bfloat16 [4096, 1024], P('fsdp'), may hold values from -0.09375 to 0.09375
- feed_norm_gain: bfloat16 [1024], P('fsdp'), may hold values from 0.5 to 1.5
- feed_norm_shift: bfloat16 [1024], P('fsdp'), may hold values from -3 to 3
Outputs:
- layer_out: bfloat16 [3, 8, 2, 256, 1024], P(None, 'fsdp', None, 'ctx')
- hidden_grad: float32 [3, 8, 2, 256, 1024], P(None, 'fsdp', None, 'ctx')
- encoder_grad: float32 [8, 512, 1024], P('fsdp', 'ctx')
- grad_query_weight: float32 [1024, 1024], P('fsdp')
- grad_key_weight: float32 [1024, 1024], P('fsdp')
- grad_value_weight: float32 [1024, 1024], P('fsdp')
- grad_relative_weight: float32 [1024, 512], P('fsdp')
- grad_output_weight: float32 [1024, 1024], P('fsdp')
- grad_self_norm_gain: float32 [1024], P('fsdp')
- grad_self_norm_shift: float32 [1024], P('fsdp')
- grad_cross_query_weight: float32 [1024, 1024], P('fsdp')
- grad_cross_key_weight: float32 [1024, 1024], P('fsdp')
- grad_cross_value_weight: float32 [1024, 1024], P('fsdp')
- grad_cross_output_weight: float32 [1024, 1024], P('fsdp')
- grad_cross_norm_gain: float32 [1024], P('fsdp')
- grad_cross_norm_shift: float32 [1024], P('fsdp')
- grad_up_weight: float32 [1024, 4096], P('fsdp')
- grad_down_weight: float32 [4096, 1024], P('fsdp')
- grad_feed_norm_gain: float32 [1024], P('fsdp')
- grad_feed_norm_shift: float32 [1024], P('fsdp')
Inputs may be any that keep to these rules, and one draw needn't show every extreme that they name: `slot_len`: one slot in every draw is 512 long. `enc_len`: one slot in every draw has all 512 encoder rows. `rel_bucket`: entry d is the bucket of distance d: 0 at d = 0, never falling, rising by at most one from a distance to the next, and reaching 31 before d = 256.
All inputs are finite; a program needn't handle non-finite values.
Results may differ from a plain program's by a relative error of at most 0.03.
Values may be sent and summed in bfloat16 or wider, within the bound.
No kernel may reach another device: no remote copies, remote signals or barrier semaphores. Data moves between devices by JAX's collectives and lax.ppermute only.
A program may use at most 256 MiB of HBM per device.

v0:
```python
import jax
import jax.numpy as jnp
from jax import lax
from jax.sharding import PartitionSpec as P

HEAD_DIM = 64
BUCKETS = 32


eps_norm = 1e-05
neg_fill = -1e30


def layer_norm(values, norm_gain, norm_shift):
    row_mean = jnp.mean(values, axis=-1, keepdims=True)
    centered = values - row_mean
    variance = jnp.mean(centered * centered, axis=-1, keepdims=True)
    return centered * lax.rsqrt(variance + eps_norm) * norm_gain + norm_shift


def gelu_exact(values):
    return jax.nn.gelu(values, approximate=False)


def matmul(left_side, right_side):
    return jnp.dot(left_side, right_side, preferred_element_type=jnp.float32)


def matmul_back(left_side, right_side):
    return lax.dot_general(
        left_side, right_side, (((1,), (1,)), ((), ())), preferred_element_type=jnp.float32
    )


def outer_rows(left_side, right_side):
    return lax.dot_general(
        left_side, right_side, (((0,), (0,)), ((), ())), preferred_element_type=jnp.float32
    )


def norm_backward(values, norm_gain, norm_shift, cotangent):
    outputs, pullback = jax.vjp(layer_norm, values, norm_gain, norm_shift)
    return pullback(cotangent)


def soft_forward(scores, own_score):
    row_max = jnp.maximum(jnp.max(scores, axis=-1), own_score)
    exp_terms = jnp.exp(scores - row_max[..., None])
    own_exp = jnp.exp(own_score - row_max)
    row_sum = jnp.sum(exp_terms, axis=-1) + own_exp
    probs_low = (exp_terms / row_sum[..., None]).astype(jnp.bfloat16)
    own_low = (own_exp / row_sum).astype(jnp.bfloat16)
    return (probs_low, own_low, row_max + jnp.log(row_sum))


def soft_backward(scores, own_score, log_total, back_probs, back_own):
    probs = jnp.exp(scores - log_total[..., None])
    own_prob = jnp.exp(own_score - log_total)
    row_delta = jnp.sum(probs * back_probs, axis=-1) + own_prob * back_own
    back_scores = (probs * (back_probs - row_delta[..., None])).astype(jnp.bfloat16)
    back_own_score = (own_prob * (back_own - row_delta)).astype(jnp.bfloat16)
    return (probs.astype(jnp.bfloat16), own_prob.astype(jnp.bfloat16), back_scores, back_own_score)


def self_scores(
    lane, query_rows, embed_rows, key_own, key_main, one_hot, distance, key_valid, score_scale
):
    rel_bias = jnp.einsum("tbj,thb->thj", one_hot, embed_rows, preferred_element_type=jnp.float32)
    scores = (
        score_scale
        * jnp.einsum("the,jhe->thj", query_rows, key_main, preferred_element_type=jnp.float32)
        + rel_bias
    )
    if lane == 0:
        allowed = (distance >= 0) & key_valid[None, :]
        own_score = jnp.full(scores.shape[:2], neg_fill, jnp.float32)
    else:
        allowed = (distance > 0) & key_valid[None, :]
        own_score = score_scale * jnp.sum(
            query_rows.astype(jnp.float32) * key_own.astype(jnp.float32), axis=-1
        )
        own_score = own_score + embed_rows[:, :, 0].astype(jnp.float32)
    return (jnp.where(allowed[:, None, :], scores, neg_fill), own_score)


def fetch_all(
    query_weight,
    key_weight,
    value_weight,
    relative_weight,
    output_weight,
    self_norm_gain,
    self_norm_shift,
    cross_query_weight,
    cross_key_weight,
    cross_value_weight,
    cross_output_weight,
    cross_norm_gain,
    cross_norm_shift,
    up_weight,
    down_weight,
    feed_norm_gain,
    feed_norm_shift,
):
    self_set = (
        lax.all_gather(query_weight, "fsdp", axis=0, tiled=True),
        lax.all_gather(key_weight, "fsdp", axis=0, tiled=True),
        lax.all_gather(value_weight, "fsdp", axis=0, tiled=True),
        lax.all_gather(relative_weight, "fsdp", axis=0, tiled=True),
        lax.all_gather(output_weight, "fsdp", axis=0, tiled=True),
        lax.all_gather(self_norm_gain, "fsdp", axis=0, tiled=True),
        lax.all_gather(self_norm_shift, "fsdp", axis=0, tiled=True),
    )
    cross_set = (
        lax.all_gather(cross_query_weight, "fsdp", axis=0, tiled=True),
        lax.all_gather(cross_key_weight, "fsdp", axis=0, tiled=True),
        lax.all_gather(cross_value_weight, "fsdp", axis=0, tiled=True),
        lax.all_gather(cross_output_weight, "fsdp", axis=0, tiled=True),
        lax.all_gather(cross_norm_gain, "fsdp", axis=0, tiled=True),
        lax.all_gather(cross_norm_shift, "fsdp", axis=0, tiled=True),
    )
    feed_set = (
        lax.all_gather(up_weight, "fsdp", axis=0, tiled=True),
        lax.all_gather(down_weight, "fsdp", axis=0, tiled=True),
        lax.all_gather(feed_norm_gain, "fsdp", axis=0, tiled=True),
        lax.all_gather(feed_norm_shift, "fsdp", axis=0, tiled=True),
    )
    return (self_set, cross_set, feed_set)


def reduce_shards(grad_list):
    return (
        lax.psum_scatter(
            grad_list[0].astype(jnp.bfloat16), "fsdp", scatter_dimension=0, tiled=True
        ).astype(jnp.float32),
        lax.psum_scatter(
            grad_list[1].astype(jnp.bfloat16), "fsdp", scatter_dimension=0, tiled=True
        ).astype(jnp.float32),
        lax.psum_scatter(
            grad_list[2].astype(jnp.bfloat16), "fsdp", scatter_dimension=0, tiled=True
        ).astype(jnp.float32),
        lax.psum_scatter(
            grad_list[3].astype(jnp.bfloat16), "fsdp", scatter_dimension=0, tiled=True
        ).astype(jnp.float32),
        lax.psum_scatter(
            grad_list[4].astype(jnp.bfloat16), "fsdp", scatter_dimension=0, tiled=True
        ).astype(jnp.float32),
        lax.psum_scatter(
            grad_list[5].astype(jnp.bfloat16), "fsdp", scatter_dimension=0, tiled=True
        ).astype(jnp.float32),
        lax.psum_scatter(
            grad_list[6].astype(jnp.bfloat16), "fsdp", scatter_dimension=0, tiled=True
        ).astype(jnp.float32),
        lax.psum_scatter(
            grad_list[7].astype(jnp.bfloat16), "fsdp", scatter_dimension=0, tiled=True
        ).astype(jnp.float32),
        lax.psum_scatter(
            grad_list[8].astype(jnp.bfloat16), "fsdp", scatter_dimension=0, tiled=True
        ).astype(jnp.float32),
        lax.psum_scatter(
            grad_list[9].astype(jnp.bfloat16), "fsdp", scatter_dimension=0, tiled=True
        ).astype(jnp.float32),
        lax.psum_scatter(
            grad_list[10].astype(jnp.bfloat16), "fsdp", scatter_dimension=0, tiled=True
        ).astype(jnp.float32),
        lax.psum_scatter(
            grad_list[11].astype(jnp.bfloat16), "fsdp", scatter_dimension=0, tiled=True
        ).astype(jnp.float32),
        lax.psum_scatter(
            grad_list[12].astype(jnp.bfloat16), "fsdp", scatter_dimension=0, tiled=True
        ).astype(jnp.float32),
        lax.psum_scatter(
            grad_list[13].astype(jnp.bfloat16), "fsdp", scatter_dimension=0, tiled=True
        ).astype(jnp.float32),
        lax.psum_scatter(
            grad_list[14].astype(jnp.bfloat16), "fsdp", scatter_dimension=0, tiled=True
        ).astype(jnp.float32),
        lax.psum_scatter(
            grad_list[15].astype(jnp.bfloat16), "fsdp", scatter_dimension=0, tiled=True
        ).astype(jnp.float32),
        lax.psum_scatter(
            grad_list[16].astype(jnp.bfloat16), "fsdp", scatter_dimension=0, tiled=True
        ).astype(jnp.float32),
    )


def on_device(
    hidden,
    encoder_out,
    out_grad,
    slot_len,
    enc_len,
    rel_bucket,
    query_weight,
    key_weight,
    value_weight,
    relative_weight,
    output_weight,
    self_norm_gain,
    self_norm_shift,
    cross_query_weight,
    cross_key_weight,
    cross_value_weight,
    cross_output_weight,
    cross_norm_gain,
    cross_norm_shift,
    up_weight,
    down_weight,
    feed_norm_gain,
    feed_norm_shift,
):
    lane_count, micro_count, half_count, half_rows, model_width = hidden.shape
    head_count = model_width // HEAD_DIM
    score_scale = HEAD_DIM ** (-0.5)
    ctx_count = lax.axis_size("ctx")
    seq_len = half_count * half_rows * ctx_count
    row_count = half_count * half_rows
    all_rows = lane_count * row_count
    local_rows = lax.axis_index("ctx") * half_rows + jnp.arange(half_rows, dtype=jnp.int32)
    positions = jnp.concatenate([local_rows, seq_len - 1 - local_rows])
    whole_rows = jnp.arange(seq_len // 2, dtype=jnp.int32)
    key_positions = jnp.concatenate([whole_rows, seq_len - 1 - whole_rows])
    distance = positions[:, None] - key_positions[None, :]
    levels = jnp.arange(BUCKETS + 1, dtype=jnp.int32)
    bounds = jnp.sum((rel_bucket[None, :] < levels[:, None]).astype(jnp.int32), axis=1)
    one_hot = (
        (distance[:, None, :] >= bounds[None, :BUCKETS, None])
        & (distance[:, None, :] < bounds[None, 1:, None])
    ).astype(jnp.bfloat16)
    out_list = []
    hidden_list = []
    encoder_list = []
    grad_total = None
    shard_total = None
    for micro_index in range(micro_count):
        current = fetch_all(
            query_weight,
            key_weight,
            value_weight,
            relative_weight,
            output_weight,
            self_norm_gain,
            self_norm_shift,
            cross_query_weight,
            cross_key_weight,
            cross_value_weight,
            cross_output_weight,
            cross_norm_gain,
            cross_norm_shift,
            up_weight,
            down_weight,
            feed_norm_gain,
            feed_norm_shift,
        )
        query_full, key_full, value_full, relative_full, output_full, gain_one, shift_one = current[
            0
        ]
        cquery_full, ckey_full, cvalue_full, coutput_full, gain_two, shift_two = current[1]
        up_full, down_full, gain_three, shift_three = current[2]
        gain_one = gain_one.astype(jnp.float32)
        shift_one = shift_one.astype(jnp.float32)
        gain_two = gain_two.astype(jnp.float32)
        shift_two = shift_two.astype(jnp.float32)
        gain_three = gain_three.astype(jnp.float32)
        shift_three = shift_three.astype(jnp.float32)
        length = slot_len[micro_index]
        enc_length = enc_len[micro_index]
        x_low = hidden[:, micro_index].reshape(lane_count, row_count, model_width)
        x_flat = x_low.reshape(all_rows, model_width)
        lane_shape = (lane_count, row_count, head_count, HEAD_DIM)
        query_all = matmul(x_flat, query_full).astype(jnp.bfloat16).reshape(lane_shape)
        key_all = matmul(x_flat, key_full).astype(jnp.bfloat16).reshape(lane_shape)
        value_all = matmul(x_flat, value_full).astype(jnp.bfloat16).reshape(lane_shape)
        embed_all = (
            matmul(x_flat, relative_full)
            .astype(jnp.bfloat16)
            .reshape(lane_count, row_count, head_count, BUCKETS)
        )
        key_main = lax.all_gather(
            key_all[0].reshape(half_count, half_rows, model_width), "ctx", axis=1, tiled=True
        )
        value_main = lax.all_gather(
            value_all[0].reshape(half_count, half_rows, model_width), "ctx", axis=1, tiled=True
        )
        key_main = key_main.reshape(seq_len, head_count, HEAD_DIM)
        value_main = value_main.reshape(seq_len, head_count, HEAD_DIM)
        key_valid = key_positions < length
        attended_list = []
        log_list = []
        for lane in range(lane_count):
            scores, own_score = self_scores(
                lane,
                query_all[lane],
                embed_all[lane],
                key_all[lane],
                key_main,
                one_hot,
                distance,
                key_valid,
                score_scale,
            )
            probs_low, own_low, log_total = soft_forward(scores, own_score)
            mixed = jnp.einsum(
                "thj,jhe->the", probs_low, value_main, preferred_element_type=jnp.float32
            )
            mixed = mixed + own_low.astype(jnp.float32)[..., None] * value_all[lane].astype(
                jnp.float32
            )
            attended_list.append(mixed.astype(jnp.bfloat16))
            log_list.append(log_total)
        attended = jnp.stack(attended_list).reshape(all_rows, model_width)
        full_shape = (lane_count, row_count, model_width)
        resid_one = x_low.astype(jnp.float32) + matmul(attended, output_full).reshape(full_shape)
        normed_one = layer_norm(resid_one, gain_one, shift_one)
        normed_one_low = normed_one.astype(jnp.bfloat16).reshape(all_rows, model_width)
        enc_local = encoder_out[micro_index]
        enc_key = lax.all_gather(
            matmul(enc_local, ckey_full).astype(jnp.bfloat16), "ctx", axis=0, tiled=True
        )
        enc_value = lax.all_gather(
            matmul(enc_local, cvalue_full).astype(jnp.bfloat16), "ctx", axis=0, tiled=True
        )
        enc_key = enc_key.reshape(-1, head_count, HEAD_DIM)
        enc_value = enc_value.reshape(-1, head_count, HEAD_DIM)
        cross_query = (
            matmul(normed_one_low, cquery_full)
            .astype(jnp.bfloat16)
            .reshape(all_rows, head_count, HEAD_DIM)
        )
        enc_valid = jnp.arange(enc_key.shape[0], dtype=jnp.int32) < enc_length
        cross_scores = score_scale * jnp.einsum(
            "the,jhe->thj", cross_query, enc_key, preferred_element_type=jnp.float32
        )
        cross_scores = jnp.where(enc_valid[None, None, :], cross_scores, neg_fill)
        no_own = jnp.full((all_rows, head_count), neg_fill, jnp.float32)
        cross_probs, cross_own, cross_log = soft_forward(cross_scores, no_own)
        cross_attended = jnp.einsum(
            "thj,jhe->the", cross_probs, enc_value, preferred_element_type=jnp.float32
        )
        cross_attended = cross_attended.astype(jnp.bfloat16).reshape(all_rows, model_width)
        resid_two = normed_one + matmul(cross_attended, coutput_full).reshape(full_shape)
        normed_two = layer_norm(resid_two, gain_two, shift_two)
        normed_two_low = normed_two.astype(jnp.bfloat16).reshape(all_rows, model_width)
        pre_act = matmul(normed_two_low, up_full)
        act_low = gelu_exact(pre_act).astype(jnp.bfloat16)
        resid_three = normed_two + matmul(act_low, down_full).reshape(full_shape)
        layer_out = layer_norm(resid_three, gain_three, shift_three).astype(jnp.bfloat16)
        row_valid = (positions < length).astype(jnp.float32)
        cotangent = (
            out_grad[:, micro_index].reshape(full_shape).astype(jnp.float32)
            * row_valid[None, :, None]
        )
        back_resid_three, grad_gain_three, grad_shift_three = norm_backward(
            resid_three, gain_three, shift_three, cotangent
        )
        back_feed = back_resid_three.astype(jnp.bfloat16).reshape(all_rows, model_width)
        grad_down = outer_rows(act_low, back_feed)
        back_act = matmul_back(back_feed, down_full)
        act_unused, gelu_pull = jax.vjp(gelu_exact, pre_act)
        back_pre = gelu_pull(back_act)[0].astype(jnp.bfloat16)
        grad_up = outer_rows(normed_two_low, back_pre)
        back_normed_two = back_resid_three + matmul_back(back_pre, up_full).reshape(full_shape)
        back_resid_two, grad_gain_two, grad_shift_two = norm_backward(
            resid_two, gain_two, shift_two, back_normed_two
        )
        back_cross = back_resid_two.astype(jnp.bfloat16).reshape(all_rows, model_width)
        grad_coutput = outer_rows(cross_attended, back_cross)
        back_cross_att = (
            matmul_back(back_cross, coutput_full)
            .astype(jnp.bfloat16)
            .reshape(all_rows, head_count, HEAD_DIM)
        )
        back_cprobs = jnp.einsum(
            "the,jhe->thj", back_cross_att, enc_value, preferred_element_type=jnp.float32
        )
        zero_own = jnp.zeros((all_rows, head_count), jnp.float32)
        cprobs_low, cown_low, back_cscores, back_cown = soft_backward(
            cross_scores, no_own, cross_log, back_cprobs, zero_own
        )
        back_cquery = score_scale * jnp.einsum(
            "thj,jhe->the", back_cscores, enc_key, preferred_element_type=jnp.float32
        )
        back_cquery = back_cquery.astype(jnp.bfloat16).reshape(all_rows, model_width)
        part_key = score_scale * jnp.einsum(
            "thj,the->jhe", back_cscores, cross_query, preferred_element_type=jnp.float32
        )
        part_value = jnp.einsum(
            "thj,the->jhe", cprobs_low, back_cross_att, preferred_element_type=jnp.float32
        )
        back_enc_key = lax.psum_scatter(
            part_key.reshape(-1, model_width).astype(jnp.bfloat16),
            "ctx",
            scatter_dimension=0,
            tiled=True,
        ).astype(jnp.float32)
        back_enc_value = lax.psum_scatter(
            part_value.reshape(-1, model_width).astype(jnp.bfloat16),
            "ctx",
            scatter_dimension=0,
            tiled=True,
        ).astype(jnp.float32)
        back_enc_key = back_enc_key.astype(jnp.bfloat16)
        back_enc_value = back_enc_value.astype(jnp.bfloat16)
        grad_ckey = outer_rows(enc_local, back_enc_key)
        grad_cvalue = outer_rows(enc_local, back_enc_value)
        encoder_grad = matmul_back(back_enc_key, ckey_full) + matmul_back(
            back_enc_value, cvalue_full
        )
        grad_cquery = outer_rows(normed_one_low, back_cquery)
        back_normed_one = back_resid_two + matmul_back(back_cquery, cquery_full).reshape(full_shape)
        back_resid_one, grad_gain_one, grad_shift_one = norm_backward(
            resid_one, gain_one, shift_one, back_normed_one
        )
        back_self = back_resid_one.astype(jnp.bfloat16).reshape(all_rows, model_width)
        grad_output = outer_rows(attended, back_self)
        back_attended = matmul_back(back_self, output_full).astype(jnp.bfloat16).reshape(lane_shape)
        key_main_grad = jnp.zeros((seq_len, head_count, HEAD_DIM), jnp.float32)
        value_main_grad = jnp.zeros((seq_len, head_count, HEAD_DIM), jnp.float32)
        query_list = []
        embed_list = []
        key_self_list = []
        value_self_list = []
        for lane in range(lane_count):
            scores, own_score = self_scores(
                lane,
                query_all[lane],
                embed_all[lane],
                key_all[lane],
                key_main,
                one_hot,
                distance,
                key_valid,
                score_scale,
            )
            back_probs = jnp.einsum(
                "the,jhe->thj", back_attended[lane], value_main, preferred_element_type=jnp.float32
            )
            back_own = jnp.sum(
                back_attended[lane].astype(jnp.float32) * value_all[lane].astype(jnp.float32),
                axis=-1,
            )
            probs_low, own_low, back_scores, back_own_score = soft_backward(
                scores, own_score, log_list[lane], back_probs, back_own
            )
            own_term = back_own_score.astype(jnp.float32)
            back_query = jnp.einsum(
                "thj,jhe->the", back_scores, key_main, preferred_element_type=jnp.float32
            )
            back_query = score_scale * (
                back_query + own_term[..., None] * key_all[lane].astype(jnp.float32)
            )
            key_main_grad = key_main_grad + score_scale * jnp.einsum(
                "thj,the->jhe", back_scores, query_all[lane], preferred_element_type=jnp.float32
            )
            value_main_grad = value_main_grad + jnp.einsum(
                "thj,the->jhe", probs_low, back_attended[lane], preferred_element_type=jnp.float32
            )
            back_embed = jnp.einsum(
                "thj,tbj->thb", back_scores, one_hot, preferred_element_type=jnp.float32
            )
            back_embed = back_embed.at[:, :, 0].add(own_term)
            query_list.append(back_query.astype(jnp.bfloat16))
            embed_list.append(back_embed.astype(jnp.bfloat16))
            if lane > 0:
                key_self_list.append(
                    score_scale * own_term[..., None] * query_all[lane].astype(jnp.float32)
                )
                value_self_list.append(
                    own_low.astype(jnp.float32)[..., None] * back_attended[lane].astype(jnp.float32)
                )
        back_key_main = lax.psum_scatter(
            key_main_grad.reshape(half_count, seq_len // 2, model_width).astype(jnp.bfloat16),
            "ctx",
            scatter_dimension=1,
            tiled=True,
        ).astype(jnp.float32)
        back_value_main = lax.psum_scatter(
            value_main_grad.reshape(half_count, seq_len // 2, model_width).astype(jnp.bfloat16),
            "ctx",
            scatter_dimension=1,
            tiled=True,
        ).astype(jnp.float32)
        head_shape = (row_count, head_count, HEAD_DIM)
        back_key = jnp.stack([back_key_main.reshape(head_shape)] + key_self_list).astype(
            jnp.bfloat16
        )
        back_value = jnp.stack([back_value_main.reshape(head_shape)] + value_self_list).astype(
            jnp.bfloat16
        )
        back_key = back_key.reshape(all_rows, model_width)
        back_value = back_value.reshape(all_rows, model_width)
        back_query_all = jnp.stack(query_list).reshape(all_rows, model_width)
        back_embed_all = jnp.stack(embed_list).reshape(all_rows, head_count * BUCKETS)
        grad_query = outer_rows(x_flat, back_query_all)
        grad_key = outer_rows(x_flat, back_key)
        grad_value = outer_rows(x_flat, back_value)
        grad_relative = outer_rows(x_flat, back_embed_all)
        input_terms = (
            matmul_back(back_query_all, query_full)
            + matmul_back(back_key, key_full)
            + matmul_back(back_value, value_full)
            + matmul_back(back_embed_all, relative_full)
        )
        hidden_grad = back_resid_one + input_terms.reshape(full_shape)
        weight_grads = (
            grad_query,
            grad_key,
            grad_value,
            grad_relative,
            grad_output,
            grad_gain_one,
            grad_shift_one,
            grad_cquery,
            grad_ckey,
            grad_cvalue,
            grad_coutput,
            grad_gain_two,
            grad_shift_two,
            grad_up,
            grad_down,
            grad_gain_three,
            grad_shift_three,
        )
        slab_shape = (lane_count, half_count, half_rows, model_width)
        layer_out, hidden_grad, encoder_grad, weight_grads = (
            layer_out.reshape(slab_shape),
            hidden_grad.reshape(slab_shape),
            encoder_grad,
            weight_grads,
        )
        out_list.append(layer_out)
        hidden_list.append(hidden_grad)
        encoder_list.append(encoder_grad)
        if micro_index == 0:
            grad_total = weight_grads
        else:
            grad_total = tuple(
                (left_item + right_item for left_item, right_item in zip(grad_total, weight_grads))
            )
    shard_total = reduce_shards(grad_total)
    totals = (
        lax.psum(shard_total[0].astype(jnp.bfloat16), "ctx").astype(jnp.float32),
        lax.psum(shard_total[1].astype(jnp.bfloat16), "ctx").astype(jnp.float32),
        lax.psum(shard_total[2].astype(jnp.bfloat16), "ctx").astype(jnp.float32),
        lax.psum(shard_total[3].astype(jnp.bfloat16), "ctx").astype(jnp.float32),
        lax.psum(shard_total[4].astype(jnp.bfloat16), "ctx").astype(jnp.float32),
        lax.psum(shard_total[5].astype(jnp.bfloat16), "ctx").astype(jnp.float32),
        lax.psum(shard_total[6].astype(jnp.bfloat16), "ctx").astype(jnp.float32),
        lax.psum(shard_total[7].astype(jnp.bfloat16), "ctx").astype(jnp.float32),
        lax.psum(shard_total[8].astype(jnp.bfloat16), "ctx").astype(jnp.float32),
        lax.psum(shard_total[9].astype(jnp.bfloat16), "ctx").astype(jnp.float32),
        lax.psum(shard_total[10].astype(jnp.bfloat16), "ctx").astype(jnp.float32),
        lax.psum(shard_total[11].astype(jnp.bfloat16), "ctx").astype(jnp.float32),
        lax.psum(shard_total[12].astype(jnp.bfloat16), "ctx").astype(jnp.float32),
        lax.psum(shard_total[13].astype(jnp.bfloat16), "ctx").astype(jnp.float32),
        lax.psum(shard_total[14].astype(jnp.bfloat16), "ctx").astype(jnp.float32),
        lax.psum(shard_total[15].astype(jnp.bfloat16), "ctx").astype(jnp.float32),
        lax.psum(shard_total[16].astype(jnp.bfloat16), "ctx").astype(jnp.float32),
    )
    return (
        jnp.stack(out_list, axis=1),
        jnp.stack(hidden_list, axis=1),
        jnp.stack(encoder_list, axis=0),
    ) + tuple(totals)


def solution(mesh):
    placed = (
        P(None, "fsdp", None, "ctx", None),
        P("fsdp", "ctx", None),
        P(None, "fsdp", None, "ctx", None),
        P("fsdp"),
        P("fsdp"),
        P(),
        P("fsdp", None),
        P("fsdp", None),
        P("fsdp", None),
        P("fsdp", None),
        P("fsdp", None),
        P("fsdp"),
        P("fsdp"),
        P("fsdp", None),
        P("fsdp", None),
        P("fsdp", None),
        P("fsdp", None),
        P("fsdp"),
        P("fsdp"),
        P("fsdp", None),
        P("fsdp", None),
        P("fsdp"),
        P("fsdp"),
    )
    return jax.shard_map(
        on_device,
        mesh=mesh,
        in_specs=placed,
        out_specs=(
            P(None, "fsdp", None, "ctx", None),
            P(None, "fsdp", None, "ctx", None),
            P("fsdp", "ctx", None),
            P("fsdp", None),
            P("fsdp", None),
            P("fsdp", None),
            P("fsdp", None),
            P("fsdp", None),
            P("fsdp"),
            P("fsdp"),
            P("fsdp", None),
            P("fsdp", None),
            P("fsdp", None),
            P("fsdp", None),
            P("fsdp"),
            P("fsdp"),
            P("fsdp", None),
            P("fsdp", None),
            P("fsdp"),
            P("fsdp"),
        ),
        check_vma=False,
    )
```

profile of v0, /device:TPU:0, one launch (start us, length us, event | category | flops | bytes accessed | tf_op | source)
XLA Modules:
  0.0 2183.8 jit_solution(16944726912514255110)
XLA Ops:
  11.3 47.0 %all-gather.26.cloned.1.call-done = bf16[1024,1024]{1,0:T(8,128)(2,1)} async-done(((bf16[256,1024]{1,0:T(8,128)(2,1)}), bf16[1024,1024]{1,0:T(8,128)(2,1)}) %all-gather.26.cloned.1.call-update) | async-done | bytes 2097168 | tf_op jit(solution)/shard_map/all_gather | solution.py:108
  61.5 43.1 %all-gather.30.cloned.1.call-done = bf16[1024,1024]{1,0:T(8,128)(2,1)} async-done(((bf16[256,1024]{1,0:T(8,128)(2,1)}), bf16[1024,1024]{1,0:T(8,128)(2,1)}) %all-gather.30.cloned.1.call-update) | async-done | bytes 2097168 | tf_op jit(solution)/shard_map/all_gather | solution.py:107
  113.9 36.9 %all-gather.40.cloned.1.call-done = bf16[1024,1024]{1,0:T(8,128)(2,1)} async-done(((bf16[256,1024]{1,0:T(8,128)(2,1)}), bf16[1024,1024]{1,0:T(8,128)(2,1)}) %all-gather.40.cloned.1.call-update) | async-done | bytes 2097168 | tf_op jit(solution)/shard_map/all_gather | solution.py:117
  153.7 43.2 %all-gather.44.cloned.1.call-done = bf16[1024,1024]{1,0:T(8,128)(2,1)} async-done(((bf16[256,1024]{1,0:T(8,128)(2,1)}), bf16[1024,1024]{1,0:T(8,128)(2,1)}) %all-gather.44.cloned.1.call-update) | async-done | bytes 2097168 | tf_op jit(solution)/shard_map/all_gather | solution.py:116
  353.4 19.1 all-gather.58.cloned.1.call-done
  424.8 41.4 %all-gather.48.cloned.1.call-done = bf16[1024,1024]{1,0:T(8,128)(2,1)} async-done(((bf16[256,1024]{1,0:T(8,128)(2,1)}), bf16[1024,1024]{1,0:T(8,128)(2,1)}) %all-gather.48.cloned.1.call-update) | async-done | bytes 2097168 | tf_op jit(solution)/shard_map/all_gather | solution.py:115
  468.6 21.7 all-gather.42.cloned.1.call-done
  491.8 23.7 %all-gather.46.cloned.1.call-done = bf16[512,1024]{1,0:T(8,128)(2,1)} async-done(((bf16[64,1024]{1,0:T(8,128)(2,1)}), bf16[512,1024]{1,0:T(8,128)(2,1)}) %all-gather.46.cloned.1.call-update) | async-done | bytes 1048592 | tf_op jit(solution)/shard_map/all_gather | solution.py:317
  543.1 23.0 %all-gather.62.cloned.1.call-done = bf16[512,1024]{1,0:T(8,128)(2,1)} async-done(((bf16[64,1024]{1,0:T(8,128)(2,1)}), bf16[512,1024]{1,0:T(8,128)(2,1)}) %all-gather.62.cloned.1.call-update) | async-done | bytes 1048592 | tf_op jit(solution)/shard_map/all_gather | solution.py:317
  577.1 36.3 %all-gather.50.cloned.1.call-done = bf16[1024,1024]{1,0:T(8,128)(2,1)} async-done(((bf16[256,1024]{1,0:T(8,128)(2,1)}), bf16[1024,1024]{1,0:T(8,128)(2,1)}) %all-gather.50.cloned.1.call-update) | async-done | bytes 2097168 | tf_op jit(solution)/shard_map/all_gather | solution.py:118
  618.6 144.6 %all-gather.52.cloned.1.call-done = bf16[1024,4096]{1,0:T(8,128)(2,1)} async-done(((bf16[256,4096]{1,0:T(8,128)(2,1)}), bf16[1024,4096]{1,0:T(8,128)(2,1)}) %all-gather.52.cloned.1.call-update) | async-done | bytes 8388624 | tf_op jit(solution)/shard_map/all_gather | solution.py:123
  775.7 137.0 %all-gather.54.cloned.1.call-done = bf16[4096,1024]{1,0:T(8,128)(2,1)} async-done(((bf16[1024,1024]{1,0:T(8,128)(2,1)}), bf16[4096,1024]{1,0:T(8,128)(2,1)}) %all-gather.54.cloned.1.call-update) | async-done | bytes 8388624 | tf_op jit(solution)/shard_map/all_gather | solution.py:124
  1257.3 72.0 %all-reduce.19.cloned.1.call-done = (bf16[2,256,1024]{2,0,1:T(2,128)(2,1)}, bf16[2,256,1024]{2,0,1:T(2,128)(2,1)}, bf16[2,256,1024]{2,0,1:T(2,128)(2,1)}, bf16[2,256,1024]{2,0,1:T(2,128)(2,1)}) async-done(((bf16[2,256,1024]{2,0,1:T(2,128)(2,1)}, bf16[2,256,1024]{2,0,1:T(2,128)(2,1)}, bf16[2,256,1024]{2,0,1:T(2,128)(2,1)}, bf16[2,256,1024]{2,0,1:T(2,128)(2,1)}), (bf16[2,256,1024]{2,0,1:T(2,128)(2,1)}, ...) | async-done | bytes 4194320
  1411.0 19.8 all-reduce.13
  1431.3 12.9 all-reduce.10
  1450.7 45.4 %reduce-scatter.34.cloned.1.call-done = bf16[256,1024]{1,0:T(8,128)(2,1)} async-done(((bf16[1024,1024]{1,0:T(8,128)(2,1)}), bf16[256,1024]{1,0:T(8,128)(2,1)}) %reduce-scatter.34.cloned.1.call-update) | async-done | bytes 524304 | tf_op jit(solution)/shard_map/reduce_scatter | solution.py:154
  1496.2 45.6 %reduce-scatter.40.cloned.1.call-done = bf16[256,1024]{1,0:T(8,128)(2,1)} async-done(((bf16[1024,1024]{1,0:T(8,128)(2,1)}), bf16[256,1024]{1,0:T(8,128)(2,1)}) %reduce-scatter.40.cloned.1.call-update) | async-done | bytes 524304 | tf_op jit(solution)/shard_map/reduce_scatter | solution.py:163
  1541.8 45.4 %reduce-scatter.36.cloned.1.call-done = bf16[256,1024]{0,1:T(8,128)(2,1)} async-done(((bf16[1024,1024]{0,1:T(8,128)(2,1)}), bf16[256,1024]{0,1:T(8,128)(2,1)}) %reduce-scatter.36.cloned.1.call-update) | async-done | bytes 524304 | tf_op jit(solution)/shard_map/reduce_scatter | solution.py:157
  1587.2 45.6 %reduce-scatter.38.cloned.1.call-done = bf16[256,1024]{0,1:T(8,128)(2,1)} async-done(((bf16[1024,1024]{0,1:T(8,128)(2,1)}), bf16[256,1024]{0,1:T(8,128)(2,1)}) %reduce-scatter.38.cloned.1.call-update) | async-done | bytes 524304 | tf_op jit(solution)/shard_map/reduce_scatter | solution.py:160
  1632.8 46.1 %reduce-scatter.26.cloned.1.call-done = bf16[256,1024]{0,1:T(8,128)(2,1)} async-done(((bf16[1024,1024]{0,1:T(8,128)(2,1)}), bf16[256,1024]{0,1:T(8,128)(2,1)}) %reduce-scatter.26.cloned.1.call-update) | async-done | bytes 524304 | tf_op jit(solution)/shard_map/reduce_scatter | solution.py:136
  1678.9 45.4 %reduce-scatter.28.cloned.1.call-done = bf16[256,1024]{0,1:T(8,128)(2,1)} async-done(((bf16[1024,1024]{0,1:T(8,128)(2,1)}), bf16[256,1024]{0,1:T(8,128)(2,1)}) %reduce-scatter.28.cloned.1.call-update) | async-done | bytes 524304 | tf_op jit(solution)/shard_map/reduce_scatter | solution.py:139
  1724.3 146.2 %reduce-scatter.42.cloned.1.call-done = bf16[256,4096]{1,0:T(8,128)(2,1)} async-done(((bf16[1024,4096]{1,0:T(8,128)(2,1)}), bf16[256,4096]{1,0:T(8,128)(2,1)}) %reduce-scatter.42.cloned.1.call-update) | async-done | bytes 2097168 | tf_op jit(solution)/shard_map/reduce_scatter | solution.py:172
  1870.5 147.6 %reduce-scatter.44.cloned.1.call-done = bf16[1024,1024]{1,0:T(8,128)(2,1)} async-done(((bf16[4096,1024]{1,0:T(8,128)(2,1)}), bf16[1024,1024]{1,0:T(8,128)(2,1)}) %reduce-scatter.44.cloned.1.call-update) | async-done | bytes 2097168 | tf_op jit(solution)/shard_map/reduce_scatter | solution.py:175
  2034.4 123.9 %all-reduce.17.cloned.1.call-done = (bf16[256,1024]{0,1:T(8,128)(2,1)}, bf16[256,1024]{0,1:T(8,128)(2,1)}, bf16[256,1024]{0,1:T(8,128)(2,1)}, bf16[256,512]{0,1:...) async-done(((bf16[256,1024]{0,1:T(8,128)(2,1)}, ...) | async-done | bytes 8650768 | tf_op jit(solution)/shard_map/psum | solution.py:542
  (1400 shorter events, 750.2 us)
Async XLA Ops:
  10.6 281.6 %all-gather.34.cloned.1.call-start = ((), (), s32[]{:S(2)}) async-start(), calls=%async_computation.19 | async-start | bytes 2621440 | tf_op jit(solution)/shard_map/all_gather | solution.py:106
  11.2 313.3 %all-gather.28.cloned.1.call-start = ((), (), s32[]{:S(2)}) async-start(), calls=%async_computation.16 | async-start | bytes 1179648 | tf_op jit(solution)/shard_map/all_gather | solution.py:282
  61.4 267.0 %all-gather.32.cloned.1.call-start = ((), (), s32[]{:S(2)}) async-start(), calls=%async_computation.18 | async-start | bytes 1179648 | tf_op jit(solution)/shard_map/all_gather | solution.py:279
  109.3 263.2 %all-gather.58.cloned.1.call-start = ((), (), s32[]{:S(2)}) async-start(), calls=%async_computation.31 | async-start | bytes 1179648 | tf_op jit(solution)/shard_map/all_gather | solution.py:279
  112.5 307.5 %all-gather.38.cloned.1.call-start = ((), (), s32[]{:S(2)}) async-start(), calls=%async_computation.21 | async-start | bytes 2621440 | tf_op jit(solution)/shard_map/all_gather | solution.py:110
  113.3 352.9 %all-gather.48.cloned.1.call-start = ((), (), s32[]{:S(2)}) async-start(), calls=%async_computation.26 | async-start | bytes 2621440 | tf_op jit(solution)/shard_map/all_gather | solution.py:115
  113.8 376.4 %all-gather.42.cloned.1.call-start = ((), (), s32[]{:S(2)}) async-start(), calls=%async_computation.23 | async-start | bytes 1179648 | tf_op jit(solution)/shard_map/all_gather | solution.py:320
  153.7 361.8 %all-gather.46.cloned.1.call-start = ((), (), s32[]{:S(2)}) async-start(), calls=%async_computation.25 | async-start | bytes 1179648 | tf_op jit(solution)/shard_map/all_gather | solution.py:317
  199.7 341.1 %all-gather.60.cloned.1.call-start = ((), (), s32[]{:S(2)}) async-start(), calls=%async_computation.32 | async-start | bytes 1179648 | tf_op jit(solution)/shard_map/all_gather | solution.py:320
  200.9 365.2 %all-gather.62.cloned.1.call-start = ((), (), s32[]{:S(2)}) async-start(), calls=%async_computation.33 | async-start | bytes 1179648 | tf_op jit(solution)/shard_map/all_gather | solution.py:317
  203.7 409.7 %all-gather.50.cloned.1.call-start = ((), (), s32[]{:S(2)}) async-start(), calls=%async_computation.27 | async-start | bytes 2621440 | tf_op jit(solution)/shard_map/all_gather | solution.py:118
  204.4 558.8 %all-gather.52.cloned.1.call-start = ((), (), s32[]{:S(2)}) async-start(), calls=%async_computation.28 | async-start | bytes 10485760 | tf_op jit(solution)/shard_map/all_gather | solution.py:123
  205.0 707.7 %all-gather.54.cloned.1.call-start = ((), (), s32[]{:S(2)}) async-start(), calls=%async_computation.29 | async-start | bytes 10485760 | tf_op jit(solution)/shard_map/all_gather | solution.py:124
  205.7 1024.2 %reduce-scatter.46.cloned.1.call-start = ((), (), s32[]{:S(2)}) async-start(), calls=%async_computation.45 | async-start | bytes 1179648
  1177.6 270.9 %reduce-scatter.30.cloned.1.call-start = ((), (), s32[]{:S(2)}) async-start(), calls=%async_computation.37 | async-start | bytes 1310720 | tf_op jit(solution)/shard_map/reduce_scatter | solution.py:142
  1220.8 275.4 %reduce-scatter.34.cloned.1.call-start = ((), (), s32[]{:S(2)}) async-start(), calls=%async_computation.39 | async-start | bytes 2621440 | tf_op jit(solution)/shard_map/reduce_scatter | solution.py:154
  1225.2 316.5 %reduce-scatter.40.cloned.1.call-start = ((), (), s32[]{:S(2)}) async-start(), calls=%async_computation.42 | async-start | bytes 2621440 | tf_op jit(solution)/shard_map/reduce_scatter | solution.py:163
  1229.7 357.5 %reduce-scatter.36.cloned.1.call-start = ((), (), s32[]{:S(2)}) async-start(), calls=%async_computation.40 | async-start | bytes 2621440 | tf_op jit(solution)/shard_map/reduce_scatter | solution.py:157
  1238.7 394.1 %reduce-scatter.38.cloned.1.call-start = ((), (), s32[]{:S(2)}) async-start(), calls=%async_computation.41 | async-start | bytes 2621440 | tf_op jit(solution)/shard_map/reduce_scatter | solution.py:160
  1247.5 431.3 %reduce-scatter.26.cloned.1.call-start = ((), (), s32[]{:S(2)}) async-start(), calls=%async_computation.35 | async-start | bytes 2621440 | tf_op jit(solution)/shard_map/reduce_scatter | solution.py:136
  1341.6 382.8 %reduce-scatter.28.cloned.1.call-start = ((), (), s32[]{:S(2)}) async-start(), calls=%async_computation.36 | async-start | bytes 2621440 | tf_op jit(solution)/shard_map/reduce_scatter | solution.py:139
  1365.0 505.5 %reduce-scatter.42.cloned.1.call-start = ((), (), s32[]{:S(2)}) async-start(), calls=%async_computation.43 | async-start | bytes 10485760 | tf_op jit(solution)/shard_map/reduce_scatter | solution.py:172
  1386.3 631.8 %reduce-scatter.44.cloned.1.call-start = ((), (), s32[]{:S(2)}) async-start(), calls=%async_computation.44 | async-start | bytes 10485760 | tf_op jit(solution)/shard_map/reduce_scatter | solution.py:175
  1407.6 750.7 %all-reduce.17.cloned.1.call-start = ((), (), s32[]{:S(2)}) async-start(), calls=%async_computation.49 | async-start | bytes 17301504 | tf_op jit(solution)/shard_map/psum | solution.py:542
  (407 other events, 6186.5 us)
Sparse Core Ops, SparseCore 0:
  9.6 48.6 all-gather.25
  59.8 44.6 all-gather.29
  106.1 44.6 all-gather.39
  152.2 44.6 all-gather.43
  226.5 45.5 all-gather.33
  374.0 45.9 all-gather.37
  421.4 44.6 all-gather.47
  567.5 45.9 all-gather.49
  614.9 148.3 all-gather.51
  764.8 147.8 all-gather.53
  1128.7 35.9 reduce-scatter.49
  1207.1 35.9 reduce-scatter.51
  1247.7 81.5 all-reduce.18
  1362.2 42.5 reduce-scatter.23
  1407.0 43.6 reduce-scatter.31
  1453.0 43.0 reduce-scatter.33
  1498.6 43.1 reduce-scatter.39
  1543.9 43.1 reduce-scatter.35
  1589.6 43.1 reduce-scatter.37
  1635.6 43.1 reduce-scatter.25
  1681.1 43.1 reduce-scatter.27
  1726.7 143.7 reduce-scatter.41
  1872.9 145.1 reduce-scatter.43
  2023.8 134.5 all-reduce.16
  (12 shorter events, 308.9 us)
where the time goes:
time: 2190 us; the launch traced here: 2180 us
  waiting for transfers between devices  1420 us (65%)
  matrix products  306 us (14%)
  local copies, waits for them, and re-layouts  235 us (11%)
  other arithmetic  114 us (5%)
  blocking collectives  85.6 us (4%)
    reduce_scatter x1, waiting for transfers between devices, reduce_shards(): lax.psum_scatter(grad_list[14].astype(jnp.bfloat16), 'fsdp', scatter_dime...  148 us
    reduce_scatter x1, waiting for transfers between devices, reduce_shards(): lax.psum_scatter(grad_list[13].astype(jnp.bfloat16), 'fsdp', scatter_dime...  146 us
    all_gather x1, waiting for transfers between devices, fetch_all(): lax.all_gather(up_weight, 'fsdp', axis=0, tiled=True)  145 us
    all_gather x1, waiting for transfers between devices, fetch_all(): lax.all_gather(down_weight, 'fsdp', axis=0, tiled=True)  137 us
    psum x1, waiting for transfers between devices, on_device(): lax.psum(shard_total[0].astype(jnp.bfloat16), 'ctx').astype(jnp.float32)  124 us
    unnamed x41, waiting for transfers between devices  79.8 us
    dot_general x22, matrix products, outer_rows(): lax.dot_general(left_side, right_side, (((0,), (0,)), ((), ())), preferre...  74.4 us
    unnamed x824, local copies, waits for them, and re-layouts  66.3 us
  transfers between devices with their start and end apart: 36, of which 27 were waited for; matrix products, arithmetic and copies ran while one was open for 20% of the time, Pallas kernels for 0%

commit v1 on v0

v1 whole, which is shorter than its diff:
```python
import functools

import jax
import jax.numpy as jnp
from jax import lax
from jax.experimental import pallas as pl
from jax.experimental.pallas import tpu as pltpu
from jax.sharding import PartitionSpec as P

HEAD_DIM = 64
BUCKETS = 32
LANE = 128
GROUP = 4
eps_norm = 1e-05
neg_fill = -1e30
bf16 = jnp.bfloat16
f32 = jnp.float32
CORE, XBIT, YBIT = 1, 2, 4
VMEM_LIMIT = 60 * 1024 * 1024


def gelu_exact(values):
    return jax.nn.gelu(values, approximate=False)


def matmul(left_side, right_side):
    return jnp.dot(left_side, right_side, preferred_element_type=f32)


def matmul_back(left_side, right_side):
    return lax.dot_general(left_side, right_side, (((1,), (1,)), ((), ())), preferred_element_type=f32)


def outer_rows(left_side, right_side):
    return lax.dot_general(left_side, right_side, (((0,), (0,)), ((), ())), preferred_element_type=f32)


def norm_forward(values, gain, shift):
    row_mean = jnp.mean(values, axis=-1, keepdims=True)
    centered = values - row_mean
    scale = lax.rsqrt(jnp.mean(centered * centered, axis=-1, keepdims=True) + eps_norm)
    unit = centered * scale
    return unit * gain + shift, unit, scale


def norm_backward(unit, scale, gain, cotangent):
    back_unit = cotangent * gain
    first = jnp.mean(back_unit, axis=-1, keepdims=True)
    second = jnp.mean(back_unit * unit, axis=-1, keepdims=True)
    back = scale * (back_unit - first - unit * second)
    return back, jnp.sum(cotangent * unit, axis=0), jnp.sum(cotangent, axis=0)


def dot_nt(left_side, right_side):
    return lax.dot_general(left_side, right_side, (((1,), (1,)), ((), ())), preferred_element_type=f32)


def dot_nn(left_side, right_side):
    return lax.dot_general(left_side, right_side, (((1,), (0,)), ((), ())), preferred_element_type=f32)


def dot_tn(left_side, right_side):
    return lax.dot_general(left_side, right_side, (((0,), (0,)), ((), ())), preferred_element_type=f32)


def pick_lanes(table, index):
    return jnp.take_along_axis(table, index, axis=1)


def stack_heads(pair, low_half):
    zero = jnp.zeros_like(pair)
    return jnp.concatenate([jnp.where(low_half, pair, zero), jnp.where(low_half, zero, pair)], axis=0)


def rows_of(ref, first, last, cols):
    block = ref[first:last, 0, :, cols]
    return block.reshape(block.shape[0] * block.shape[1], block.shape[2])


def self_forward_kernel(
    length_ref, bounds_ref, posq_ref, posk_ref, q_ref, e_ref, k_ref, v_ref, o_ref, p_ref, own_ref,
    index_ref, mask_ref,
):
    slot = pl.program_id(0)
    lanes, _, rows, _ = q_ref.shape
    pieces = k_ref.shape[0] - (lanes - 1)
    keys = pieces * k_ref.shape[2]

    @pl.when(pl.program_id(1) == 0)
    def _():
        distance = posq_ref[...] - posk_ref[...]
        bucket = jnp.zeros(distance.shape, jnp.int32)
        for level in range(1, BUCKETS):
            bucket = bucket + (distance >= bounds_ref[level]).astype(jnp.int32)
        index_ref[...] = bucket
        valid = posk_ref[...] < length_ref[slot]
        mask_ref[0] = jnp.where(valid & (distance >= 0), 0.0, neg_fill)
        mask_ref[1] = jnp.where(valid & (distance > 0), 0.0, neg_fill)

    low_half = lax.broadcasted_iota(jnp.int32, (1, LANE), 1) < HEAD_DIM
    lane_id = lax.broadcasted_iota(jnp.int32, (1, LANE), 1)
    tables = [e_ref[lane, 0].astype(f32) for lane in range(lanes)]
    own_all = [jnp.zeros((rows, LANE), f32) for _ in range(lanes)]
    for pair in range(GROUP // 2):
        cols = slice(pair * LANE, (pair + 1) * LANE)
        q_pair = rows_of(q_ref, 0, lanes, cols) * jnp.asarray(HEAD_DIM**-0.5, bf16)
        k_main = rows_of(k_ref, 0, pieces, cols)
        v_main = rows_of(v_ref, 0, pieces, cols)
        scores = dot_nt(stack_heads(q_pair, low_half), k_main)
        own_pair = []
        for half in range(2):
            head = pair * 2 + half
            keep = low_half if half == 0 else jnp.logical_not(low_half)
            for lane in range(lanes):
                start = (half * lanes + lane) * rows
                part = scores[start : start + rows]
                bias = jnp.concatenate(
                    [
                        pick_lanes(tables[lane], index_ref[:, c * LANE : (c + 1) * LANE] + head * BUCKETS)
                        for c in range(keys // LANE)
                    ],
                    axis=1,
                )
                part = part + bias + mask_ref[min(lane, 1)]
                top = jnp.max(part, axis=1, keepdims=True)
                if lane > 0:
                    q_row = q_pair[lane * rows : (lane + 1) * rows].astype(f32)
                    k_row = k_ref[pieces + lane - 1, 0, :, cols].astype(f32)
                    own = jnp.sum(jnp.where(keep, q_row * k_row, 0.0), axis=1, keepdims=True)
                    own = own + tables[lane][:, head * BUCKETS : head * BUCKETS + 1]
                    top = jnp.maximum(top, own)
                    own_exp = jnp.exp(own - top)
                terms = jnp.exp(part - top)
                total = jnp.sum(terms, axis=1, keepdims=True)
                if lane > 0:
                    total = total + own_exp
                inverse = 1.0 / total
                p_ref[0, head, lane * rows : (lane + 1) * rows, :] = (terms * inverse).astype(bf16)
                if lane > 0:
                    own_prob = own_exp * inverse
                    own_all[lane] = jnp.where(lane_id == head, own_prob, own_all[lane])
                else:
                    own_prob = jnp.zeros((rows, 1), f32)
                own_pair.append(own_prob)
        p_low = p_ref[0, pair * 2 : pair * 2 + 2].reshape(2 * lanes * rows, keys)
        mixed = dot_nn(p_low, v_main)
        for lane in range(lanes):
            first = lane * rows
            second = (lanes + lane) * rows
            out = jnp.where(low_half, mixed[first : first + rows], mixed[second : second + rows])
            if lane > 0:
                own_prob = jnp.where(low_half, own_pair[lane], own_pair[lanes + lane])
                v_row = v_ref[pieces + lane - 1, 0, :, cols].astype(f32)
                out = out + own_prob.astype(bf16).astype(f32) * v_row
            o_ref[lane, 0, :, cols] = out.astype(bf16)
    for lane in range(lanes):
        own_ref[0, 0, lane * rows : (lane + 1) * rows, :] = own_all[lane]


def self_backward_kernel(
    posq_ref, posk_ref, low_ref, high_ref, p_ref, own_ref, do_ref, q_ref, k_ref, v_ref,
    dq_ref, dk_ref, dv_ref, de_ref, sums_ref,
):
    lanes, _, rows, _ = q_ref.shape
    pieces = k_ref.shape[0] - (lanes - 1)
    piece_rows = k_ref.shape[2]
    keys = pieces * piece_rows
    scale = HEAD_DIM**-0.5

    @pl.when((pl.program_id(0) == 0) & (pl.program_id(1) == 0))
    def _():
        ends = lax.broadcasted_iota(jnp.int32, (keys, keys), 1)
        sums_ref[...] = jnp.where(posk_ref[...] <= ends, 1.0, 0.0).astype(bf16)

    lane_id = lax.broadcasted_iota(jnp.int32, (1, LANE), 1)
    low_half = lane_id < HEAD_DIM
    near = posq_ref[...] - low_ref[...]
    far = posq_ref[...] - high_ref[...]
    back_embed = [jnp.zeros((rows, LANE), f32) for _ in range(lanes)]
    for pair in range(GROUP // 2):
        cols = slice(pair * LANE, (pair + 1) * LANE)
        q_pair = rows_of(q_ref, 0, lanes, cols) * jnp.asarray(scale, bf16)
        do_pair = rows_of(do_ref, 0, lanes, cols)
        k_main = rows_of(k_ref, 0, pieces, cols)
        v_main = rows_of(v_ref, 0, pieces, cols)
        q_stack = stack_heads(q_pair, low_half)
        do_stack = stack_heads(do_pair, low_half)
        back_probs = dot_nt(do_stack, v_main)
        p_low = p_ref[0, pair * 2 : pair * 2 + 2].reshape(2 * lanes * rows, keys)
        probs = p_low.astype(f32)
        weighted = probs * back_probs
        delta = jnp.sum(weighted, axis=1, keepdims=True)
        down_pair = []
        delta_list = []
        for half in range(2):
            head = pair * 2 + half
            keep = low_half if half == 0 else jnp.logical_not(low_half)
            for lane in range(lanes):
                start = (half * lanes + lane) * rows
                part = delta[start : start + rows]
                if lane > 0:
                    do_row = do_pair[lane * rows : (lane + 1) * rows].astype(f32)
                    v_row = v_ref[pieces + lane - 1, 0, :, cols].astype(f32)
                    back_own = jnp.sum(jnp.where(keep, do_row * v_row, 0.0), axis=1, keepdims=True)
                    own_prob = own_ref[0, 0, lane * rows : (lane + 1) * rows, head : head + 1]
                    part = part + own_prob * back_own
                    down_pair.append((own_prob * (back_own - part)).astype(bf16).astype(f32))
                else:
                    down_pair.append(None)
                delta_list.append(part)
        delta = jnp.concatenate(delta_list, axis=0)
        back_scores = (weighted - probs * delta).astype(bf16)
        back_q = dot_nn(back_scores, k_main)
        back_k = dot_tn(q_stack, back_scores)
        back_v = dot_tn(do_stack, p_low)
        dk_ref[:pieces, 0, :, cols] = back_k.T.astype(bf16).reshape(pieces, piece_rows, LANE)
        dv_ref[:pieces, 0, :, cols] = back_v.T.astype(bf16).reshape(pieces, piece_rows, LANE)
        prefix = dot_nn(back_scores, sums_ref[...])
        for lane in range(lanes):
            first = lane * rows
            second = (lanes + lane) * rows
            back = jnp.where(low_half, back_q[first : first + rows], back_q[second : second + rows])
            if lane > 0:
                k_row = k_ref[pieces + lane - 1, 0, :, cols].astype(f32)
                down = jnp.where(low_half, down_pair[lane], down_pair[lanes + lane])
                back = back + down * k_row
                own_low = jnp.where(
                    low_half,
                    own_ref[0, 0, lane * rows : (lane + 1) * rows, pair * 2 : pair * 2 + 1],
                    own_ref[0, 0, lane * rows : (lane + 1) * rows, pair * 2 + 1 : pair * 2 + 2],
                )
                own_low = own_low.astype(bf16).astype(f32)
                dk_ref[pieces + lane - 1, 0, :, cols] = (
                    down * q_pair[first : first + rows].astype(f32)
                ).astype(bf16)
                dv_ref[pieces + lane - 1, 0, :, cols] = (
                    own_low * do_pair[first : first + rows].astype(f32)
                ).astype(bf16)
            dq_ref[lane, 0, :, cols] = (back * scale).astype(bf16)
            for half in range(2):
                head = pair * 2 + half
                start = (half * lanes + lane) * rows
                upper = jnp.zeros((rows, LANE), f32)
                lower = jnp.zeros((rows, LANE), f32)
                for c in range(keys // LANE):
                    table = prefix[start : start + rows, c * LANE : (c + 1) * LANE]
                    spot = near - c * LANE
                    upper = jnp.where((spot >= 0) & (spot < LANE), pick_lanes(table, spot & (LANE - 1)), upper)
                    spot = far - c * LANE
                    lower = jnp.where((spot >= 0) & (spot < LANE), pick_lanes(table, spot & (LANE - 1)), lower)
                change = upper - lower
                if lane > 0:
                    change = change + jnp.where(lane_id == head * BUCKETS, down_pair[half * lanes + lane], 0.0)
                back_embed[lane] = jnp.where(lane_id // BUCKETS == head, change, back_embed[lane])
    for lane in range(lanes):
        de_ref[lane, 0] = back_embed[lane].astype(bf16)


def cross_forward_kernel(length_ref, posk_ref, q_ref, k_ref, v_ref, o_ref, p_ref):
    slot = pl.program_id(0)
    lanes, _, rows, _ = q_ref.shape
    pieces = k_ref.shape[0]
    keys = pieces * k_ref.shape[2]
    low_half = lax.broadcasted_iota(jnp.int32, (1, LANE), 1) < HEAD_DIM
    fill = jnp.where(posk_ref[...] < length_ref[slot], 0.0, neg_fill)
    count = lanes * rows
    for pair in range(GROUP // 2):
        cols = slice(pair * LANE, (pair + 1) * LANE)
        q_pair = rows_of(q_ref, 0, lanes, cols) * jnp.asarray(HEAD_DIM**-0.5, bf16)
        k_main = rows_of(k_ref, 0, pieces, cols)
        v_main = rows_of(v_ref, 0, pieces, cols)
        scores = dot_nt(stack_heads(q_pair, low_half), k_main) + fill
        top = jnp.max(scores, axis=1, keepdims=True)
        terms = jnp.exp(scores - top)
        inverse = 1.0 / jnp.sum(terms, axis=1, keepdims=True)
        p_low = (terms * inverse).astype(bf16)
        p_ref[0, pair * 2 : pair * 2 + 2] = p_low.reshape(2, count, keys)
        mixed = dot_nn(p_low, v_main)
        out = jnp.where(low_half, mixed[:count], mixed[count:]).astype(bf16)
        o_ref[:, 0, :, cols] = out.reshape(lanes, rows, LANE)


def cross_backward_kernel(p_ref, do_ref, q_ref, k_ref, v_ref, dq_ref, dk_ref, dv_ref):
    lanes, _, rows, _ = q_ref.shape
    pieces = k_ref.shape[0]
    piece_rows = k_ref.shape[2]
    keys = pieces * piece_rows
    count = lanes * rows
    scale = HEAD_DIM**-0.5
    low_half = lax.broadcasted_iota(jnp.int32, (1, LANE), 1) < HEAD_DIM
    for pair in range(GROUP // 2):
        cols = slice(pair * LANE, (pair + 1) * LANE)
        q_pair = rows_of(q_ref, 0, lanes, cols) * jnp.asarray(scale, bf16)
        do_pair = rows_of(do_ref, 0, lanes, cols)
        k_main = rows_of(k_ref, 0, pieces, cols)
        v_main = rows_of(v_ref, 0, pieces, cols)
        q_stack = stack_heads(q_pair, low_half)
        do_stack = stack_heads(do_pair, low_half)
        back_probs = dot_nt(do_stack, v_main)
        p_low = p_ref[0, pair * 2 : pair * 2 + 2].reshape(2 * count, keys)
        probs = p_low.astype(f32)
        weighted = probs * back_probs
        delta = jnp.sum(weighted, axis=1, keepdims=True)
        back_scores = (weighted - probs * delta).astype(bf16)
        back_q = dot_nn(back_scores, k_main)
        back_k = dot_tn(q_stack, back_scores)
        back_v = dot_tn(do_stack, p_low)
        dk_ref[:, 0, :, cols] = back_k.T.astype(bf16).reshape(pieces, piece_rows, LANE)
        dv_ref[:, 0, :, cols] = back_v.T.astype(bf16).reshape(pieces, piece_rows, LANE)
        back = jnp.where(low_half, back_q[:count], back_q[count:]) * scale
        dq_ref[:, 0, :, cols] = back.astype(bf16).reshape(lanes, rows, LANE)


def head_block(array, width=GROUP * HEAD_DIM):
    return pl.BlockSpec((array.shape[0], 1, array.shape[2], width), lambda s, g: (0, s, 0, g))


def whole_block(array):
    return pl.BlockSpec(array.shape, lambda s, g: (0,) * array.ndim)


SMEM_SPEC = pl.BlockSpec(memory_space=pltpu.SMEM)


def params():
    return pltpu.CompilerParams(vmem_limit_bytes=VMEM_LIMIT)


def shaped(shape, dtype):
    return jax.ShapeDtypeStruct(shape, dtype)


def attention_cost(matmuls, rows, keys, width, slots, passes):
    return pl.CostEstimate(
        flops=2 * matmuls * slots * rows * keys * width * 2,
        bytes_accessed=4 * slots * rows * keys * (width // HEAD_DIM),
        transcendentals=passes * slots * rows * keys * (width // HEAD_DIM),
    )


def self_forward(length, bounds, posq, posk, q, e, k, v):
    lanes, slots, rows, width = q.shape
    heads = width // HEAD_DIM
    keys = posk.shape[1]
    count = lanes * rows
    groups = heads // GROUP
    return pl.pallas_call(
        self_forward_kernel,
        grid=(slots, groups),
        in_specs=[
            SMEM_SPEC, SMEM_SPEC, whole_block(posq), whole_block(posk),
            head_block(q), head_block(e, GROUP * BUCKETS), head_block(k), head_block(v),
        ],
        out_specs=[
            head_block(q),
            pl.BlockSpec((1, GROUP, count, keys), lambda s, g: (s, g, 0, 0)),
            pl.BlockSpec((1, 1, count, LANE), lambda s, g: (s, g, 0, 0)),
        ],
        out_shape=[
            shaped(q.shape, bf16),
            shaped((slots, heads, count, keys), bf16),
            shaped((slots, groups, count, LANE), f32),
        ],
        scratch_shapes=[pltpu.VMEM((rows, keys), jnp.int32), pltpu.VMEM((2, rows, keys), f32)],
        compiler_params=params(),
        cost_estimate=attention_cost(2, count, keys, width, slots, 1),
        name="self_forward",
    )(length, bounds, posq, posk, q, e, k, v)


def self_backward(posq, posk_col, low, high, p, own, do, q, k, v):
    lanes, slots, rows, width = q.shape
    heads = width // HEAD_DIM
    keys = p.shape[3]
    count = lanes * rows
    return pl.pallas_call(
        self_backward_kernel,
        grid=(slots, heads // GROUP),
        in_specs=[
            whole_block(posq), whole_block(posk_col), whole_block(low), whole_block(high),
            pl.BlockSpec((1, GROUP, count, keys), lambda s, g: (s, g, 0, 0)),
            pl.BlockSpec((1, 1, count, LANE), lambda s, g: (s, g, 0, 0)),
            head_block(do), head_block(q), head_block(k), head_block(v),
        ],
        out_specs=[
            head_block(q), head_block(k), head_block(v),
            pl.BlockSpec((lanes, 1, rows, GROUP * BUCKETS), lambda s, g: (0, s, 0, g)),
        ],
        out_shape=[
            shaped(q.shape, bf16), shaped(k.shape, bf16), shaped(v.shape, bf16),
            shaped((lanes, slots, rows, heads * BUCKETS), bf16),
        ],
        scratch_shapes=[pltpu.VMEM((keys, keys), bf16)],
        compiler_params=params(),
        cost_estimate=attention_cost(6, count, keys, width, slots, 1),
        name="self_backward",
    )(posq, posk_col, low, high, p, own, do, q, k, v)


def cross_forward(length, posk, q, k, v):
    lanes, slots, rows, width = q.shape
    heads = width // HEAD_DIM
    keys = posk.shape[1]
    count = lanes * rows
    return pl.pallas_call(
        cross_forward_kernel,
        grid=(slots, heads // GROUP),
        in_specs=[SMEM_SPEC, whole_block(posk), head_block(q), head_block(k), head_block(v)],
        out_specs=[head_block(q), pl.BlockSpec((1, GROUP, count, keys), lambda s, g: (s, g, 0, 0))],
        out_shape=[shaped(q.shape, bf16), shaped((slots, heads, count, keys), bf16)],
        compiler_params=params(),
        cost_estimate=attention_cost(2, count, keys, width, slots, 1),
        name="cross_forward",
    )(length, posk, q, k, v)


def cross_backward(p, do, q, k, v):
    lanes, slots, rows, width = q.shape
    heads = width // HEAD_DIM
    keys = p.shape[3]
    count = lanes * rows
    return pl.pallas_call(
        cross_backward_kernel,
        grid=(slots, heads // GROUP),
        in_specs=[
            pl.BlockSpec((1, GROUP, count, keys), lambda s, g: (s, g, 0, 0)),
            head_block(do), head_block(q), head_block(k), head_block(v),
        ],
        out_specs=[head_block(q), head_block(k), head_block(v)],
        out_shape=[shaped(q.shape, bf16), shaped(k.shape, bf16), shaped(v.shape, bf16)],
        compiler_params=params(),
        cost_estimate=attention_cost(5, count, keys, width, slots, 0),
        name="cross_backward",
    )(p, do, q, k, v)


def ctx_hop(array, bit):
    size = lax.axis_size("ctx")
    return lax.ppermute(array, "ctx", [(i, i ^ bit) for i in range(size)])


def z_hop(array, step):
    size = lax.axis_size("fsdp")
    return lax.ppermute(array, "fsdp", [(i, (i + step) % size) for i in range(size)])


def ctx_spread(array, axis, cut):
    from_x = ctx_hop(array, XBIT)
    from_y = ctx_hop(array, YBIT)
    size = array.shape[axis]
    corner_one = ctx_hop(lax.slice_in_dim(from_y, 0, cut, axis=axis), XBIT)
    corner_two = ctx_hop(lax.slice_in_dim(from_x, cut, size, axis=axis), YBIT)
    near = [array, from_x, from_y, corner_one, corner_two]
    return near + [ctx_hop(item, CORE) for item in near]


SPREAD_PLAN = tuple(
    (offset + core, part) for core in (0, 1) for offset, part in ((0, 0), (XBIT, 0), (YBIT, 0), (XBIT + YBIT, 1), (XBIT + YBIT, 2))
)


def piece_number(index):
    return (index & 1) * 4 + (index >> 1)


def block_copies(layout):
    copies = []
    row = 0
    for number, (shard_rows, columns) in enumerate(layout):
        piece_rows = shard_rows // 8
        if columns >= 1024:
            for block in range(columns // 1024):
                copies.append((row, piece_rows, 0, 1024, number, 0, block * 1024))
                row += piece_rows
        else:
            parts = 1024 // columns
            rows = piece_rows // parts
            for part in range(parts):
                copies.append((row, rows, part * columns, columns, number, part * rows, 0))
            row += rows
    return tuple(copies), row


def to_buffer(pieces, layout):
    rows = []
    for piece, (shard_rows, columns) in zip(pieces, layout):
        piece_rows = shard_rows // 8
        if columns >= 1024:
            for block in range(columns // 1024):
                rows.append(piece[:, block * 1024 : (block + 1) * 1024])
        else:
            parts = 1024 // columns
            step = piece_rows // parts
            rows.append(jnp.concatenate([piece[i * step : (i + 1) * step] for i in range(parts)], axis=1))
    return jnp.concatenate(rows, axis=0)


def place_copies(copies, cut):
    def chosen(part):
        if part == 0:
            return copies
        if part == 1:
            return tuple(item for item in copies if item[0] < cut)
        return tuple((item[0] - cut,) + item[1:] for item in copies if item[0] >= cut)

    return chosen


def assemble_kernel(layout, copies, cut, steps, place_ref, *refs):
    count = len(layout)
    locals_ = refs[:count]
    arrivals = refs[count : count + len(SPREAD_PLAN)]
    outs = refs[count + len(SPREAD_PLAN) : -1]
    sem = refs[-1]
    chosen = place_copies(copies, cut)
    moves = []
    for number, (shard_rows, _) in enumerate(layout):
        start = pl.multiple_of(place_ref[0] * shard_rows, shard_rows)
        moves.append(pltpu.make_async_copy(locals_[number], outs[number].at[pl.ds(start, shard_rows), :], sem))
    for arrival, (offset, part) in zip(arrivals, SPREAD_PLAN):
        for step in range(1, steps):
            for row, rows, col, cols, number, prow, wcol in chosen(part):
                shard_rows = layout[number][0]
                piece_rows = shard_rows // 8
                start = place_ref[step] * shard_rows + place_ref[steps + offset] * piece_rows + prow
                start = pl.multiple_of(start, 16)
                moves.append(
                    pltpu.make_async_copy(
                        arrival.at[step - 1, pl.ds(row, rows), pl.ds(col, cols)],
                        outs[number].at[pl.ds(start, rows), pl.ds(wcol, cols)],
                        sem,
                    )
                )
    for move in moves:
        move.start()
    for move in moves:
        move.wait()


def gather_group(weights, layout, cut, z_index, c_index):
    steps = lax.axis_size("fsdp")
    copies, _ = block_copies(layout)
    number = piece_number(c_index)
    mine = to_buffer(
        [lax.dynamic_slice_in_dim(w, number * (rows // 8), rows // 8, 0) for w, (rows, _) in zip(weights, layout)],
        layout,
    )
    ring = [mine]
    for _ in range(steps - 1):
        ring.append(z_hop(ring[-1], 1))
    arrivals = ctx_spread(jnp.stack(ring[1:]), 1, cut)
    place = jnp.stack(
        [(z_index - step) % steps for step in range(steps)] + [piece_number(c_index ^ j) for j in range(8)]
    ).astype(jnp.int32)
    vmem = pl.BlockSpec(memory_space=pltpu.VMEM)
    total = sum(rows * columns for rows, columns in layout) * steps * 2
    return pl.pallas_call(
        functools.partial(assemble_kernel, layout, copies, cut, steps),
        in_specs=[SMEM_SPEC] + [vmem] * (len(weights) + len(arrivals)),
        out_specs=[pl.BlockSpec(memory_space=pl.ANY)] * len(weights),
        out_shape=[shaped((rows * steps, columns), bf16) for rows, columns in layout],
        scratch_shapes=[pltpu.SemaphoreType.DMA],
        compiler_params=params(),
        cost_estimate=pl.CostEstimate(flops=0, bytes_accessed=2 * total, transcendentals=0),
        name="assemble",
    )(place, *weights, *arrivals)


def fold_kernel(copies, buffer_rows, extra, quarter, table_ref, *refs):
    count = (len(refs) - 4) // 2
    keeps, arrivals, outs = refs[:count], refs[count : 2 * count], refs[2 * count :]
    step = pl.program_id(0)
    for number, out in enumerate(outs):

        @pl.when(step // quarter == number)
        def _(out=out):
            for row, rows, col, cols, weight, prow, wcol in copies:
                total = keeps[weight][0, prow : prow + rows, wcol : wcol + cols].astype(f32)
                total = total + arrivals[weight][0, prow : prow + rows, wcol : wcol + cols].astype(f32)
                out[0, row : row + rows, col : col + cols] = total.astype(bf16)
            if extra:
                total = keeps[-1][0].astype(f32) + arrivals[-1][0].astype(f32)
                out[0, buffer_rows:, :] = total.astype(bf16)


def fold_cores(keeps, arrivals, copies, buffer_rows, extra_rows, table, steps):
    quarter = steps
    total_steps = 4 * steps

    def by_table(array):
        return pl.BlockSpec((1,) + array.shape[1:], lambda t, tab: (tab[t], 0, 0))

    def by_extra(array):
        return pl.BlockSpec((1,) + array.shape[1:], lambda t, tab: (tab[total_steps + t], 0, 0))

    def specs(arrays):
        out = [by_table(a) for a in arrays]
        if extra_rows:
            out[-1] = by_extra(arrays[-1])
        return out

    rows = buffer_rows + extra_rows

    def out_spec(number):
        return pl.BlockSpec((1, rows, 1024), lambda t, tab: (jnp.clip(t - number * quarter, 0, quarter - 1), 0, 0))

    return pl.pallas_call(
        functools.partial(fold_kernel, copies, buffer_rows, extra_rows > 0, quarter),
        grid_spec=pltpu.PrefetchScalarGridSpec(
            num_scalar_prefetch=1,
            grid=(total_steps,),
            in_specs=specs(keeps) + specs(arrivals),
            out_specs=[out_spec(n) for n in range(4)],
        ),
        out_shape=[shaped((quarter, rows, 1024), bf16)] * 4,
        compiler_params=params(),
        cost_estimate=pl.CostEstimate(flops=0, bytes_accessed=6 * total_steps * rows * 1024, transcendentals=0),
        name="fold_cores",
    )(table, *keeps, *arrivals)


def unpack_kernel(layout, copies, cut, place_ref, *refs):
    arrivals = refs[: len(SPREAD_PLAN)]
    outs = refs[len(SPREAD_PLAN) :]
    chosen = place_copies(copies, cut)
    for arrival, (offset, part) in zip(arrivals, SPREAD_PLAN):
        for row, rows, col, cols, number, prow, wcol in chosen(part):
            piece_rows = layout[number][0] // 8
            start = pl.multiple_of(place_ref[offset] * piece_rows + prow, 8)
            outs[number][pl.ds(start, rows), wcol : wcol + cols] = arrival[row : row + rows, col : col + cols].astype(f32)


def reduce_group(keeps, sends, layout, cut, extra, z_index, c_index):
    steps = lax.axis_size("fsdp")
    half = steps // 2
    copies, buffer_rows = block_copies(layout)
    keeps = [k.reshape(steps * 4, rows // 8, columns) for k, (rows, columns) in zip(keeps, layout)]
    arrivals = [
        ctx_hop(s.reshape(steps * 4, rows // 8, columns), CORE) for s, (rows, columns) in zip(sends, layout)
    ]
    extra_rows = 0
    if extra is not None:
        rows = extra.shape[1]
        extra_rows = rows // steps
        pairs = extra.reshape(4, 2, rows, 1024)
        keeps.append(pairs[:, 0].reshape(4 * steps, extra_rows, 1024))
        arrivals.append(ctx_hop(pairs[:, 1].reshape(4 * steps, extra_rows, 1024), CORE))
    table, extra_table = [], []
    for first_x, on in ((True, 1), (True, 0), (False, 1), (False, 0)):
        for other in range(2):
            for kk in range(half):
                k = kk if first_x else kk + half
                offset = (other * 2 + on) if first_x else (on * 2 + other)
                table.append(((z_index + k) % steps) * 4 + ((c_index >> 1) ^ offset))
                extra_table.append(jnp.int32(offset * steps + k))
    table = jnp.stack(table + extra_table).astype(jnp.int32)
    send_x, keep_x, send_y, keep_y = fold_cores(keeps, arrivals, copies, buffer_rows, extra_rows, table, steps)
    got_x = ctx_hop(send_x, XBIT)
    got_y = ctx_hop(send_y, YBIT)

    def add(a, b):
        return (a.astype(f32) + b.astype(f32)).astype(bf16)

    second_x = ctx_hop(add(keep_x[half:], got_x[half:]), YBIT)
    second_y = ctx_hop(add(keep_y[half:], got_y[half:]), XBIT)
    done = []
    for keep, got, second in ((keep_x, got_x, second_x), (keep_y, got_y, second_y)):
        for kk in range(half):
            done.append(keep[kk].astype(f32) + got[kk].astype(f32) + second[kk].astype(f32))
    total = done[0][:buffer_rows]
    for k in range(1, steps):
        total = total + z_hop(done[k][:buffer_rows].astype(bf16), k).astype(f32)
    arrivals = ctx_spread(total.astype(bf16), 0, cut)
    place = jnp.stack([piece_number(c_index ^ j) for j in range(8)]).astype(jnp.int32)
    vmem = pl.BlockSpec(memory_space=pltpu.VMEM)
    grads = pl.pallas_call(
        functools.partial(unpack_kernel, layout, copies, cut),
        in_specs=[SMEM_SPEC] + [vmem] * len(arrivals),
        out_specs=[vmem] * len(layout),
        out_shape=[shaped((rows, columns), f32) for rows, columns in layout],
        compiler_params=params(),
        cost_estimate=pl.CostEstimate(flops=0, bytes_accessed=6 * 8 * buffer_rows * 1024, transcendentals=0),
        name="unpack",
    )(place, *arrivals)
    extra_sum = None
    if extra is not None:
        extra_sum = jnp.concatenate([item[buffer_rows:] for item in done], axis=0)
    return grads, extra_sum


def on_device(
    hidden, encoder_out, out_grad, slot_len, enc_len, rel_bucket,
    query_weight, key_weight, value_weight, relative_weight, output_weight, self_norm_gain, self_norm_shift,
    cross_query_weight, cross_key_weight, cross_value_weight, cross_output_weight, cross_norm_gain,
    cross_norm_shift, up_weight, down_weight, feed_norm_gain, feed_norm_shift,
):
    lanes, slots, halves, half_rows, width = hidden.shape
    rows = halves * half_rows
    enc_rows = encoder_out.shape[1]
    ctx_count = lax.axis_size("ctx")
    steps = lax.axis_size("fsdp")
    z_index = lax.axis_index("fsdp")
    c_index = lax.axis_index("ctx")
    seq_len = ctx_count * rows
    all_rows = lanes * slots * rows
    slab = (lanes, slots, rows, width)
    paired = ctx_count == 8 and steps % 2 == 0 and query_weight.shape[0] % 256 == 0 and width == 1024

    norms = jnp.stack(
        [self_norm_gain, self_norm_shift, cross_norm_gain, cross_norm_shift, feed_norm_gain, feed_norm_shift]
    )
    norms = lax.all_gather(norms, "fsdp", axis=1, tiled=True).astype(f32)
    gain_one, shift_one, gain_two, shift_two, gain_three, shift_three = [norms[i][None] for i in range(6)]

    self_set = (query_weight, key_weight, value_weight, output_weight, relative_weight)
    cross_set = (cross_query_weight, cross_key_weight, cross_value_weight, cross_output_weight)
    feed_set = (up_weight, down_weight)
    layouts = [tuple(w.shape for w in group) for group in (self_set, cross_set, feed_set)]
    x_all = hidden.reshape(all_rows, width)
    x_rows = hidden.reshape(slab)
    if paired:
        cuts = (64, 64, 128)
        first = gather_group(self_set, layouts[0], cuts[0], z_index, c_index)
        both = jnp.stack([x_rows[0], encoder_out.reshape(slots, rows, width)])
        spread = ctx_spread(both, 0, 1)
        peers = [c_index ^ j for j in range(8)]
        by_peer = {}
        for (offset, part), item in zip(SPREAD_PLAN, spread):
            by_peer.setdefault(offset, []).append((part, item))
        main_rows, enc_all = [], []
        for j in range(8):
            items = by_peer[j]
            if len(items) == 1:
                main_rows.append(items[0][1][0])
                enc_all.append(items[0][1][1])
            else:
                main_rows.append(items[0][1][0])
                enc_all.append(items[1][1][0])
        second = gather_group(cross_set, layouts[1], cuts[1], z_index, c_index)
        third = gather_group(feed_set, layouts[2], cuts[2], z_index, c_index)
    else:
        gather = lambda w: lax.all_gather(w, "fsdp", axis=0, tiled=True)
        first, second, third = [[gather(w) for w in group] for group in (self_set, cross_set, feed_set)]
        peers = [jnp.int32(j) for j in range(ctx_count)]
        main = lax.all_gather(x_rows[0], "ctx", axis=0)
        enc = lax.all_gather(encoder_out, "ctx", axis=0)
        main_rows = [main[j] for j in range(ctx_count)]
        enc_all = [enc[j] for j in range(ctx_count)]
    query_full, key_full, value_full, output_full, relative_full = first
    cquery_full, ckey_full, cvalue_full, coutput_full = second
    up_full, down_full = third

    place = jnp.stack(peers).astype(jnp.int32)
    local = jnp.arange(half_rows, dtype=jnp.int32)

    def both_halves(start):
        return jnp.concatenate([start + local, seq_len - 1 - start - local])

    positions = both_halves(c_index * half_rows)
    key_positions = jnp.concatenate([both_halves(place[j] * half_rows) for j in range(ctx_count)])
    enc_positions = (place[:, None] * enc_rows + jnp.arange(enc_rows, dtype=jnp.int32)[None, :]).reshape(1, -1)
    levels = jnp.arange(BUCKETS + 1, dtype=jnp.int32)
    bounds = jnp.sum((rel_bucket[None, :] < levels[:, None]).astype(jnp.int32), axis=1)
    low_edge = jnp.tile(bounds[:BUCKETS], LANE // BUCKETS)[None]
    high_edge = jnp.tile(bounds[1:], LANE // BUCKETS)[None]

    keyed = jnp.concatenate([jnp.stack(main_rows), x_rows[1:]], axis=0)
    keyed_flat = keyed.reshape(-1, width)
    q = matmul(x_all, query_full).astype(bf16).reshape(slab)
    e = matmul(x_all, relative_full).astype(bf16).reshape(lanes, slots, rows, -1)
    k = matmul(keyed_flat, key_full).astype(bf16).reshape(keyed.shape)
    v = matmul(keyed_flat, value_full).astype(bf16).reshape(keyed.shape)
    o, probs, own = self_forward(slot_len, bounds, positions[:, None], key_positions[None], q, e, k, v)
    o_flat = o.reshape(all_rows, width)
    resid_one = x_all.astype(f32) + matmul(o_flat, output_full)
    normed_one, unit_one, scale_one = norm_forward(resid_one, gain_one, shift_one)
    normed_one_low = normed_one.astype(bf16)

    enc_flat = jnp.stack(enc_all).reshape(-1, width)
    enc_shape = (ctx_count, slots, enc_rows, width)
    ck = matmul(enc_flat, ckey_full).astype(bf16).reshape(enc_shape)
    cv = matmul(enc_flat, cvalue_full).astype(bf16).reshape(enc_shape)
    cq = matmul(normed_one_low, cquery_full).astype(bf16).reshape(slab)
    oc, cprobs = cross_forward(enc_len, enc_positions, cq, ck, cv)
    oc_flat = oc.reshape(all_rows, width)
    resid_two = normed_one + matmul(oc_flat, coutput_full)
    normed_two, unit_two, scale_two = norm_forward(resid_two, gain_two, shift_two)
    normed_two_low = normed_two.astype(bf16)

    pre_act = matmul(normed_two_low, up_full)
    act, gelu_pull = jax.vjp(gelu_exact, pre_act)
    act_low = act.astype(bf16)
    resid_three = normed_two + matmul(act_low, down_full)
    normed_three, unit_three, scale_three = norm_forward(resid_three, gain_three, shift_three)
    layer_out = normed_three.astype(bf16)

    core = c_index & 1

    def split_cores(array):
        parts = array.reshape(array.shape[0], steps, 2, array.shape[1] // (2 * steps))
        pick = lambda which: lax.dynamic_index_in_dim(parts, which, 2, keepdims=False).reshape(array.shape[0], -1)
        return pick(core), pick(1 - core)

    def weight_grad(left, right):
        if not paired:
            return outer_rows(left, right).astype(bf16)
        return [outer_rows(side, right).astype(bf16) for side in left]

    splits = split_cores if paired else (lambda array: array)

    row_valid = (positions[None, None, :] < slot_len[None, :, None]).astype(f32)
    row_valid = jnp.broadcast_to(row_valid, (lanes, slots, rows)).reshape(all_rows, 1)
    cotangent = out_grad.reshape(all_rows, width).astype(f32) * row_valid
    back_three, gain_grad_three, shift_grad_three = norm_backward(unit_three, scale_three, gain_three, cotangent)
    back_feed = back_three.astype(bf16)
    grad_down = weight_grad(splits(act_low), back_feed)
    back_pre = gelu_pull(matmul_back(back_feed, down_full))[0].astype(bf16)
    grad_up = weight_grad(splits(normed_two_low), back_pre)
    back_normed_two = back_three + matmul_back(back_pre, up_full)
    back_two, gain_grad_two, shift_grad_two = norm_backward(unit_two, scale_two, gain_two, back_normed_two)

    back_cross = back_two.astype(bf16)
    grad_coutput = weight_grad(splits(oc_flat), back_cross)
    back_oc = matmul_back(back_cross, coutput_full).astype(bf16).reshape(slab)
    back_cq, back_ck, back_cv = cross_backward(cprobs, back_oc, cq, ck, cv)
    back_cq = back_cq.reshape(all_rows, width)
    back_ck = back_ck.reshape(-1, width)
    back_cv = back_cv.reshape(-1, width)
    enc_split = splits(enc_flat)
    grad_ckey = weight_grad(enc_split, back_ck)
    grad_cvalue = weight_grad(enc_split, back_cv)
    grad_cquery = weight_grad(splits(normed_one_low), back_cq)
    enc_part = (matmul_back(back_ck, ckey_full) + matmul_back(back_cv, cvalue_full)).astype(bf16)
    enc_part = enc_part.reshape(ctx_count, slots * enc_rows, width)
    back_normed_one = back_two + matmul_back(back_cq, cquery_full)
    back_one, gain_grad_one, shift_grad_one = norm_backward(unit_one, scale_one, gain_one, back_normed_one)

    back_self = back_one.astype(bf16)
    grad_output = weight_grad(splits(o_flat), back_self)
    back_o = matmul_back(back_self, output_full).astype(bf16).reshape(slab)
    back_q, back_k, back_v, back_e = self_backward(
        positions[:, None], key_positions[:, None], low_edge, high_edge, probs, own, back_o, q, k, v
    )
    back_q = back_q.reshape(all_rows, width)
    back_e = back_e.reshape(all_rows, -1)
    back_k = back_k.reshape(-1, width)
    back_v = back_v.reshape(-1, width)
    x_split = splits(x_all)
    keyed_split = splits(keyed_flat)
    grad_query = weight_grad(x_split, back_q)
    grad_relative = weight_grad(x_split, back_e)
    grad_key = weight_grad(keyed_split, back_k)
    grad_value = weight_grad(keyed_split, back_v)
    keyed_part = matmul_back(back_k, key_full) + matmul_back(back_v, value_full)
    main_count = ctx_count * slots * rows
    main_part = keyed_part[:main_count].astype(bf16).reshape(ctx_count, slots * rows, width)
    back_x = back_one + matmul_back(back_q, query_full) + matmul_back(back_e, relative_full)

    norm_grads = jnp.stack(
        [gain_grad_one, shift_grad_one, gain_grad_two, shift_grad_two, gain_grad_three, shift_grad_three]
    )
    norm_grads = lax.psum(norm_grads, ("fsdp", "ctx"))
    norm_grads = lax.dynamic_slice_in_dim(norm_grads, z_index * (width // steps), width // steps, 1)

    self_grads = [grad_query, grad_key, grad_value, grad_output, grad_relative]
    cross_grads = [grad_cquery, grad_ckey, grad_cvalue, grad_coutput]
    feed_grads = [grad_up, grad_down]
    if paired:
        def reduce(grads, index, extra):
            keeps = [g[0] for g in grads]
            sends = [g[1] for g in grads]
            return reduce_group(keeps, sends, layouts[index], cuts[index], extra, z_index, c_index)

        third_grads, _ = reduce(feed_grads, 2, None)
        second_grads, enc_sum = reduce(cross_grads, 1, enc_part)
        first_grads, main_sum = reduce(self_grads, 0, main_part)
    else:
        def reduce(g):
            shard = lax.psum_scatter(g, "fsdp", scatter_dimension=0, tiled=True)
            return lax.psum(shard, "ctx").astype(f32)

        first_grads, second_grads, third_grads = [
            [reduce(g) for g in group] for group in (self_grads, cross_grads, feed_grads)
        ]
        scatter = lambda part: lax.psum_scatter(part, "ctx", scatter_dimension=0, tiled=True)
        enc_sum = scatter(enc_part).astype(f32).reshape(-1, width)
        main_sum = scatter(main_part).astype(f32).reshape(-1, width)
    encoder_grad = enc_sum.reshape(slots, enc_rows, width)
    hidden_grad = back_x + jnp.concatenate([main_sum, keyed_part[main_count:]], axis=0)

    out_shape = hidden.shape
    return (
        layer_out.reshape(out_shape), hidden_grad.reshape(out_shape), encoder_grad,
        first_grads[0], first_grads[1], first_grads[2], first_grads[4], first_grads[3], norm_grads[0], norm_grads[1],
        second_grads[0], second_grads[1], second_grads[2], second_grads[3], norm_grads[2], norm_grads[3],
        third_grads[0], third_grads[1], norm_grads[4], norm_grads[5],
    )


def solution(mesh):
    rows = P("fsdp", None)
    vector = P("fsdp")
    slab = P(None, "fsdp", None, "ctx", None)
    encoder = P("fsdp", "ctx", None)
    weights = (rows,) * 5 + (vector,) * 2 + (rows,) * 4 + (vector,) * 2 + (rows,) * 2 + (vector,) * 2
    return jax.shard_map(
        on_device,
        mesh=mesh,
        in_specs=(slab, encoder, slab, vector, vector, P()) + weights,
        out_specs=(slab, slab, encoder) + weights,
        check_vma=False,
    )
```

time: 2190 us -> 913 us (0.42)
  waiting for transfers between devices: 1420 us -> 151 us
  Pallas kernels: 0 us -> 187 us
  matrix products: 306 us -> 175 us
  other arithmetic: 114 us -> 33.6 us
  starting transfers between devices: 2.09 us -> 80 us
  local copies, waits for them, and re-layouts: 235 us -> 175 us
    all_gather x19 -> x0, waiting for transfers between devices: 647 us -> none  [the longest x1 145 us: fetch_all(): lax.all_gather(up_weight, 'fsdp', axis=0, tiled=True)]
    reduce_scatter x11 -> x0, waiting for transfers between devices: 570 us -> none  [the longest x1 148 us: reduce_shards(): lax.psum_scatter(grad_list[14].astype(jnp.bfloat16), 'fsdp', scatter_dime...]
    pallas_call x0 -> x13, Pallas kernels: none -> 187 us  [the longest x1 42.2 us: self_forward(): pl.pallas_call(self_forward_kernel, grid=(slots, groups), in_specs=[SMEM_...]
    ppermute x0 -> x106, waiting for transfers between devices: none -> 151 us  [the longest x88 115 us: ctx_hop(): return lax.ppermute(array, 'ctx', [(i, i ^ bit) for i in range(size)])]
    psum x1 -> x0, waiting for transfers between devices: 124 us -> none  [on_device(): lax.psum(shard_total[0].astype(jnp.bfloat16), 'ctx').astype(jnp.float32)]
    dot_general x82 -> x11, matrix products: 184 us -> 66.1 us  [matmul(): return jnp.dot(left_side, right_side, preferred_element_type=f32)]
    ppermute x0 -> x106, starting transfers between devices: none -> 80 us  [the longest x88 51.1 us: ctx_hop(): return lax.ppermute(array, 'ctx', [(i, i ^ bit) for i in range(size)])]
    unnamed x41 -> x0, waiting for transfers between devices: 79.8 us -> none
  transfers between devices with their start and end apart: 36 -> 106, of which waited for: 27 -> 19; matrix products, arithmetic and copies ran while one was open for 20% -> 34% of each run, Pallas kernels for 0% -> 13%
where the time goes in v1:
time: 913 us; the launch traced here: 897 us
  Pallas kernels  187 us (20%)
  local copies, waits for them, and re-layouts  175 us (19%)
  matrix products  175 us (19%)
  waiting for transfers between devices  151 us (17%)
  blocking collectives  92.9 us (10%)
  starting transfers between devices  80 us (9%)
  other arithmetic  33.6 us (4%)
    ppermute x88, waiting for transfers between devices, ctx_hop(): return lax.ppermute(array, 'ctx', [(i, i ^ bit) for i in range(size)])  115 us
    psum x1, blocking collectives, on_device(): norm_grads = lax.psum(norm_grads, ('fsdp', 'ctx'))  72.9 us
    dot_general x11, matrix products, matmul(): return jnp.dot(left_side, right_side, preferred_element_type=f32)  66.1 us
    dot_general x22, matrix products, outer_rows(): lax.dot_general(left_side, right_side, (((0,), (0,)), ((), ())), preferre...  61.1 us
    unnamed x290, local copies, waits for them, and re-layouts  58.1 us
    dynamic_slice x14, local copies, waits for them, and re-layouts, split_cores(): lax.dynamic_index_in_dim(parts, which, 2, keepdims=False)  57.7 us
    ppermute x88, starting transfers between devices, ctx_hop(): return lax.ppermute(array, 'ctx', [(i, i ^ bit) for i in range(size)])  51.1 us
    dot_general x11, matrix products, matmul_back(): lax.dot_general(left_side, right_side, (((1,), (1,)), ((), ())), preferre...  48.2 us
  transfers between devices with their start and end apart: 106, of which 19 were waited for; matrix products, arithmetic and copies ran while one was open for 34% of the time, Pallas kernels for 13%

profile of v1, /device:TPU:0, one launch (start us, length us, event | category | flops | bytes accessed | tf_op | source)
XLA Modules:
  0.0 897.5 jit_solution(11483629037290687411)
XLA Ops:
  30.2 20.0 %all_gather.3 = bf16[6,1024]{1,0:T(8,128)(2,1)S(1)} all-gather(bf16[6,256]{1,0:T(8,128)(2,1)S(1)} %stack.318), channel_id=1, replica_groups=mesh['ctx'=8,'fsdp'=4] {'fsdp'}, dimensions={1}, use_global_device_ids=true | all-gather | bytes 15360 | tf_op jit(solution)/shard_map/all_gather | solution.py:712
  85.4 10.7 %collective-permute-done.2 = bf16[144,1024]{1,0:T(8,128)(2,1)S(1)} collective-permute-done((bf16[144,1024]{1,0:T(8,128)(2,1)S(1)}, bf16[144,1024]{1,0:T(8,128)(2,1)S(1)}, u32[]{:S(2)}, u32[]{:S(2)}) %collective-permute-start.2) | collective-permute-done | bytes 294944 | tf_op jit(solution)/shard_map/ppermute | solution.py:444
  104.6 12.3 %collective-permute-done.23.refs_6_ = bf16[3,128,1024]{2,1,0:T(8,128)(2,1)} collective-permute-done((bf16[3,128,1024]{2,1,0:T(8,128)(2,1)}, bf16[3,128,1024]{2,1,0:T(8,128)(2,1)}, u32[]{:S(2)}, u32[]{:S(2)}) %collective-permute-start.23) | collective-permute-done | bytes 786464 | tf_op jit(solution)/shard_map/ppermute | solution.py:439
  123.3 14.8 %collective-permute-done.17 = bf16[1,2,64,1024]{3,2,1,0:T(8,128)(2,1)} collective-permute-done((bf16[1,2,64,1024]{3,2,1,0:T(8,128)(2,1)}, bf16[1,2,64,1024]{3,2,1,0:T(8,128)(2,1)}, u32[]{:S(2)}, u32[]{:S(2)}) %collective-permute-start.17) | collective-permute-done | bytes 262176 | tf_op jit(solution)/shard_map/ppermute | solution.py:439
  215.9 7.2 assemble.3
  239.6 42.2 %self_forward.1 = (bf16[3,2,64,1024]{3,2,1,0:T(8,128)(2,1)}, bf16[2,16,192,512]{3,2,1,0:T(8,128)(2,1)}, f32[2,4,192,128]{3,2,1,0:T(8,128)}) custom-call(s32[2]{0:T(128)} %length_ref.2, s32[33]{0:T(128)} %copy-done.98, s32[64,1]{1,0:T(8,128)} %copy.89.posq_ref, s32[1,512]{1,0:T(1,128)} %bitcast.404, bf16[3,2,64,1024]{3,2,1,0:T(8,128)(2,1)} %bitcast.379, ...), custom_call_target="tpu_custom_call" | custom-call | flops 1610612736 | bytes 12582912 | tf_op jit(solution)/shard_map/self_forward/pallas_call | solution.py:347
  308.1 11.8 %cross_forward.1 = (bf16[3,2,64,1024]{3,2,1,0:T(8,128)(2,1)}, bf16[2,16,192,512]{3,2,1,0:T(8,128)(2,1)}) custom-call(s32[2]{0:T(128)} %length_ref.3, s32[1,512]{1,0:T(1,128)} %add.649.posk_ref, bf16[3,2,64,1024]{3,2,1,0:T(8,128)(2,1)} %bitcast.438, bf16[8,2,64,1024]{3,2,1,0:T(8,128)(2,1)} %bitcast.430, bf16[8,2,64,1024]{3,2,1,0:T(8,128)(2,1)} %bitcast.428), custom_call_target="tpu_custom_call" | custom-call | flops 1610612736 | bytes 12582912 | tf_op jit(solution)/shard_map/cross_forward/pallas_call | solution.py:405
  353.4 11.5 %assemble.5 = (bf16[1024,4096]{1,0:T(8,128)(2,1)}, bf16[4096,1024]{1,0:T(8,128)(2,1)}) custom-call(s32[12]{0:T(128)} %stack.150.place_ref, bf16[256,4096]{1,0:T(8,128)(2,1)} %refs_0_.5, bf16[1024,1024]{1,0:T(8,128)(2,1)} %refs_1_.5, bf16[3,256,1024]{2,1,0:T(8,128)(2,1)} %pad_maximum_fusion.refs_2_, bf16[3,256,1024]{2,1,0:T(8,128)(2,1)} %collective-permute-done.36.refs_3_, ...), custom_call_target="tpu_custom_call" | custom-call | bytes 33554432 | tf_op jit(solution)/shard_map/assemble/pallas_call | solution.py:557
  365.0 20.2 %multiply_convert_fusion = (bf16[384,4096]{1,0:T(8,128)(2,1)}, f32[384,4096]{1,0:T(8,128)}, f32[384,4096]{1,0:T(8,128)}) fusion(bf16[384,1024]{1,0:T(8,128)(2,1)S(1)} %fusion.9, bf16[1024,4096]{1,0:T(8,128)(2,1)} %get-tuple-element.77), kind=kOutput, calls=%fused_computation.3 | convolution fusion | flops 3323461632 | bytes 24903680 | tf_op jit(solution)/shard_map/dot_general | solution.py:27
  390.0 8.2 fusion.55
  402.1 14.5 %add_convert_fusion = bf16[384,4096]{1,0:T(8,128)(2,1)} fusion(f32[384,4096]{1,0:T(8,128)} %get-tuple-element.125, f32[384,4096]{1,0:T(8,128)} %get-tuple-element.190, bf16[4096,1024]{1,0:T(8,128)(2,1)} %get-tuple-element.78, f32[384,1024]{1,0:T(8,128)S(1)} %get-tuple-element.146), kind=kOutput, calls=%fused_computation.2 | convolution fusion | flops 3243638784 | bytes 25690112 | tf_op jit(solution)/shard_map/dot_general | solution.py:31
  416.6 8.2 multiply_reduce_fusion.1
  428.3 13.6 %cross_backward.1 = (bf16[3,2,64,1024]{3,2,1,0:T(8,128)(2,1)}, bf16[8,2,64,1024]{3,2,1,0:T(8,128)(2,1)}, bf16[8,2,64,1024]{3,2,1,0:T(8,128)(2,1)}) custom-call(bf16[2,16,192,512]{3,2,1,0:T(8,128)(2,1)} %get-tuple-element.79.p_ref, bf16[3,2,64,1024]{3,2,1,0:T(8,128)(2,1)} %bitcast.441, bf16[3,2,64,1024]{3,2,1,0:T(8,128)(2,1)} %bitcast.439, ...), custom_call_target="tpu_custom_call" | custom-call | flops 4026531840 | bytes 12582912 | tf_op jit(solution)/shard_map/cross_backward/pallas_call | solution.py:422
  450.4 37.5 %self_backward.1 = (bf16[3,2,64,1024]{3,2,1,0:T(8,128)(2,1)}, bf16[10,2,64,1024]{3,2,1,0:T(8,128)(2,1)}, bf16[10,2,64,1024]{3,2,1,0:T(8,128)(2,1)}, bf16[3,2,64,512]{3,2,1,0:T(8,128)(2,1)}) custom-call(s32[64,1]{1,0:T(8,128)} %copy.89.posq_ref, s32[512,1]{1,0:T(8,128)} %copy.91.posk_ref, s32[1,128]{1,0:T(1,128)} %broadcast_in_dim_tile.6.low_ref, ...), custom_call_target="tpu_custom_call" | custom-call | flops 4831838208 | bytes 12582912 | tf_op jit(solution)/shard_map/self_backward/pallas_call | solution.py:376
  524.8 9.3 %constant_dynamic-slice_fusion.2 = (bf16[384,4,1,512]{3,2,1,0:T(2,128)(2,1)}, bf16[384,4,1,512]{3,2,1,0:T(2,128)(2,1)}) fusion(bf16[384,4,2,512]{3,2,1,0:T(2,128)(2,1)S(1)} %reshape.618, s32[]{:T(128)S(6)} %select_n.189, s32[]{:T(128)S(6)} %select_n.188), kind=kLoop, calls=%fused_computation.180 | loop fusion | bytes 6291464 | tf_op jit(solution)/shard_map/jit(dynamic_index_in_dim)/dynamic_slice | solution.py:801
  569.5 13.2 %fold_cores.4 = (bf16[4,160,1024]{2,1,0:T(8,128)(2,1)}, bf16[4,160,1024]{2,1,0:T(8,128)(2,1)}, bf16[4,160,1024]{2,1,0:T(8,128)(2,1)}, bf16[4,160,1024]{2,1,0:T(8,128)(2,1)}) custom-call(s32[32]{0:T(128)} %stack.353.table_ref, bf16[16,32,1024]{2,1,0:T(8,128)(2,1)} %bitcast.327, bf16[16,32,1024]{2,1,0:T(8,128)(2,1)} %bitcast.377, ...), custom_call_target="tpu_custom_call" | custom-call | bytes 15728640 | tf_op jit(solution)/shard_map/fold_cores/pallas_call | solution.py:607
  599.9 13.6 %fold_cores.3 = (bf16[4,176,1024]{2,1,0:T(8,128)(2,1)}, bf16[4,176,1024]{2,1,0:T(8,128)(2,1)}, bf16[4,176,1024]{2,1,0:T(8,128)(2,1)}, bf16[4,176,1024]{2,1,0:T(8,128)(2,1)}) custom-call(s32[32]{0:T(128)} %stack.353.table_ref, bf16[16,32,1024]{2,1,0:T(8,128)(2,1)} %bitcast.324, bf16[16,32,1024]{2,1,0:T(8,128)(2,1)} %bitcast.371, ...), custom_call_target="tpu_custom_call" | custom-call | bytes 17301504 | tf_op jit(solution)/shard_map/fold_cores/pallas_call | solution.py:607
  621.8 72.9 %psum.7 = f32[6,1024]{1,0:T(8,128)S(1)} all-reduce(f32[6,1024]{1,0:T(8,128)S(1)} %stack.361), channel_id=1, replica_groups=mesh['ctx'=8,'fsdp'=4] {'fsdp','ctx'}, use_global_device_ids=true, to_apply=%region_19.20 | all-reduce | flops 6144 | bytes 49152 | tf_op jit(solution)/shard_map/psum | solution.py:862
  714.2 7.0 collective-permute-done.61
  724.7 15.3 %fold_cores.5 = (bf16[4,256,1024]{2,1,0:T(8,128)(2,1)}, bf16[4,256,1024]{2,1,0:T(8,128)(2,1)}, bf16[4,256,1024]{2,1,0:T(8,128)(2,1)}, bf16[4,256,1024]{2,1,0:T(8,128)(2,1)}) custom-call(s32[32]{0:T(128)} %stack.353.table_ref, bf16[16,32,4096]{2,1,0:T(8,128)(2,1)} %bitcast.322, bf16[16,128,1024]{2,1,0:T(8,128)(2,1)} %bitcast.321, ...), custom_call_target="tpu_custom_call" | custom-call | bytes 25165824 | tf_op jit(solution)/shard_map/fold_cores/pallas_call | solution.py:607
  752.6 30.6 %collective-permute-done.93 = bf16[4,256,1024]{2,1,0:T(8,128)(2,1)S(1)} collective-permute-done((bf16[4,256,1024]{2,1,0:T(8,128)(2,1)}, bf16[4,256,1024]{2,1,0:T(8,128)(2,1)S(1)}, u32[]{:S(2)}, u32[]{:S(2)}) %collective-permute-start.93) | collective-permute-done | bytes 2097184 | tf_op jit(solution)/shard_map/ppermute | solution.py:439
  795.4 11.9 %collective-permute-done.94 = bf16[2,256,1024]{2,1,0:T(8,128)(2,1)S(1)} collective-permute-done((bf16[2,256,1024]{2,1,0:T(8,128)(2,1)S(1)}, bf16[2,256,1024]{2,1,0:T(8,128)(2,1)S(1)}, u32[]{:S(2)}, u32[]{:S(2)}) %collective-permute-start.94) | collective-permute-done | bytes 1048608 | tf_op jit(solution)/shard_map/ppermute | solution.py:439
  827.1 17.2 %collective-permute-done.95 = bf16[256,1024]{1,0:T(8,128)(2,1)S(1)} collective-permute-done((bf16[256,1024]{1,0:T(8,128)(2,1)S(1)}, bf16[256,1024]{1,0:T(8,128)(2,1)S(1)}, u32[]{:S(2)}, u32[]{:S(2)}) %collective-permute-start.95) | collective-permute-done | bytes 524320 | tf_op jit(solution)/shard_map/ppermute | solution.py:444
  855.0 13.6 %collective-permute-done.69.refs_3_ = bf16[64,1024]{1,0:T(8,128)(2,1)S(1)} collective-permute-done((bf16[64,1024]{1,0:T(8,128)(2,1)S(1)}, bf16[64,1024]{1,0:T(8,128)(2,1)S(1)}, u32[]{:S(2)}, u32[]{:S(2)}) %collective-permute-start.69) | collective-permute-done | bytes 131104 | tf_op jit(solution)/shard_map/ppermute | solution.py:439
  (681 shorter events, 456.9 us)
Async XLA Ops:
  3.5 68.8 %collective-permute-start.13 = (bf16[2,2,64,1024]{3,2,1,0:T(8,128)(2,1)}, bf16[2,2,64,1024]{3,2,1,0:T(8,128)(2,1)}, u32[]{:S(2)}, u32[]{:S(2)}) collective-permute-start(bf16[2,2,64,1024]{3,2,1,0:T(8,128)(2,1)} %pad_maximum_fusion.3), channel_id=1, source_target_pairs={{0,8},{4,12},{8,0},{12,4},{16,24},{20,28},{24,16},{28,20},{1,9},{5... | collective-permute-start | bytes 1572872 | tf_op jit(solution)/shard_map/ppermute | solution.py:439
  6.4 67.2 %collective-permute-start.12 = (bf16[2,2,64,1024]{3,2,1,0:T(8,128)(2,1)}, bf16[2,2,64,1024]{3,2,1,0:T(8,128)(2,1)}, u32[]{:S(2)}, u32[]{:S(2)}) collective-permute-start(bf16[2,2,64,1024]{3,2,1,0:T(8,128)(2,1)} %pad_maximum_fusion.3), channel_id=1, source_target_pairs={{0,4},{4,0},{8,12},{12,8},{16,20},{20,16},{24,28},{28,24},{1,5},{5... | collective-permute-start | bytes 1572872 | tf_op jit(solution)/shard_map/ppermute | solution.py:439
  9.1 44.2 %collective-permute-start.19 = (bf16[128,1024]{1,0:T(8,128)(2,1)}, bf16[128,1024]{1,0:T(8,128)(2,1)}, u32[]{:S(2)}, u32[]{:S(2)}) collective-permute-start(bf16[128,1024]{1,0:T(8,128)(2,1)} %pad_maximum_fusion.5), channel_id=1, source_target_pairs={{0,1},{1,2},{2,3},{3,0},{4,5},{5,6},{6,7},{7,4},{8,9},{9,10},{10,1... | collective-permute-start | bytes 786440 | tf_op jit(solution)/shard_map/ppermute | solution.py:444
  18.0 37.2 %collective-permute-start = (bf16[144,1024]{1,0:T(8,128)(2,1)}, bf16[144,1024]{1,0:T(8,128)(2,1)}, u32[]{:S(2)}, u32[]{:S(2)}) collective-permute-start(bf16[144,1024]{1,0:T(8,128)(2,1)} %constant_dynamic-update-slice_fusion), channel_id=1, source_target_pairs={{0,1},{1,2},{2,3},{3,0},{4,5},{5,6},{6,7},{7,4},{8,9},{9,10},{10,1... | collective-permute-start | bytes 884744 | tf_op jit(solution)/shard_map/ppermute | solution.py:444
  27.1 45.1 %collective-permute-start.33 = (bf16[256,1024]{1,0:T(8,128)(2,1)}, bf16[256,1024]{1,0:T(8,128)(2,1)}, u32[]{:S(2)}, u32[]{:S(2)}) collective-permute-start(bf16[256,1024]{1,0:T(8,128)(2,1)} %dynamic-slice_dynamic-update-slice_fusion), channel_id=1, source_target_pairs={{0,1},{1,2},{2,3},{3,0},{4,5},{5,6},{6,7},{7,4},{8,9},{9,10},{10,1... | collective-permute-start | bytes 1572872 | tf_op jit(solution)/shard_map/ppermute | solution.py:444
  98.8 39.6 %collective-permute-start.22 = (bf16[3,128,1024]{2,1,0:T(8,128)(2,1)}, bf16[3,128,1024]{2,1,0:T(8,128)(2,1)}, u32[]{:S(2)}, u32[]{:S(2)}) collective-permute-start(bf16[3,128,1024]{2,1,0:T(8,128)(2,1)} %pad_maximum_fusion.2.refs_4_), channel_id=1, source_target_pairs={{0,8},{4,12},{8,0},{12,4},{16,24},{20,28},{24,16},{28,20},{1,9},{5... | collective-permute-start | bytes 2359304 | tf_op jit(solution)/shard_map/ppermute | solution.py:439
  99.4 39.1 %collective-permute-start.4 = (bf16[3,144,1024]{2,1,0:T(8,128)(2,1)S(1)}, bf16[3,144,1024]{2,1,0:T(8,128)(2,1)}, u32[]{:S(2)}, u32[]{:S(2)}) collective-permute-start(bf16[3,144,1024]{2,1,0:T(8,128)(2,1)S(1)} %pad_maximum_fusion.1.refs_5_), channel_id=1, source_target_pairs={{0,16},{4,20},{8,24},{12,28},{16,0},{20,4},{24,8},{28,12},{1,17},{... | collective-permute-start | bytes 2654216 | tf_op jit(solution)/shard_map/ppermute | solution.py:439
  101.7 60.1 %collective-permute-start.3 = (bf16[3,144,1024]{2,1,0:T(8,128)(2,1)S(1)}, bf16[3,144,1024]{2,1,0:T(8,128)(2,1)}, u32[]{:S(2)}, u32[]{:S(2)}) collective-permute-start(bf16[3,144,1024]{2,1,0:T(8,128)(2,1)S(1)} %pad_maximum_fusion.1.refs_5_), channel_id=1, source_target_pairs={{0,8},{4,12},{8,0},{12,4},{16,24},{20,28},{24,16},{28,20},{1,9},{5... | collective-permute-start | bytes 2654216 | tf_op jit(solution)/shard_map/ppermute | solution.py:439
  116.9 44.5 %collective-permute-start.26 = (bf16[3,128,1024]{2,1,0:T(8,128)(2,1)}, bf16[3,128,1024]{2,1,0:T(8,128)(2,1)}, u32[]{:S(2)}, u32[]{:S(2)}) collective-permute-start(bf16[3,128,1024]{2,1,0:T(8,128)(2,1)} %pad_maximum_fusion.2.refs_4_), channel_id=1, source_target_pairs={{0,4},{4,0},{8,12},{12,8},{16,20},{20,16},{24,28},{28,24},{1,5},{5... | collective-permute-start | bytes 2359304 | tf_op jit(solution)/shard_map/ppermute | solution.py:439
  213.2 140.2 %collective-permute-start.40 = (bf16[3,256,1024]{2,1,0:T(8,128)(2,1)}, bf16[3,256,1024]{2,1,0:T(8,128)(2,1)}, u32[]{:S(2)}, u32[]{:S(2)}) collective-permute-start(bf16[3,256,1024]{2,1,0:T(8,128)(2,1)} %pad_maximum_fusion.refs_2_), channel_id=1, source_target_pairs={{0,4},{4,0},{8,12},{12,8},{16,20},{20,16},{24,28},{28,24},{1,5},{5... | collective-permute-start | bytes 4718600 | tf_op jit(solution)/shard_map/ppermute | solution.py:439
  213.7 109.0 %collective-permute-start.37 = (bf16[3,256,1024]{2,1,0:T(8,128)(2,1)}, bf16[3,256,1024]{2,1,0:T(8,128)(2,1)}, u32[]{:S(2)}, u32[]{:S(2)}) collective-permute-start(bf16[3,256,1024]{2,1,0:T(8,128)(2,1)} %pad_maximum_fusion.refs_2_), channel_id=1, source_target_pairs={{0,16},{4,20},{8,24},{12,28},{16,0},{20,4},{24,8},{28,12},{1,17},{... | collective-permute-start | bytes 4718600 | tf_op jit(solution)/shard_map/ppermute | solution.py:439
  214.2 111.7 %collective-permute-start.36 = (bf16[3,256,1024]{2,1,0:T(8,128)(2,1)}, bf16[3,256,1024]{2,1,0:T(8,128)(2,1)}, u32[]{:S(2)}, u32[]{:S(2)}) collective-permute-start(bf16[3,256,1024]{2,1,0:T(8,128)(2,1)} %pad_maximum_fusion.refs_2_), channel_id=1, source_target_pairs={{0,8},{4,12},{8,0},{12,4},{16,24},{20,28},{24,16},{28,20},{1,9},{5... | collective-permute-start | bytes 4718600 | tf_op jit(solution)/shard_map/ppermute | solution.py:439
  490.3 65.0 %collective-permute-start.49 = (bf16[16,32,512]{2,1,0:T(8,128)(2,1)}, bf16[16,32,512]{2,1,0:T(8,128)(2,1)}, u32[]{:S(2)}, u32[]{:S(2)}) collective-permute-start(bf16[16,32,512]{2,1,0:T(8,128)(2,1)} %bitcast.98), channel_id=1, source_target_pairs={{0,4},{4,0},{8,12},{12,8},{16,20},{20,16},{24,28},{28,24},{1,5},{5... | collective-permute-start | bytes 1572872 | tf_op jit(solution)/shard_map/ppermute | solution.py:439
  524.3 35.8 %collective-permute-start.56 = (bf16[16,32,1024]{2,1,0:T(8,128)(2,1)}, bf16[16,32,1024]{2,1,0:T(8,128)(2,1)}, u32[]{:S(2)}, u32[]{:S(2)}) collective-permute-start(bf16[16,32,1024]{2,1,0:T(8,128)(2,1)} %bitcast.119), channel_id=1, source_target_pairs={{0,4},{4,0},{8,12},{12,8},{16,20},{20,16},{24,28},{28,24},{1,5},{5... | collective-permute-start | bytes 3145736 | tf_op jit(solution)/shard_map/ppermute | solution.py:439
  565.0 159.6 %collective-permute-start.88 = (bf16[16,32,4096]{2,1,0:T(8,128)(2,1)}, bf16[16,32,4096]{2,1,0:T(8,128)(2,1)}, u32[]{:S(2)}, u32[]{:S(2)}) collective-permute-start(bf16[16,32,4096]{2,1,0:T(8,128)(2,1)} %bitcast.152), channel_id=1, source_target_pairs={{0,4},{4,0},{8,12},{12,8},{16,20},{20,16},{24,28},{28,24},{1,5},{5... | collective-permute-start | bytes 12582920 | tf_op jit(solution)/shard_map/ppermute | solution.py:439
  565.1 159.5 %collective-permute-start.89 = (bf16[16,128,1024]{2,1,0:T(8,128)(2,1)}, bf16[16,128,1024]{2,1,0:T(8,128)(2,1)}, u32[]{:S(2)}, u32[]{:S(2)}) collective-permute-start(bf16[16,128,1024]{2,1,0:T(8,128)(2,1)} %bitcast.154), channel_id=1, source_target_pairs={{0,4},{4,0},{8,12},{12,8},{16,20},{20,16},{24,28},{28,24},{1,5},{5... | collective-permute-start | bytes 12582920 | tf_op jit(solution)/shard_map/ppermute | solution.py:439
  598.3 104.9 %collective-permute-start.62 = (bf16[4,160,1024]{2,1,0:T(8,128)(2,1)}, bf16[4,160,1024]{2,1,0:T(8,128)(2,1)}, u32[]{:S(2)}, u32[]{:S(2)}) collective-permute-start(bf16[4,160,1024]{2,1,0:T(8,128)(2,1)} %get-tuple-element.96), channel_id=1, source_target_pairs={{0,16},{4,20},{8,24},{12,28},{16,0},{20,4},{24,8},{28,12},{1,17},{... | collective-permute-start | bytes 3932168 | tf_op jit(solution)/shard_map/ppermute | solution.py:439
  613.5 94.3 %collective-permute-start.51 = (bf16[4,176,1024]{2,1,0:T(8,128)(2,1)}, bf16[4,176,1024]{2,1,0:T(8,128)(2,1)}, u32[]{:S(2)}, u32[]{:S(2)}) collective-permute-start(bf16[4,176,1024]{2,1,0:T(8,128)(2,1)} %get-tuple-element.88), channel_id=1, source_target_pairs={{0,8},{4,12},{8,0},{12,4},{16,24},{20,28},{24,16},{28,20},{1,9},{5... | collective-permute-start | bytes 4325384 | tf_op jit(solution)/shard_map/ppermute | solution.py:439
  618.9 91.6 %collective-permute-start.53 = (bf16[4,176,1024]{2,1,0:T(8,128)(2,1)}, bf16[4,176,1024]{2,1,0:T(8,128)(2,1)}, u32[]{:S(2)}, u32[]{:S(2)}) collective-permute-start(bf16[4,176,1024]{2,1,0:T(8,128)(2,1)} %get-tuple-element.90), channel_id=1, source_target_pairs={{0,16},{4,20},{8,24},{12,28},{16,0},{20,4},{24,8},{28,12},{1,17},{... | collective-permute-start | bytes 4325384 | tf_op jit(solution)/shard_map/ppermute | solution.py:439
  740.0 43.2 %collective-permute-start.93 = (bf16[4,256,1024]{2,1,0:T(8,128)(2,1)}, bf16[4,256,1024]{2,1,0:T(8,128)(2,1)S(1)}, u32[]{:S(2)}, u32[]{:S(2)}) collective-permute-start(bf16[4,256,1024]{2,1,0:T(8,128)(2,1)} %get-tuple-element.109), channel_id=1, source_target_pairs={{0,16},{4,20},{8,24},{12,28},{16,0},{20,4},{24,8},{28,12},{1,17},{... | collective-permute-start | bytes 6291464 | tf_op jit(solution)/shard_map/ppermute | solution.py:439
  740.6 48.3 %collective-permute-start.76 = (bf16[128,1024]{1,0:T(8,128)(2,1)S(1)}, bf16[128,1024]{1,0:T(8,128)(2,1)S(1)}, u32[]{:S(2)}, u32[]{:S(2)}) collective-permute-start(bf16[128,1024]{1,0:T(8,128)(2,1)S(1)} %fusion.27), channel_id=1, source_target_pairs={{0,1},{1,2},{2,3},{3,0},{4,5},{5,6},{6,7},{7,4},{8,9},{9,10},{10,1... | collective-permute-start | bytes 786440 | tf_op jit(solution)/shard_map/ppermute | solution.py:444
  740.7 47.6 %collective-permute-start.90 = (bf16[4,256,1024]{2,1,0:T(8,128)(2,1)}, bf16[4,256,1024]{2,1,0:T(8,128)(2,1)S(1)}, u32[]{:S(2)}, u32[]{:S(2)}) collective-permute-start(bf16[4,256,1024]{2,1,0:T(8,128)(2,1)} %get-tuple-element.107), channel_id=1, source_target_pairs={{0,8},{4,12},{8,0},{12,4},{16,24},{20,28},{24,16},{28,20},{1,9},{5... | collective-permute-start | bytes 6291464 | tf_op jit(solution)/shard_map/ppermute | solution.py:439
  744.2 45.5 %collective-permute-start.78 = (bf16[128,1024]{1,0:T(8,128)(2,1)S(1)}, bf16[128,1024]{1,0:T(8,128)(2,1)S(1)}, u32[]{:S(2)}, u32[]{:S(2)}) collective-permute-start(bf16[128,1024]{1,0:T(8,128)(2,1)S(1)} %fusion.29), channel_id=1, source_target_pairs={{0,3},{1,0},{2,1},{3,2},{4,7},{5,4},{6,5},{7,6},{8,11},{9,8},{10,9... | collective-permute-start | bytes 786440 | tf_op jit(solution)/shard_map/ppermute | solution.py:444
  750.9 43.7 %collective-permute-start.77 = (bf16[128,1024]{1,0:T(8,128)(2,1)S(1)}, bf16[128,1024]{1,0:T(8,128)(2,1)S(1)}, u32[]{:S(2)}, u32[]{:S(2)}) collective-permute-start(bf16[128,1024]{1,0:T(8,128)(2,1)S(1)} %fusion.28), channel_id=1, source_target_pairs={{0,2},{1,3},{2,0},{3,1},{4,6},{5,7},{6,4},{7,5},{8,10},{9,11},{10,... | collective-permute-start | bytes 786440 | tf_op jit(solution)/shard_map/ppermute | solution.py:444
  (213 other events, 3163.9 us)

commit v2 on v1

v2 whole, which is shorter than its diff:
```python
import functools

import jax
import jax.numpy as jnp
from jax import lax
from jax.experimental import pallas as pl
from jax.experimental.pallas import tpu as pltpu
from jax.sharding import PartitionSpec as P

HEAD_DIM = 64
BUCKETS = 32
LANE = 128
GROUP = 4
SUB = 8
eps_norm = 1e-05
neg_fill = -1e30
bf16 = jnp.bfloat16
f32 = jnp.float32
CORE, XBIT, YBIT = 1, 2, 4
VMEM_LIMIT = 63 * 1024 * 1024


def matmul(left_side, right_side):
    return jnp.dot(left_side, right_side, preferred_element_type=f32)


def matmul_back(left_side, right_side):
    return lax.dot_general(left_side, right_side, (((1,), (1,)), ((), ())), preferred_element_type=f32)


def outer_rows(left_side, right_side):
    return lax.dot_general(left_side, right_side, (((0,), (0,)), ((), ())), preferred_element_type=f32)


def norm_forward(values, gain, shift):
    row_mean = jnp.mean(values, axis=-1, keepdims=True)
    centered = values - row_mean
    scale = lax.rsqrt(jnp.mean(centered * centered, axis=-1, keepdims=True) + eps_norm)
    unit = centered * scale
    return unit * gain + shift, unit, scale


def norm_backward(unit, scale, gain, cotangent):
    back_unit = cotangent * gain
    first = jnp.mean(back_unit, axis=-1, keepdims=True)
    second = jnp.mean(back_unit * unit, axis=-1, keepdims=True)
    back = scale * (back_unit - first - unit * second)
    return back, jnp.sum(cotangent * unit, axis=0), jnp.sum(cotangent, axis=0)


def dot_nt(left_side, right_side):
    return lax.dot_general(left_side, right_side, (((1,), (1,)), ((), ())), preferred_element_type=f32)


def dot_nn(left_side, right_side):
    return lax.dot_general(left_side, right_side, (((1,), (0,)), ((), ())), preferred_element_type=f32)


def dot_tn(left_side, right_side):
    return lax.dot_general(left_side, right_side, (((0,), (0,)), ((), ())), preferred_element_type=f32)


def stack_heads(pair, low_half):
    zero = jnp.zeros_like(pair)
    return jnp.concatenate([jnp.where(low_half, pair, zero), jnp.where(low_half, zero, pair)], axis=0)


def rows_of(ref, first, last, cols):
    block = ref[first:last, 0, :, cols]
    return block.reshape(block.shape[0] * block.shape[1], block.shape[2])


def fill_one_hot(bucket_ref, one_hot_ref):
    keys = bucket_ref.shape[1]
    levels = lax.broadcasted_iota(jnp.int32, (BUCKETS, keys), 0)

    def fill(row, carry):
        line = jnp.broadcast_to(bucket_ref[pl.ds(row, 1), :], (BUCKETS, keys))
        start = pl.multiple_of(lax.rem(row, SUB) * BUCKETS, BUCKETS)
        one_hot_ref[row // SUB, pl.ds(start, BUCKETS), :] = jnp.where(line == levels, 1.0, 0.0).astype(bf16)
        return carry

    lax.fori_loop(0, bucket_ref.shape[0], fill, 0)


def fill_buckets(distance, bounds_ref, bucket_ref):
    bucket_ref[...] = jnp.zeros(distance.shape, jnp.int32)

    def fill(level, carry):
        bucket_ref[...] += (distance >= bounds_ref[level]).astype(jnp.int32)
        return carry

    lax.fori_loop(1, BUCKETS, fill, 0)


def own_block_mask(rows):
    row = lax.broadcasted_iota(jnp.int32, (rows, SUB * BUCKETS), 0)
    col = lax.broadcasted_iota(jnp.int32, (rows, SUB * BUCKETS), 1)
    return (row & (SUB - 1)) == (col // BUCKETS)


def self_forward_kernel(
    length_ref, bounds_ref, posq_ref, posk_ref, q_ref, e_ref, k_ref, v_ref, o_ref, p_ref, own_ref,
    bucket_ref, one_hot_ref, spread_ref, bias_ref,
):
    slot = pl.program_id(0)
    group = pl.program_id(1)
    lanes, _, rows, _ = q_ref.shape
    pieces = k_ref.shape[0] - (lanes - 1)
    keys = pieces * k_ref.shape[2]
    heads = bias_ref.shape[0]
    span = SUB * BUCKETS

    @pl.when((slot == 0) & (group == 0))
    def _():
        fill_buckets(posq_ref[...] - posk_ref[...], bounds_ref, bucket_ref)
        fill_one_hot(bucket_ref, one_hot_ref)

    @pl.when(group == 0)
    def _():
        keep = own_block_mask(lanes * rows)
        source = lax.broadcasted_iota(jnp.int32, (LANE, span), 0)
        target = lax.broadcasted_iota(jnp.int32, (LANE, span), 1) & (BUCKETS - 1)
        for part in range(LANE // BUCKETS):
            copy = jnp.where(source == target + part * BUCKETS, 1.0, 0.0).astype(bf16)
            for block in range(heads * BUCKETS // LANE):
                rows_e = rows_of(e_ref, 0, lanes, slice(block * LANE, (block + 1) * LANE))
                head = block * (LANE // BUCKETS) + part
                spread_ref[head] = jnp.where(keep, dot_nn(rows_e, copy), 0.0)
        distance = posq_ref[...] - posk_ref[...]
        valid = posk_ref[...] < length_ref[slot]
        fills = [jnp.where(valid & (distance >= edge), 0.0, neg_fill) for edge in (0, 1)]
        for g in range(rows // SUB):
            starts = [lane * rows + g * SUB for lane in range(lanes)]
            left = [spread_ref[:, start : start + SUB, :].reshape(heads * SUB, span) for start in starts]
            bias = dot_nn(jnp.concatenate(left, axis=0).astype(bf16), one_hot_ref[g])
            bias = bias.reshape(lanes, heads, SUB, keys)
            for lane, start in enumerate(starts):
                fill = fills[min(lane, 1)][None, g * SUB : (g + 1) * SUB, :]
                bias_ref[:, start : start + SUB, :] = bias[lane] + fill

    low_half = lax.broadcasted_iota(jnp.int32, (1, LANE), 1) < HEAD_DIM
    lane_id = lax.broadcasted_iota(jnp.int32, (1, LANE), 1)
    own_all = [jnp.zeros((rows, LANE), f32) for _ in range(lanes)]
    e_cols = pl.ds(pl.multiple_of(group * (GROUP * BUCKETS), LANE), GROUP * BUCKETS)
    tables = [None] + [e_ref[lane, 0, :, e_cols].astype(f32) for lane in range(1, lanes)]
    for pair in range(GROUP // 2):
        cols = slice(pair * LANE, (pair + 1) * LANE)
        q_pair = rows_of(q_ref, 0, lanes, cols) * jnp.asarray(HEAD_DIM**-0.5, bf16)
        k_main = rows_of(k_ref, 0, pieces, cols)
        v_main = rows_of(v_ref, 0, pieces, cols)
        scores = dot_nt(stack_heads(q_pair, low_half), k_main)
        own_pair = []
        for half in range(2):
            head = pair * 2 + half
            keep = low_half if half == 0 else jnp.logical_not(low_half)
            for lane in range(lanes):
                start = (half * lanes + lane) * rows
                part = scores[start : start + rows]
                part = part + bias_ref[group * GROUP + head, lane * rows : (lane + 1) * rows, :]
                top = jnp.max(part, axis=1, keepdims=True)
                if lane > 0:
                    q_row = q_pair[lane * rows : (lane + 1) * rows].astype(f32)
                    k_row = k_ref[pieces + lane - 1, 0, :, cols].astype(f32)
                    own = jnp.sum(jnp.where(keep, q_row * k_row, 0.0), axis=1, keepdims=True)
                    own = own + tables[lane][:, head * BUCKETS : head * BUCKETS + 1]
                    top = jnp.maximum(top, own)
                    own_exp = jnp.exp(own - top)
                terms = jnp.exp(part - top)
                total = jnp.sum(terms, axis=1, keepdims=True)
                if lane > 0:
                    total = total + own_exp
                inverse = 1.0 / total
                p_ref[0, head, lane * rows : (lane + 1) * rows, :] = (terms * inverse).astype(bf16)
                if lane > 0:
                    own_prob = own_exp * inverse
                    own_all[lane] = jnp.where(lane_id == head, own_prob, own_all[lane])
                else:
                    own_prob = jnp.zeros((rows, 1), f32)
                own_pair.append(own_prob)
        p_low = p_ref[0, pair * 2 : pair * 2 + 2].reshape(2 * lanes * rows, keys)
        mixed = dot_nn(p_low, v_main)
        for lane in range(lanes):
            first = lane * rows
            second = (lanes + lane) * rows
            out = jnp.where(low_half, mixed[first : first + rows], mixed[second : second + rows])
            if lane > 0:
                own_prob = jnp.where(low_half, own_pair[lane], own_pair[lanes + lane])
                v_row = v_ref[pieces + lane - 1, 0, :, cols].astype(f32)
                out = out + own_prob.astype(bf16).astype(f32) * v_row
            o_ref[lane, 0, :, cols] = out.astype(bf16)
    for lane in range(lanes):
        own_ref[0, 0, lane * rows : (lane + 1) * rows, :] = own_all[lane]


def self_backward_kernel(
    held, bounds_ref, posq_ref, posk_ref, p_ref, own_ref, do_ref, q_ref, k_ref, v_ref, *refs,
):
    dq_ref, dk_ref, dv_ref, de_ref = refs[held : held + 4]
    bucket_ref, one_hot_ref, turned_ref, scores_ref, down_ref, wide_ref = refs[held + 4 :]
    group = pl.program_id(1)
    lanes, _, rows, _ = q_ref.shape
    pieces = k_ref.shape[0] - (lanes - 1)
    piece_rows = k_ref.shape[2]
    keys = pieces * piece_rows
    scale = HEAD_DIM**-0.5

    heads = scores_ref.shape[0]
    span = SUB * BUCKETS

    @pl.when((pl.program_id(0) == 0) & (group == 0))
    def _():
        fill_buckets(posq_ref[...] - posk_ref[...], bounds_ref, bucket_ref)
        fill_one_hot(bucket_ref, one_hot_ref)
        for g in range(rows // SUB):
            turned_ref[g] = one_hot_ref[g].T

    lane_id = lax.broadcasted_iota(jnp.int32, (1, LANE), 1)
    low_half = lane_id < HEAD_DIM
    downs = [jnp.zeros((rows, LANE), f32) for _ in range(lanes)]
    for pair in range(GROUP // 2):
        cols = slice(pair * LANE, (pair + 1) * LANE)
        q_pair = rows_of(q_ref, 0, lanes, cols) * jnp.asarray(scale, bf16)
        do_pair = rows_of(do_ref, 0, lanes, cols)
        k_main = rows_of(k_ref, 0, pieces, cols)
        v_main = rows_of(v_ref, 0, pieces, cols)
        q_stack = stack_heads(q_pair, low_half)
        do_stack = stack_heads(do_pair, low_half)
        back_probs = dot_nt(do_stack, v_main)
        p_low = p_ref[0, pair * 2 : pair * 2 + 2].reshape(2 * lanes * rows, keys)
        probs = p_low.astype(f32)
        weighted = probs * back_probs
        delta = jnp.sum(weighted, axis=1, keepdims=True)
        down_pair = []
        delta_list = []
        for half in range(2):
            head = pair * 2 + half
            keep = low_half if half == 0 else jnp.logical_not(low_half)
            for lane in range(lanes):
                start = (half * lanes + lane) * rows
                part = delta[start : start + rows]
                if lane > 0:
                    do_row = do_pair[lane * rows : (lane + 1) * rows].astype(f32)
                    v_row = v_ref[pieces + lane - 1, 0, :, cols].astype(f32)
                    back_own = jnp.sum(jnp.where(keep, do_row * v_row, 0.0), axis=1, keepdims=True)
                    own_prob = own_ref[0, 0, lane * rows : (lane + 1) * rows, head : head + 1]
                    part = part + own_prob * back_own
                    down_pair.append((own_prob * (back_own - part)).astype(bf16).astype(f32))
                else:
                    down_pair.append(None)
                delta_list.append(part)
        delta = jnp.concatenate(delta_list, axis=0)
        back_scores = (weighted - probs * delta).astype(bf16)
        back_q = dot_nn(back_scores, k_main)
        back_k = dot_tn(q_stack, back_scores)
        back_v = dot_tn(do_stack, p_low)
        dk_ref[:pieces, 0, :, cols] = back_k.T.astype(bf16).reshape(pieces, piece_rows, LANE)
        dv_ref[:pieces, 0, :, cols] = back_v.T.astype(bf16).reshape(pieces, piece_rows, LANE)
        scores_ref[pl.ds(group * GROUP + pair * 2, 2)] = back_scores.astype(f32).reshape(2, lanes * rows, keys)
        for lane in range(lanes):
            first = lane * rows
            second = (lanes + lane) * rows
            back = jnp.where(low_half, back_q[first : first + rows], back_q[second : second + rows])
            if lane > 0:
                k_row = k_ref[pieces + lane - 1, 0, :, cols].astype(f32)
                down = jnp.where(low_half, down_pair[lane], down_pair[lanes + lane])
                back = back + down * k_row
                own_low = jnp.where(
                    low_half,
                    own_ref[0, 0, lane * rows : (lane + 1) * rows, pair * 2 : pair * 2 + 1],
                    own_ref[0, 0, lane * rows : (lane + 1) * rows, pair * 2 + 1 : pair * 2 + 2],
                )
                own_low = own_low.astype(bf16).astype(f32)
                dk_ref[pieces + lane - 1, 0, :, cols] = (
                    down * q_pair[first : first + rows].astype(f32)
                ).astype(bf16)
                dv_ref[pieces + lane - 1, 0, :, cols] = (
                    own_low * do_pair[first : first + rows].astype(f32)
                ).astype(bf16)
            dq_ref[lane, 0, :, cols] = (back * scale).astype(bf16)
            if lane > 0:
                for half in range(2):
                    spot = (pair * 2 + half) * BUCKETS
                    downs[lane] = jnp.where(lane_id == spot, down_pair[half * lanes + lane], downs[lane])
    for lane in range(1, lanes):
        down_ref[group, lane] = downs[lane]

    @pl.when(group == pl.num_programs(1) - 1)
    def _():
        keep = own_block_mask(lanes * heads * SUB)
        source = lax.broadcasted_iota(jnp.int32, (span, LANE), 0) & (BUCKETS - 1)
        target = lax.broadcasted_iota(jnp.int32, (span, LANE), 1) & (BUCKETS - 1)
        fold = jnp.where(source == target, 1.0, 0.0).astype(bf16)
        per_block = LANE // BUCKETS
        for g in range(rows // SUB):
            starts = [lane * rows + g * SUB for lane in range(lanes)]
            left = [scores_ref[:, start : start + SUB, :].reshape(heads * SUB, keys) for start in starts]
            sums = dot_nn(jnp.concatenate(left, axis=0).astype(bf16), turned_ref[g])
            embed = dot_nn(jnp.where(keep, sums, 0.0).astype(bf16), fold).reshape(lanes, heads, SUB, LANE)
            for lane in range(lanes):
                for block in range(heads // per_block):
                    out = embed[lane, block * per_block]
                    for part in range(1, per_block):
                        out = jnp.where(lane_id // BUCKETS == part, embed[lane, block * per_block + part], out)
                    if lane > 0:
                        out = out + down_ref[block, lane, g * SUB : (g + 1) * SUB, :]
                    wide_ref[lane, g * SUB : (g + 1) * SUB, block * LANE : (block + 1) * LANE] = out
        for lane in range(lanes):
            de_ref[lane, 0] = wide_ref[lane].astype(bf16)


def cross_forward_kernel(length_ref, posk_ref, q_ref, k_ref, v_ref, o_ref, p_ref):
    slot = pl.program_id(0)
    lanes, _, rows, _ = q_ref.shape
    pieces = k_ref.shape[0]
    keys = pieces * k_ref.shape[2]
    low_half = lax.broadcasted_iota(jnp.int32, (1, LANE), 1) < HEAD_DIM
    fill = jnp.where(posk_ref[...] < length_ref[slot], 0.0, neg_fill)
    count = lanes * rows
    for pair in range(GROUP // 2):
        cols = slice(pair * LANE, (pair + 1) * LANE)
        q_pair = rows_of(q_ref, 0, lanes, cols) * jnp.asarray(HEAD_DIM**-0.5, bf16)
        k_main = rows_of(k_ref, 0, pieces, cols)
        v_main = rows_of(v_ref, 0, pieces, cols)
        scores = dot_nt(stack_heads(q_pair, low_half), k_main) + fill
        top = jnp.max(scores, axis=1, keepdims=True)
        terms = jnp.exp(scores - top)
        inverse = 1.0 / jnp.sum(terms, axis=1, keepdims=True)
        p_low = (terms * inverse).astype(bf16)
        p_ref[0, pair * 2 : pair * 2 + 2] = p_low.reshape(2, count, keys)
        mixed = dot_nn(p_low, v_main)
        out = jnp.where(low_half, mixed[:count], mixed[count:]).astype(bf16)
        o_ref[:, 0, :, cols] = out.reshape(lanes, rows, LANE)


def cross_backward_kernel(p_ref, do_ref, q_ref, k_ref, v_ref, dq_ref, dk_ref, dv_ref):
    lanes, _, rows, _ = q_ref.shape
    pieces = k_ref.shape[0]
    piece_rows = k_ref.shape[2]
    keys = pieces * piece_rows
    count = lanes * rows
    scale = HEAD_DIM**-0.5
    low_half = lax.broadcasted_iota(jnp.int32, (1, LANE), 1) < HEAD_DIM
    for pair in range(GROUP // 2):
        cols = slice(pair * LANE, (pair + 1) * LANE)
        q_pair = rows_of(q_ref, 0, lanes, cols) * jnp.asarray(scale, bf16)
        do_pair = rows_of(do_ref, 0, lanes, cols)
        k_main = rows_of(k_ref, 0, pieces, cols)
        v_main = rows_of(v_ref, 0, pieces, cols)
        q_stack = stack_heads(q_pair, low_half)
        do_stack = stack_heads(do_pair, low_half)
        back_probs = dot_nt(do_stack, v_main)
        p_low = p_ref[0, pair * 2 : pair * 2 + 2].reshape(2 * count, keys)
        probs = p_low.astype(f32)
        weighted = probs * back_probs
        delta = jnp.sum(weighted, axis=1, keepdims=True)
        back_scores = (weighted - probs * delta).astype(bf16)
        back_q = dot_nn(back_scores, k_main)
        back_k = dot_tn(q_stack, back_scores)
        back_v = dot_tn(do_stack, p_low)
        dk_ref[:, 0, :, cols] = back_k.T.astype(bf16).reshape(pieces, piece_rows, LANE)
        dv_ref[:, 0, :, cols] = back_v.T.astype(bf16).reshape(pieces, piece_rows, LANE)
        back = jnp.where(low_half, back_q[:count], back_q[count:]) * scale
        dq_ref[:, 0, :, cols] = back.astype(bf16).reshape(lanes, rows, LANE)


def head_block(array, width=GROUP * HEAD_DIM):
    return pl.BlockSpec((array.shape[0], 1, array.shape[2], width), lambda s, g: (0, s, 0, g))


def slot_block(array):
    return pl.BlockSpec((array.shape[0], 1) + array.shape[2:], lambda s, g: (0, s, 0, 0))


def whole_block(array):
    return pl.BlockSpec(array.shape, lambda s, g: (0,) * array.ndim)


SMALL = pl.CostEstimate(flops=1000, bytes_accessed=1000, transcendentals=0)
SMEM_SPEC = pl.BlockSpec(memory_space=pltpu.SMEM)


def params():
    return pltpu.CompilerParams(vmem_limit_bytes=VMEM_LIMIT)


def shaped(shape, dtype):
    return jax.ShapeDtypeStruct(shape, dtype)


def self_forward(length, bounds, posq, posk, q, e, k, v):
    lanes, slots, rows, width = q.shape
    heads = width // HEAD_DIM
    keys = posk.shape[1]
    count = lanes * rows
    groups = heads // GROUP
    return pl.pallas_call(
        self_forward_kernel,
        grid=(slots, groups),
        in_specs=[
            SMEM_SPEC, SMEM_SPEC, whole_block(posq), whole_block(posk),
            head_block(q), slot_block(e), head_block(k), head_block(v),
        ],
        out_specs=[
            head_block(q),
            pl.BlockSpec((1, GROUP, count, keys), lambda s, g: (s, g, 0, 0)),
            pl.BlockSpec((1, 1, count, LANE), lambda s, g: (s, g, 0, 0)),
        ],
        out_shape=[
            shaped(q.shape, bf16),
            shaped((slots, heads, count, keys), bf16),
            shaped((slots, groups, count, LANE), f32),
        ],
        scratch_shapes=[
            pltpu.VMEM((rows, keys), jnp.int32),
            pltpu.VMEM((rows // SUB, SUB * BUCKETS, keys), bf16),
            pltpu.VMEM((heads, count, SUB * BUCKETS), f32),
            pltpu.VMEM((heads, count, keys), f32),
        ],
        compiler_params=params(),
        cost_estimate=SMALL,
        name="self_forward",
    )(length, bounds, posq, posk, q, e, k, v)


def self_backward(bounds, posq, posk, p, own, do, q, k, v, part, parts, made=()):
    lanes, slots, rows, width = q.shape
    heads = width // HEAD_DIM // parts
    keys = p.shape[3]
    count = lanes * rows
    groups = heads // GROUP
    base = part * groups

    def block(array):
        return pl.BlockSpec((array.shape[0], 1, array.shape[2], GROUP * HEAD_DIM), lambda s, g: (0, s, 0, base + g))

    inputs = [bounds, posq, posk, p, own, do, q, k, v]
    return pl.pallas_call(
        functools.partial(self_backward_kernel, len(made)),
        grid=(slots, groups),
        in_specs=[
            SMEM_SPEC, whole_block(posq), whole_block(posk),
            pl.BlockSpec((1, GROUP, count, keys), lambda s, g: (s, base + g, 0, 0)),
            pl.BlockSpec((1, 1, count, LANE), lambda s, g: (s, base + g, 0, 0)),
            block(do), block(q), block(k), block(v),
        ] + [pl.BlockSpec(memory_space=pl.ANY)] * len(made),
        out_specs=[
            block(q), block(k), block(v),
            pl.BlockSpec((lanes, 1, rows, heads * BUCKETS), lambda s, g: (0, s, 0, part)),
        ],
        out_shape=[
            shaped(q.shape, bf16), shaped(k.shape, bf16), shaped(v.shape, bf16),
            shaped((lanes, slots, rows, heads * parts * BUCKETS), bf16),
        ],
        scratch_shapes=[
            pltpu.VMEM((rows, keys), jnp.int32),
            pltpu.VMEM((rows // SUB, SUB * BUCKETS, keys), bf16),
            pltpu.VMEM((rows // SUB, keys, SUB * BUCKETS), bf16),
            pltpu.VMEM((heads, count, keys), f32),
            pltpu.VMEM((groups, lanes, rows, LANE), f32),
            pltpu.VMEM((lanes, rows, heads * BUCKETS), f32),
        ],
        input_output_aliases={len(inputs) + i: i for i in range(len(made))},
        compiler_params=params(),
        cost_estimate=SMALL,
        name="self_backward",
    )(*inputs, *made)


def cross_forward(length, posk, q, k, v):
    lanes, slots, rows, width = q.shape
    heads = width // HEAD_DIM
    keys = posk.shape[1]
    count = lanes * rows
    return pl.pallas_call(
        cross_forward_kernel,
        grid=(slots, heads // GROUP),
        in_specs=[SMEM_SPEC, whole_block(posk), head_block(q), head_block(k), head_block(v)],
        out_specs=[head_block(q), pl.BlockSpec((1, GROUP, count, keys), lambda s, g: (s, g, 0, 0))],
        out_shape=[shaped(q.shape, bf16), shaped((slots, heads, count, keys), bf16)],
        compiler_params=params(),
        cost_estimate=SMALL,
        name="cross_forward",
    )(length, posk, q, k, v)


def cross_backward(p, do, q, k, v):
    lanes, slots, rows, width = q.shape
    heads = width // HEAD_DIM
    keys = p.shape[3]
    count = lanes * rows
    return pl.pallas_call(
        cross_backward_kernel,
        grid=(slots, heads // GROUP),
        in_specs=[
            pl.BlockSpec((1, GROUP, count, keys), lambda s, g: (s, g, 0, 0)),
            head_block(do), head_block(q), head_block(k), head_block(v),
        ],
        out_specs=[head_block(q), head_block(k), head_block(v)],
        out_shape=[shaped(q.shape, bf16), shaped(k.shape, bf16), shaped(v.shape, bf16)],
        compiler_params=params(),
        cost_estimate=SMALL,
        name="cross_backward",
    )(p, do, q, k, v)


FEED_BLOCK = 512


def norm_parts(values):
    row_mean = jnp.mean(values, axis=-1, keepdims=True)
    centered = values - row_mean
    scale = lax.rsqrt(jnp.mean(centered * centered, axis=-1, keepdims=True) + eps_norm)
    return centered * scale, scale


def feed_kernel(
    sending, loading, core_ref, base_ref, mixed_ref, outer_ref, norms_ref, cot_ref, valid_ref, *refs,
):
    layout, copies, cut, parts, number_in = loading
    sources, refs = refs[:number_in], refs[number_in:]
    feed_body(sending, (layout, copies, cut, parts, sources), core_ref, base_ref, mixed_ref, outer_ref, norms_ref, cot_ref, valid_ref, *refs)


def feed_body(
    sending, loading, core_ref, base_ref, mixed_ref, outer_ref, norms_ref, cot_ref, valid_ref,
    out_ref, low_ref, act_ref, back_pre_ref, feed_ref, back_ref, cross_ref, back_mixed_ref, grads_ref, *rest,
):
    if sending:
        up_send_ref, down_send_ref, outer_send_ref, *rest = rest
    unit_ref, total_ref, turned_ref, act_all_ref, slope_ref, row_scale_ref, up_all_ref, down_all_ref, sems = rest
    phase, block = pl.program_id(0), pl.program_id(1)
    last = pl.num_programs(1) - 1
    cols = pl.ds(pl.multiple_of(block * FEED_BLOCK, FEED_BLOCK), FEED_BLOCK)

    up_ref = lambda: up_all_ref[:, cols]
    down_ref = lambda: down_all_ref[cols, :]
    layout, copies, cut, parts, sources = loading

    def loads():
        return group_loads(layout, copies, cut, parts, core_ref, sources, (up_all_ref, down_all_ref), sems, 1)

    @pl.when((phase == 0) & (block == 0))
    def _():
        for _, load in loads():
            load.start()
        unit, scale = norm_parts(base_ref[...] + dot_nn(mixed_ref[...], outer_ref[...]))
        normed = unit * norms_ref[2:3, :] + norms_ref[3:4, :]
        unit_ref[...] = unit
        row_scale_ref[...] = scale
        total_ref[...] = normed
        low_ref[...] = normed.astype(bf16)
        if sending:
            turned_ref[...] = core_columns(low_ref, 1 - core_ref[0], sending).T
        for _, load in loads():
            load.wait()

    @pl.when(phase == 0)
    def _():
        pre = dot_nn(low_ref[...], up_ref())
        below = 0.5 * (1.0 + lax.erf(pre * 0.7071067811865476))
        act = (pre * below).astype(bf16)
        slope_ref[:, cols] = below + pre * (jnp.exp(-0.5 * pre * pre) * 0.3989422804014327)
        act_all_ref[:, cols] = act
        act_ref[...] = act
        total_ref[...] += dot_nn(act, down_ref())

    @pl.when((phase == 0) & (block == last))
    def _():
        unit, scale = norm_parts(total_ref[...])
        gain = norms_ref[4:5, :]
        out_ref[...] = (unit * gain + norms_ref[5:6, :]).astype(bf16)
        cotangent = cot_ref[...].astype(f32) * valid_ref[...]
        back, gain_grad, shift_grad = norm_backward(unit, scale, gain, cotangent)
        grads_ref[2:3, :] = gain_grad[None]
        grads_ref[3:4, :] = shift_grad[None]
        total_ref[...] = back
        feed_ref[...] = back.astype(bf16)

    @pl.when(phase == 1)
    def _():
        back_act = dot_nt(feed_ref[...], down_ref())
        back_pre = (back_act * slope_ref[:, cols]).astype(bf16)
        back_pre_ref[...] = back_pre
        total_ref[...] += dot_nt(back_pre, up_ref())
        if sending:
            up_send_ref[...] = dot_nn(turned_ref[...], back_pre).astype(bf16)

            @pl.when((block & 1) == 1 - core_ref[0])
            def _():
                down_send_ref[...] = dot_tn(act_all_ref[:, cols], feed_ref[...]).astype(bf16)

    @pl.when((phase == 1) & (block == last))
    def _():
        back, gain_grad, shift_grad = norm_backward(
            unit_ref[...], row_scale_ref[...], norms_ref[2:3, :], total_ref[...]
        )
        back_ref[...] = back
        cross_ref[...] = back.astype(bf16)
        back_mixed_ref[...] = dot_nt(cross_ref[...], outer_ref[...]).astype(bf16)
        if sending:
            outer_send_ref[...] = dot_tn(core_columns(mixed_ref, 1 - core_ref[0], sending), cross_ref[...]).astype(bf16)
        grads_ref[0:1, :] = gain_grad[None]
        grads_ref[1:2, :] = shift_grad[None]


def feed_forward_backward(base, mixed, outer, norms, cot, valid, weights, arrivals, layout, cut, place, steps, sending):
    rows, width = base.shape
    hidden = layout[0][1]
    blocks = hidden // FEED_BLOCK
    copies, _ = block_copies(layout)
    sources = [*weights, *arrivals]
    parts = steps if arrivals else 1
    single = pl.Buffered(1)
    whole = lambda array: pl.BlockSpec(array.shape, lambda p, b, c: (0, 0), pipeline_mode=single)
    full = pl.BlockSpec((rows, width), lambda p, b, c: (0, 0))
    first = lambda p, b: jnp.where(p == 0, b, blocks - 1)
    second = lambda p, b: jnp.where(p == 0, 0, b)
    out_specs = [
        full, full,
        pl.BlockSpec((rows, FEED_BLOCK), lambda p, b, c: (0, first(p, b))),
        pl.BlockSpec((rows, FEED_BLOCK), lambda p, b, c: (0, second(p, b))),
        full, full, full, full,
        pl.BlockSpec((4, width), lambda p, b, c: (0, 0)),
    ]
    low = shaped((rows, width), bf16)
    wide = shaped((rows, hidden), bf16)
    out_shape = [low, low, wide, wide, low, shaped((rows, width), f32), low, low, shaped((4, width), f32)]
    if sending:
        assert hidden // (2 * steps) == FEED_BLOCK
        out_specs += [
            pl.BlockSpec((width // 2, FEED_BLOCK), lambda p, b, c: (0, second(p, b))),
            pl.BlockSpec((FEED_BLOCK, width), lambda p, b, c: (second(p, b) // 2, 0)),
            pl.BlockSpec((width // 2, width), lambda p, b, c: (0, 0)),
        ]
        out_shape += [
            shaped((width // 2, hidden), bf16), shaped((hidden // 2, width), bf16), shaped((width // 2, width), bf16),
        ]
    return pl.pallas_call(
        functools.partial(feed_kernel, steps if sending else 0, (layout, copies, cut, parts, len(sources))),
        grid_spec=pltpu.PrefetchScalarGridSpec(
            num_scalar_prefetch=1,
            grid=(2, blocks),
            in_specs=[
                whole(base), whole(mixed), whole(outer), whole(norms), whole(cot), whole(valid),
            ] + [pl.BlockSpec(memory_space=pl.ANY)] * len(sources),
            out_specs=out_specs,
            scratch_shapes=[
                pltpu.VMEM((rows, width), f32), pltpu.VMEM((rows, width), f32),
                pltpu.VMEM((width // 2, rows), bf16), pltpu.VMEM((rows, hidden), bf16), pltpu.VMEM((rows, hidden), f32),
                pltpu.VMEM((rows, 1), f32),
                pltpu.VMEM((width, hidden), bf16), pltpu.VMEM((hidden, width), bf16), pltpu.SemaphoreType.DMA((2,)),
            ],
        ),
        out_shape=out_shape,
        compiler_params=params(),
        cost_estimate=SMALL,
        name="feed",
    )(place, base, mixed, outer, norms, cot, valid, *sources)


def middle_kernel(
    sending, core_ref, back_cq_ref, query_ref, back_two_ref, unit_ref, scale_ref, norms_ref, outer_ref, *refs
):
    if sending:
        normed_ref, mixed_ref, back_ref, low_ref, back_mixed_ref, grads_ref, query_send_ref, outer_send_ref = refs
    else:
        back_ref, low_ref, back_mixed_ref, grads_ref = refs
    total = back_two_ref[...] + dot_nt(back_cq_ref[...], query_ref[...])
    back, gain_grad, shift_grad = norm_backward(unit_ref[...], scale_ref[...], norms_ref[0:1, :], total)
    back_ref[...] = back
    low_ref[...] = back.astype(bf16)
    grads_ref[0:1, :] = gain_grad[None]
    grads_ref[1:2, :] = shift_grad[None]
    back_mixed_ref[...] = dot_nt(low_ref[...], outer_ref[...]).astype(bf16)
    if sending:
        for left, right, out in ((normed_ref, back_cq_ref, query_send_ref), (mixed_ref, low_ref, outer_send_ref)):
            out[...] = dot_tn(core_columns(left, 1 - core_ref[0], sending), right[...]).astype(bf16)


def middle_backward(back_cq, query, back_two, unit, scale, norms, outer, normed, mixed, core, steps, sending):
    rows, width = back_two.shape
    low = shaped((rows, width), bf16)
    out_shape = [shaped((rows, width), f32), low, low, shaped((2, width), f32)]
    inputs = [back_cq, query, back_two, unit, scale, norms, outer]
    if sending:
        out_shape += [shaped((width // 2, width), bf16)] * 2
        inputs += [normed, mixed]
    vmem = pl.BlockSpec(memory_space=pltpu.VMEM)
    return pl.pallas_call(
        functools.partial(middle_kernel, steps if sending else 0),
        in_specs=[SMEM_SPEC] + [vmem] * len(inputs),
        out_specs=[vmem] * len(out_shape),
        out_shape=out_shape,
        compiler_params=params(),
        cost_estimate=SMALL,
        name="middle_backward",
    )(core, *inputs)


def pair_rows_kernel(tiles, back_k_ref, back_v_ref, key_ref, value_ref, even_ref, odd_ref, *rest):
    total = dot_nt(back_k_ref[...], key_ref[...]) + dot_nt(back_v_ref[...], value_ref[...])
    half = even_ref.shape[1]
    step = pl.program_id(0)

    @pl.when(step < tiles)
    def _():
        even_ref[0] = total[:half].astype(bf16)
        odd_ref[0] = total[half:].astype(bf16)

    if rest:

        @pl.when(step >= tiles)
        def _():
            rest[0][...] = total


def pair_rows(back_k, back_v, key, value, pieces, piece_rows):
    count, width = back_k.shape[0], key.shape[0]
    tile = 2 * piece_rows
    tiles = pieces // 2
    steps = count // tile
    resident = lambda array: pl.BlockSpec(array.shape, lambda t: (0, 0), pipeline_mode=pl.Buffered(1))
    rows = pl.BlockSpec((tile, back_k.shape[1]), lambda t: (t, 0))
    part = pl.BlockSpec((1, piece_rows, width), lambda t: (jnp.minimum(t, tiles - 1), 0, 0))
    out_specs, out_shape = [part, part], [shaped((tiles, piece_rows, width), bf16)] * 2
    if steps > tiles:
        out_specs.append(pl.BlockSpec((tile, width), lambda t: (jnp.maximum(t - tiles, 0), 0)))
        out_shape.append(shaped((count - tiles * tile, width), f32))
    return pl.pallas_call(
        functools.partial(pair_rows_kernel, tiles),
        grid=(steps,),
        in_specs=[rows, rows, resident(key), resident(value)],
        out_specs=out_specs,
        out_shape=out_shape,
        compiler_params=params(),
        cost_estimate=SMALL,
        name="pair_rows",
    )(back_k, back_v, key, value)


def own_rows_kernel(back_ref, back_q_ref, back_e_ref, query_ref, relative_ref, other_ref, out_ref):
    total = back_ref[...] + dot_nt(back_q_ref[...], query_ref[...]) + dot_nt(back_e_ref[...], relative_ref[...])
    skip = total.shape[0] - other_ref.shape[0]
    out_ref[:skip, :] = total[:skip]
    out_ref[skip:, :] = total[skip:] + other_ref[...]


def own_rows(back, back_q, back_e, query, relative, other):
    vmem = pl.BlockSpec(memory_space=pltpu.VMEM)
    return pl.pallas_call(
        own_rows_kernel,
        in_specs=[vmem] * 6,
        out_specs=vmem,
        out_shape=shaped(back.shape, f32),
        compiler_params=params(),
        cost_estimate=SMALL,
        name="own_rows",
    )(back, back_q, back_e, query, relative, other)


def after(value, *others):
    return lax.optimization_barrier((value,) + others)[0]


def ctx_hop(array, bit):
    size = lax.axis_size("ctx")
    return lax.ppermute(array, "ctx", [(i, i ^ bit) for i in range(size)])


def z_hop(array, step):
    size = lax.axis_size("fsdp")
    return lax.ppermute(array, "fsdp", [(i, (i + step) % size) for i in range(size)])


def first_spread(array):
    return array, ctx_hop(array, XBIT), ctx_hop(array, YBIT)


def corner_spread(firsts, axis, cut, *held):
    array, from_x, from_y = firsts
    if held:
        from_x, from_y, *_ = lax.optimization_barrier((from_x, from_y, *held))
    size = array.shape[axis]
    corner_one = ctx_hop(lax.slice_in_dim(from_y, 0, cut, axis=axis), XBIT)
    corner_two = ctx_hop(lax.slice_in_dim(from_x, cut, size, axis=axis), YBIT)
    return [array, from_x, from_y, corner_one, corner_two]


def core_spread(near):
    return near + [ctx_hop(item, CORE) for item in near]


def ctx_spread(array, axis, cut):
    return core_spread(corner_spread(first_spread(array), axis, cut))


SPREAD_PLAN = tuple(
    (offset + core, part) for core in (0, 1) for offset, part in ((0, 0), (XBIT, 0), (YBIT, 0), (XBIT + YBIT, 1), (XBIT + YBIT, 2))
)


def piece_number(index):
    return (index & 1) * 4 + (index >> 1)


def block_copies(layout):
    copies = []
    row = 0
    for number, (shard_rows, columns) in enumerate(layout):
        piece_rows = shard_rows // 8
        if columns >= 1024:
            for block in range(columns // 1024):
                copies.append((row, piece_rows, 0, 1024, number, 0, block * 1024))
                row += piece_rows
        else:
            parts = 1024 // columns
            rows = piece_rows // parts
            for part in range(parts):
                copies.append((row, rows, part * columns, columns, number, part * rows, 0))
            row += rows
    return tuple(copies), row


def place_copies(copies, cut):
    def chosen(part):
        if part == 0:
            return copies
        if part == 1:
            return tuple(item for item in copies if item[0] < cut)
        return tuple((item[0] - cut,) + item[1:] for item in copies if item[0] >= cut)

    return chosen


def group_loads(layout, copies, cut, steps, place_ref, sources, stages, sems, base=0):
    count = len(layout)
    chosen = place_copies(copies, cut)
    loads = []
    for number, (shard_rows, _) in enumerate(layout):
        target = stages[number]
        if steps > 1:
            start = pl.multiple_of(place_ref[base] * shard_rows, shard_rows)
            target = target.at[pl.ds(start, shard_rows), :]
        loads.append((number, pltpu.make_async_copy(sources[number], target, sems.at[number])))
    for arrival, (offset, part) in zip(sources[count:], SPREAD_PLAN):
        for step in range(1, steps):
            for row, rows, col, cols, number, prow, wcol in chosen(part):
                shard_rows = layout[number][0]
                start = place_ref[base + step] * shard_rows
                start = start + place_ref[base + steps + offset] * (shard_rows // 8) + prow
                source = arrival.at[step - 1, pl.ds(row, rows), pl.ds(col, cols)]
                target = stages[number].at[pl.ds(pl.multiple_of(start, 16), rows), pl.ds(wcol, cols)]
                loads.append((number, pltpu.make_async_copy(source, target, sems.at[number])))
    return loads


def place_of(z_index, c_index, steps):
    return jnp.stack(
        [(z_index - step) % steps for step in range(steps)] + [piece_number(c_index ^ j) for j in range(8)]
    ).astype(jnp.int32)


def project_kernel(layout, copies, cut, steps, products, pieces, tail, place_ref, *refs):
    count = len(layout)
    number_in = count + len(SPREAD_PLAN)
    own_ref, refs = (refs[0], refs[1:]) if tail else (None, refs)
    parts, sources, refs = refs[:pieces], refs[pieces : pieces + number_in], refs[pieces + number_in :]
    outs, refs = refs[: len(products)], refs[len(products) :]
    rows_out, weights_out, refs = refs[0], refs[1 : 1 + count], refs[1 + count :]
    rows_ref, stages, sems, row_sem, out_sem = refs[0], refs[1 : 1 + count], refs[-3], refs[-2], refs[-1]
    step = pl.program_id(0)
    piece_rows = parts[0].shape[0]

    def stores():
        moves = [pltpu.make_async_copy(rows_ref, rows_out, out_sem.at[count])]
        return moves + [pltpu.make_async_copy(stages[i], weights_out[i], out_sem.at[i]) for i in range(count)]

    @pl.when(step == 0)
    def _():
        loads = [
            pltpu.make_async_copy(part, rows_ref.at[pl.ds(j * piece_rows, piece_rows), :], row_sem)
            for j, part in enumerate(parts)
        ]
        loads += [load for _, load in group_loads(layout, copies, cut, steps, place_ref, sources, stages, sems)]
        for load in loads:
            load.start()
        if tail:
            rows_ref[pieces * piece_rows :, :] = own_ref[piece_rows:, :]
        for load in loads:
            load.wait()
        for move in stores():
            move.start()

    for out, (from_rows, number) in zip(outs, products):
        block = out.shape[1]
        cols = pl.ds(pl.multiple_of(step * block, LANE), block)
        left = rows_ref[...] if from_rows else own_ref[...]
        out[...] = dot_nn(left, stages[number][:, cols]).astype(bf16)

    @pl.when(step == pl.num_programs(0) - 1)
    def _():
        for move in stores():
            move.wait()


def project(own, parts, weights, arrivals, layout, cut, products, place, steps):
    copies, _ = block_copies(layout)
    count = len(layout)
    piece_rows, width = parts[0].shape
    rows = piece_rows * len(parts) + (own.shape[0] - piece_rows if own is not None else 0)
    blocks = 4
    hbm = pl.BlockSpec(memory_space=pl.ANY)
    first = [] if own is None else [own]
    shapes = [(shard_rows * steps, columns) for shard_rows, columns in layout]
    out_shape, out_specs = [], []
    for from_rows, number in products:
        left_rows = rows if from_rows else own.shape[0]
        out_shape.append(shaped((left_rows, shapes[number][1]), bf16))
        out_specs.append(pl.BlockSpec((left_rows, shapes[number][1] // blocks), lambda t: (0, t)))
    out_shape += [shaped((rows, width), bf16)] + [shaped(item, bf16) for item in shapes]
    outs = pl.pallas_call(
        functools.partial(project_kernel, layout, copies, cut, steps, products, len(parts), own is not None),
        grid=(blocks,),
        in_specs=[SMEM_SPEC]
        + [pl.BlockSpec(item.shape, lambda t: (0, 0), pipeline_mode=pl.Buffered(1)) for item in first]
        + [hbm] * (len(parts) + len(weights) + len(arrivals)),
        out_specs=out_specs + [hbm] * (1 + count),
        out_shape=out_shape,
        scratch_shapes=[pltpu.VMEM((rows, width), bf16)]
        + [pltpu.VMEM(item, bf16) for item in shapes]
        + [pltpu.SemaphoreType.DMA((count,)), pltpu.SemaphoreType.DMA, pltpu.SemaphoreType.DMA((count + 1,))],
        compiler_params=params(),
        cost_estimate=SMALL,
        name="project",
    )(place, *first, *parts, *weights, *arrivals)
    return outs[: len(products)], outs[len(products)], outs[len(products) + 1 :]


def query_kernel(norm_count, x_ref, mixed_ref, outer_ref, query_ref, vectors_ref, total_ref, unit_ref, scale_ref, low_ref, out_ref, norms_ref):
    pieces = vectors_ref.shape[0] // 16
    width = x_ref.shape[1]
    part = width // pieces
    copy_row = lax.broadcasted_iota(jnp.int32, (LANE, width), 0)
    copy_col = lax.broadcasted_iota(jnp.int32, (LANE, width), 1)
    copy = jnp.where(copy_row == lax.rem(copy_col, part), 1.0, 0.0).astype(bf16)
    wide = dot_nn(vectors_ref[...], copy)
    piece = lax.broadcasted_iota(jnp.int32, wide.shape, 0) // 16
    column = lax.broadcasted_iota(jnp.int32, wide.shape, 1) // part
    wide = jnp.where(piece == column, wide, 0.0).astype(bf16)
    pick_row = lax.broadcasted_iota(jnp.int32, (16, pieces * 16), 0)
    pick_col = lax.broadcasted_iota(jnp.int32, (16, pieces * 16), 1)
    pick = jnp.where(pick_row == lax.rem(pick_col, 16), 1.0, 0.0).astype(bf16)
    norms_ref[...] = dot_nn(pick, wide)
    unit, scale = norm_parts(x_ref[...].astype(f32) + dot_nn(mixed_ref[...], outer_ref[...]))
    total = unit * norms_ref[0:1, :] + norms_ref[1:2, :]
    unit_ref[...] = unit
    scale_ref[...] = scale
    total_ref[...] = total
    low_ref[...] = total.astype(bf16)
    out_ref[...] = dot_nn(low_ref[...], query_ref[...]).astype(bf16)


def query_rows(x, mixed, outer, query, vectors, norm_count):
    rows, width = x.shape
    full = lambda array: pl.BlockSpec(array.shape, lambda t: (0, 0))
    wide, low = shaped((rows, width), f32), shaped((rows, width), bf16)
    outs = [wide, wide, shaped((rows, 1), f32), low, low, shaped((16, width), f32)]
    return pl.pallas_call(
        functools.partial(query_kernel, norm_count),
        grid=(1,),
        in_specs=[full(x), full(mixed), full(outer), full(query), pl.BlockSpec((vectors.shape[0], LANE), lambda t: (0, 0))],
        out_specs=[full(item) for item in outs],
        out_shape=outs,
        compiler_params=params(),
        cost_estimate=SMALL,
        name="query_rows",
    )(x, mixed, outer, query, vectors)


def pieces_kernel(layouts, plans, place_ref, *refs):
    count = sum(len(layout) for layout in layouts)
    weights, outs, sem = refs[:count], refs[count:-1], refs[-1]
    moves = []
    first = 0
    for layout, copies, out in zip(layouts, plans, outs):
        for row, rows, col, cols, number, prow, wcol in copies:
            start = pl.multiple_of(place_ref[0] * (layout[number][0] // 8) + prow, 16)
            source = weights[first + number].at[pl.ds(start, rows), pl.ds(wcol, cols)]
            moves.append(pltpu.make_async_copy(source, out.at[pl.ds(row, rows), pl.ds(col, cols)], sem))
        first += len(layout)
    for move in moves:
        move.start()
    for move in moves:
        move.wait()


def own_pieces(groups, layouts, c_index):
    plans = [block_copies(layout) for layout in layouts]
    weights = [w for group in groups for w in group]
    return pl.pallas_call(
        functools.partial(pieces_kernel, layouts, [plan[0] for plan in plans]),
        in_specs=[SMEM_SPEC] + [pl.BlockSpec(memory_space=pl.ANY)] * len(weights),
        out_specs=[pl.BlockSpec(memory_space=pltpu.VMEM)] * len(groups),
        out_shape=[shaped((plan[1], 1024), bf16) for plan in plans],
        scratch_shapes=[pltpu.SemaphoreType.DMA],
        compiler_params=params(),
        cost_estimate=SMALL,
        name="own_pieces",
    )(piece_number(c_index).astype(jnp.int32).reshape(1), *weights)


def stack_kernel(count, *refs):
    out, sem = refs[count], refs[count + 1]
    moves = [pltpu.make_async_copy(refs[i], out.at[i], sem) for i in range(count)]
    for move in moves:
        move.start()
    for move in moves:
        move.wait()


def stack_rows(items):
    return pl.pallas_call(
        functools.partial(stack_kernel, len(items)),
        in_specs=[pl.BlockSpec(memory_space=pl.ANY)] * len(items),
        out_specs=pl.BlockSpec(memory_space=pltpu.VMEM),
        out_shape=shaped((len(items),) + items[0].shape, items[0].dtype),
        scratch_shapes=[pltpu.SemaphoreType.DMA],
        compiler_params=params(),
        cost_estimate=SMALL,
        name="stack_rows",
    )(*items)


def z_spread(mine):
    return [z_hop(mine, step) for step in range(1, lax.axis_size("fsdp"))]


def core_columns(ref, which, steps):
    block = ref.shape[1] // (2 * steps)
    parts = [ref[:, pl.ds(pl.multiple_of((2 * step + which) * block, block), block)] for step in range(steps)]
    return jnp.concatenate(parts, axis=1)


def send_kernel(count, steps, core_ref, left_ref, *refs):
    left = core_columns(left_ref, 1 - core_ref[0], steps)
    for right, out in zip(refs[:count], refs[count:]):
        out[...] = dot_tn(left, right[...]).astype(bf16)


def send_grads(left, rights, core, steps):
    vmem = pl.BlockSpec(memory_space=pltpu.VMEM)
    return pl.pallas_call(
        functools.partial(send_kernel, len(rights), steps),
        in_specs=[SMEM_SPEC] + [vmem] * (1 + len(rights)),
        out_specs=[vmem] * len(rights),
        out_shape=[shaped((left.shape[1] // 2, right.shape[1]), bf16) for right in rights],
        compiler_params=params(),
        cost_estimate=SMALL,
        name="send_grads",
    )(core, left, *rights)


def fold_grads_kernel(groups, steps, extra_rows, plain_rows, place_ref, *refs):
    count = len(groups)
    half = steps // 2
    lefts, refs = refs[: max(groups) + 1], refs[max(groups) + 1 :]
    rights, arrivals, refs = refs[:count], refs[count : 2 * count], refs[2 * count :]
    if extra_rows:
        extra_keep, extra_got, refs = refs[0], refs[1], refs[2:]
    if plain_rows:
        plain_keep, plain_got, refs = refs[0], refs[1], refs[2:]
    outs, work = refs[:4], refs[4:]
    step = pl.program_id(0)

    for number, group in enumerate(groups):
        work[number][...] = dot_tn(lefts[group][...], rights[number][...])
    for first_x in (True, False):

        @pl.when((step < half) if first_x else (step >= half))
        def _(first_x=first_x):
            send, keep = outs[:2] if first_x else outs[2:]
            for offset in range(4):
                y_bit, x_bit = offset >> 1, offset & 1
                on, other = (x_bit, y_bit) if first_x else (y_bit, x_bit)
                out = send if on else keep
                yx = place_ref[1] ^ offset
                row = extra_rows
                if extra_rows:
                    total = extra_keep[offset, 0].astype(f32) + extra_got[offset, 0].astype(f32)
                    out[other, 0, :extra_rows, :] = total.astype(bf16)
                for number in range(count):
                    piece, columns = arrivals[number].shape[1:]
                    total = work[number][pl.ds(pl.multiple_of(yx * piece, piece), piece), :]
                    total = (total + arrivals[number][yx].astype(f32)).astype(bf16)
                    if columns >= 1024:
                        for block in range(columns // 1024):
                            out[other, 0, row : row + piece, :] = total[:, block * 1024 : (block + 1) * 1024]
                            row += piece
                    else:
                        parts = 1024 // columns
                        low = piece // parts
                        for part in range(parts):
                            out[other, 0, row : row + low, part * columns : (part + 1) * columns] = total[
                                part * low : (part + 1) * low
                            ]
                        row += low
                if plain_rows:
                    total = plain_keep[yx].astype(f32) + plain_got[yx].astype(f32)
                    out[other, 0, row : row + plain_rows, :] = total.astype(bf16)


def fold_grads(pairs, arrivals, extra, plain, place, steps):
    half = steps // 2
    lefts = [left for left, _ in pairs]
    groups = [number for number, (_, rights) in enumerate(pairs) for _ in rights]
    rights = [right for _, some in pairs for right in some]

    def around(t, p):
        return lax.rem(p[0] + t, steps)

    def resident(array):
        return pl.BlockSpec(array.shape, lambda t, p: (0, 0), pipeline_mode=pl.Buffered(1))

    def by_z(array):
        return pl.BlockSpec((4,) + array.shape[1:], lambda t, p: (around(t, p), 0, 0))

    in_specs = [
        pl.BlockSpec((left.shape[0], left.shape[1] // (2 * steps)), lambda t, p: (0, 2 * around(t, p) + p[2]))
        for left in lefts
    ]
    in_specs += [resident(item) for item in rights] + [by_z(item) for item in arrivals]
    total_rows = sum(item.shape[1] * item.shape[2] // 1024 for item in arrivals)
    extra_rows = plain_rows = 0
    if extra is not None:
        extra_rows = extra[0].shape[2]
        in_specs += [pl.BlockSpec((4, 1, extra_rows, 1024), lambda t, p: (0, t, 0, 0))] * 2
    if plain is not None:
        plain_rows = plain[0].shape[1]
        in_specs += [by_z(item) for item in plain]
    total_rows += extra_rows + plain_rows
    a_spec = pl.BlockSpec((2, 1, total_rows, 1024), lambda t, p: (0, jnp.minimum(t, half - 1), 0, 0))
    b_spec = pl.BlockSpec((2, 1, total_rows, 1024), lambda t, p: (0, jnp.maximum(t - half, 0), 0, 0))
    return pl.pallas_call(
        functools.partial(fold_grads_kernel, groups, steps, extra_rows, plain_rows),
        grid_spec=pltpu.PrefetchScalarGridSpec(
            num_scalar_prefetch=1,
            grid=(steps,),
            in_specs=in_specs,
            out_specs=[a_spec, a_spec, b_spec, b_spec],
            scratch_shapes=[
                pltpu.VMEM((lefts[group].shape[1] // (2 * steps), right.shape[1]), f32)
                for group, right in zip(groups, rights)
            ],
        ),
        out_shape=[shaped((2, half, total_rows, 1024), bf16)] * 4,
        compiler_params=params(),
        cost_estimate=SMALL,
        name="fold_grads",
    )(place, *lefts, *rights, *arrivals, *(extra or ()), *(plain or ()))


def unpack_kernel(layout, copies, cut, place_ref, *refs):
    arrivals = refs[: len(SPREAD_PLAN)]
    outs = refs[len(SPREAD_PLAN) :]
    chosen = place_copies(copies, cut)
    for arrival, (offset, part) in zip(arrivals, SPREAD_PLAN):
        for row, rows, col, cols, number, prow, wcol in chosen(part):
            piece_rows = layout[number][0] // 8
            start = pl.multiple_of(place_ref[offset] * piece_rows + prow, 8)
            outs[number][pl.ds(start, rows), wcol : wcol + cols] = arrival[row : row + rows, col : col + cols].astype(f32)


def add_low(a, b):
    return (a.astype(f32) + b.astype(f32)).astype(bf16)


class Reduction:
    def __init__(self, pairs, sends, layout, cut, extra, plain, z_index, c_index):
        self.pairs = pairs
        self.layout, self.cut, self.c_index = layout, cut, c_index
        self.steps = steps = lax.axis_size("fsdp")
        self.half = steps // 2
        self.copies, self.rows = block_copies(layout)
        arrivals = [
            ctx_hop(s, CORE).reshape(steps * 4, rows // 8, columns) for s, (rows, columns) in zip(sends, layout)
        ]
        self.lead = 0
        if extra is not None:
            keep, send = extra
            self.lead = keep.shape[1] // steps
            split = (4, steps, self.lead, 1024)
            extra = (keep.reshape(split), ctx_hop(send, CORE).reshape(split))
        if plain is not None:
            plain = (plain[0], ctx_hop(plain[1], CORE))
        self.inputs = arrivals, extra, plain
        self.place = jnp.stack([z_index, c_index >> 1, c_index & 1]).astype(jnp.int32)

    def fold(self, *held):
        place = after(self.place, *held) if held else self.place
        self.folded = list(fold_grads(self.pairs, *self.inputs, place, self.steps))

    def first_hops(self, *held):
        self.folded[0], self.folded[2] = after(self.folded[0], *held), after(self.folded[2], *held)
        send_x, _, send_y, _ = self.folded
        self.first = ctx_hop(send_x, XBIT), ctx_hop(send_y, YBIT)

    def second_sums(self, *held):
        _, keep_x, _, keep_y = self.folded
        got_x, got_y = self.first
        if held:
            got_x, got_y, *_ = lax.optimization_barrier((got_x, got_y, *held))
        self.sums = add_low(keep_x[1], got_x[1]), add_low(keep_y[1], got_y[1])

    def second_hops(self):
        self.second = ctx_hop(self.sums[0], YBIT), ctx_hop(self.sums[1], XBIT)

    def z_sums(self, *held):
        _, keep_x, _, keep_y = self.folded
        second = lax.optimization_barrier((*self.second, *held))[:2] if held else self.second
        done = []
        for keep, got, late in ((keep_x, self.first[0], second[0]), (keep_y, self.first[1], second[1])):
            for kk in range(self.half):
                done.append(keep[0, kk].astype(f32) + got[0, kk].astype(f32) + late[kk].astype(f32))
        self.extra = [item[: self.lead] for item in done]
        self.mine = done[0][self.lead :]
        self.sums = [item[self.lead :].astype(bf16) for item in done[1:]]

    def z_hops(self):
        self.third = tuple(z_hop(item, k + 1) for k, item in enumerate(self.sums))

    def spread(self, *held):
        total = self.mine
        for item in (lax.optimization_barrier((*self.third, *held))[: len(self.third)] if held else self.third):
            total = total + item.astype(f32)
        self.arrivals = ctx_spread(total.astype(bf16), 0, self.cut)

    def grads(self):
        place = jnp.stack([piece_number(self.c_index ^ j) for j in range(8)]).astype(jnp.int32)
        vmem = pl.BlockSpec(memory_space=pltpu.VMEM)
        return pl.pallas_call(
            functools.partial(unpack_kernel, self.layout, self.copies, self.cut),
            in_specs=[SMEM_SPEC] + [vmem] * len(self.arrivals),
            out_specs=[vmem] * len(self.layout),
            out_shape=[shaped((rows, columns), f32) for rows, columns in self.layout],
            compiler_params=params(),
            cost_estimate=SMALL,
            name="unpack",
        )(place, *self.arrivals)

    def extra_sum(self):
        return jnp.concatenate(self.extra, axis=0)


def on_device(
    hidden, encoder_out, out_grad, slot_len, enc_len, rel_bucket,
    query_weight, key_weight, value_weight, relative_weight, output_weight, self_norm_gain, self_norm_shift,
    cross_query_weight, cross_key_weight, cross_value_weight, cross_output_weight, cross_norm_gain,
    cross_norm_shift, up_weight, down_weight, feed_norm_gain, feed_norm_shift,
):
    lanes, slots, halves, half_rows, width = hidden.shape
    rows = halves * half_rows
    enc_rows = encoder_out.shape[1]
    ctx_count = lax.axis_size("ctx")
    steps = lax.axis_size("fsdp")
    z_index = lax.axis_index("fsdp")
    c_index = lax.axis_index("ctx")
    seq_len = ctx_count * rows
    all_rows = lanes * slots * rows
    slab = (lanes, slots, rows, width)
    paired = ctx_count == 8 and steps % 2 == 0 and query_weight.shape[0] % 256 == 0 and width == 1024
    paired = paired and enc_rows == rows

    norms = jnp.stack(
        [self_norm_gain, self_norm_shift, cross_norm_gain, cross_norm_shift, feed_norm_gain, feed_norm_shift]
    )
    norm_count, norm_shard = norms.shape

    self_set = (query_weight, relative_weight, key_weight, value_weight)
    cross_set = (output_weight, cross_query_weight, cross_key_weight, cross_value_weight, cross_output_weight)
    feed_set = (up_weight, down_weight)
    layouts = [tuple(w.shape for w in group) for group in (self_set, cross_set, feed_set)]
    x_all = hidden.reshape(all_rows, width)
    x_rows = hidden.reshape(slab)
    if paired:
        cuts = (48, 96, 128)
        vectors = norms.reshape(norm_count, 8, norm_shard // 8).transpose(1, 0, 2)
        vectors = jnp.pad(vectors, ((0, 0), (0, 16 - norm_count), (0, 1024 - norm_shard // 8))).reshape(128, 1024)
        second_set = (*cross_set, vectors)
        second_layout = layouts[1] + (vectors.shape,)
        where = place_of(z_index, c_index, steps)
        main, enc = x_all[: slots * rows], encoder_out.reshape(slots * rows, width)
        main_x, enc_x = ctx_hop(main, XBIT), ctx_hop(enc, XBIT)
        main_y, enc_y = ctx_hop(main, YBIT), ctx_hop(enc, YBIT)
        mine = own_pieces((self_set, second_set, feed_set), (layouts[0], second_layout, layouts[2]), c_index)
        by_offset = lambda near: [item for pair in zip(near, [ctx_hop(n, CORE) for n in near]) for item in pair]
        stack = stack_rows(z_spread(mine[0]))
        main_near = [main, main_x, main_y, ctx_hop(main_y, XBIT)]
        enc_near = [enc, enc_x, enc_y, ctx_hop(enc_x, YBIT)]
        second_hops = z_spread(after(mine[1], stack))
        arrivals = ctx_spread(stack, 1, cuts[0])
        second_stack = stack_rows(second_hops)
        second_first = first_spread(second_stack)
        third_hops = z_spread(after(mine[2], second_stack))
        (q, e, k, v), keyed_flat, first = project(
            x_all, by_offset(main_near), self_set, arrivals, layouts[0], cuts[0],
            ((False, 0), (False, 1), (True, 2), (True, 3)), after(where, second_stack), steps,
        )
        peers = [c_index ^ j for j in range(8)]
    else:
        norms = lax.all_gather(norms, "fsdp", axis=1, tiled=True)
        gather = lambda w: lax.all_gather(w, "fsdp", axis=0, tiled=True)
        first, second, third = [[gather(w) for w in group] for group in (self_set, cross_set, feed_set)]
        peers = [jnp.int32(j) for j in range(ctx_count)]
        main = lax.all_gather(x_rows[0], "ctx", axis=0)
        keyed_flat = jnp.concatenate([main, x_rows[1:]], axis=0).reshape(-1, width)
        enc_flat = lax.all_gather(encoder_out, "ctx", axis=0).reshape(-1, width)
        q, e = matmul(x_all, first[0]).astype(bf16), matmul(x_all, first[1]).astype(bf16)
        k, v = matmul(keyed_flat, first[2]).astype(bf16), matmul(keyed_flat, first[3]).astype(bf16)
        ck, cv = matmul(enc_flat, second[2]).astype(bf16), matmul(enc_flat, second[3]).astype(bf16)
    query_full, relative_full, key_full, value_full = first

    place = jnp.stack(peers).astype(jnp.int32)
    local = jnp.arange(half_rows, dtype=jnp.int32)

    def both_halves(start):
        return jnp.concatenate([start + local, seq_len - 1 - start - local])

    positions = both_halves(c_index * half_rows)
    key_positions = jnp.concatenate([both_halves(place[j] * half_rows) for j in range(ctx_count)])
    enc_positions = (place[:, None] * enc_rows + jnp.arange(enc_rows, dtype=jnp.int32)[None, :]).reshape(1, -1)
    levels = jnp.arange(BUCKETS + 1, dtype=jnp.int32)
    bounds = jnp.sum((rel_bucket[None, :] < levels[:, None]).astype(jnp.int32), axis=1)

    q, e = q.reshape(slab), e.reshape(lanes, slots, rows, -1)
    k, v = k.reshape(-1, slots, rows, width), v.reshape(-1, slots, rows, width)
    o, probs, own = self_forward(slot_len, bounds, positions[:, None], key_positions[None], q, e, k, v)
    o_flat = o.reshape(all_rows, width)
    if paired:
        second_near = corner_spread(second_first, 1, cuts[1], o)
        third_stack = stack_rows(lax.optimization_barrier((*third_hops, *second_near[3:]))[: steps - 1])
        third_first = first_spread(third_stack)
        (ck, cv), enc_flat, second = project(
            None, by_offset(enc_near), second_set, core_spread(second_near), second_layout, cuts[1],
            ((True, 2), (True, 3)), after(where, third_stack), steps,
        )
        output_full, cquery_full, ckey_full, cvalue_full, coutput_full, vectors = second
        normed_one, unit_one, scale_one, normed_one_low, cq, norms = query_rows(
            x_all, o_flat, output_full, cquery_full, vectors, norm_count
        )
    else:
        output_full, cquery_full, ckey_full, cvalue_full, coutput_full = second
        norms = norms.astype(f32)
        resid_one = x_all.astype(f32) + matmul(o_flat, output_full)
        normed_one, unit_one, scale_one = norm_forward(resid_one, norms[0:1], norms[1:2])
        normed_one_low = normed_one.astype(bf16)
        cq = matmul(normed_one_low, cquery_full).astype(bf16)

    enc_shape = (ctx_count, slots, enc_rows, width)
    cq, ck, cv = cq.reshape(slab), ck.reshape(enc_shape), cv.reshape(enc_shape)
    oc, cprobs = cross_forward(enc_len, enc_positions, cq, ck, cv)
    oc_flat = oc.reshape(all_rows, width)

    core = (c_index & 1).astype(jnp.int32).reshape(1)

    def reduction(pairs, sent, index, extra=None, plain=None):
        layout = layouts[index] + (((128, 1024),) if plain is not None else ())
        return Reduction(pairs, sent, layout, cuts[index], extra, plain, z_index, c_index)

    def norm_pieces(grads):
        parts = grads.reshape(norm_count, steps, 2, 4, norm_shard // 8).transpose(2, 1, 3, 0, 4)
        parts = parts.astype(bf16).reshape(2, steps * 4, norm_count, norm_shard // 8)
        parts = jnp.where(core[0] == 0, parts, parts[::-1])
        parts = jnp.pad(parts, ((0, 0), (0, 0), (0, 16 - norm_count), (0, 1024 - norm_shard // 8)))
        return parts[0], parts[1]

    row_valid = (positions[None, None, :] < slot_len[None, :, None]).astype(f32)
    row_valid = jnp.broadcast_to(row_valid, (lanes, slots, rows)).reshape(all_rows, 1)
    if paired:
        third = core_spread(corner_spread(third_first, 1, cuts[2], oc_flat))
        feed_inputs = (feed_set, third, layouts[2], cuts[2], jnp.concatenate([core, where]))
    else:
        feed_inputs = (third, (), tuple(w.shape for w in third), 0, core)
    layer_out, normed_two_low, act_low, back_pre, back_feed, back_two, back_cross, back_oc, feed_norms, *sent = (
        feed_forward_backward(
            normed_one, oc_flat, coutput_full, norms, out_grad.reshape(all_rows, width), row_valid, *feed_inputs, steps, paired
        )
    )
    if paired:
        sent_up, sent_down, sent_coutput = sent
        third_sum = reduction([(normed_two_low, [back_pre]), (act_low, [back_feed])], [sent_up, sent_down], 2)
    back_cq, back_ck, back_cv = cross_backward(cprobs, back_oc.reshape(slab), cq, ck, cv)
    back_cq = back_cq.reshape(all_rows, width)
    back_ck = back_ck.reshape(-1, width)
    back_cv = back_cv.reshape(-1, width)
    if paired:
        third_sum.fold(back_cq)
        third_sum.first_hops()
        back_cq, back_ck = after(back_cq, *third_sum.folded), after(back_ck, *third_sum.folded)
        sent_ckey, sent_cvalue = send_grads(enc_flat, (back_ck, back_cv), core, steps)
    enc_part = pair_rows(back_ck, back_cv, ckey_full, cvalue_full, ctx_count, slots * enc_rows)
    back_one, back_self, back_o, norm_grads, *sent = middle_backward(
        back_cq, cquery_full, back_two, unit_one, scale_one, norms, output_full, normed_one_low, o_flat, core, steps, paired
    )
    norm_grads = jnp.concatenate([norm_grads, feed_norms], axis=0)
    if paired:
        sent_cquery, sent_output = sent
        second_sum = reduction(
            [(o_flat, [back_self]), (normed_one_low, [back_cq]), (enc_flat, [back_ck, back_cv]), (oc_flat, [back_cross])],
            [sent_output, sent_cquery, sent_ckey, sent_cvalue, sent_coutput],
            1,
            enc_part,
            norm_pieces(norm_grads),
        )
        back_o = after(back_o, sent_ckey, *enc_part)
    self_inputs = (bounds, positions[:, None], key_positions[None], probs, own)
    part_one = self_backward(*self_inputs, back_o.reshape(slab), q, k, v, 0, 2)
    if paired:
        second_sum.fold(part_one[0])
        third_sum.second_sums(second_sum.folded[0])
        third_sum.second_hops()
        second_sum.first_hops(*third_sum.sums)
        back_o = after(back_o, second_sum.folded[0], *third_sum.sums)
    back_q, back_k, back_v, back_e = self_backward(*self_inputs, back_o.reshape(slab), q, k, v, 1, 2, part_one)
    back_q = back_q.reshape(all_rows, width)
    back_e = back_e.reshape(all_rows, -1)
    back_k = back_k.reshape(-1, width)
    back_v = back_v.reshape(-1, width)

    if paired:
        sent_keyed = send_grads(keyed_flat, (back_k, back_v), core, steps)
        third_sum.z_sums(sent_keyed[0])
        third_sum.z_hops()
        back_q = after(back_q, *third_sum.sums)
        sent_query, sent_relative = send_grads(x_all, (back_q, back_e), core, steps)
        back_k = after(back_k, *third_sum.sums)
    *main_part, other_part = pair_rows(back_k, back_v, key_full, value_full, ctx_count, slots * rows)
    if paired:
        first_sum = reduction(
            [(x_all, [back_q, back_e]), (keyed_flat, [back_k, back_v])],
            [sent_query, sent_relative, *sent_keyed],
            0,
            main_part,
        )
        first_sum.fold()
        second_sum.second_sums(first_sum.folded[0])
        second_sum.second_hops()
        first_sum.first_hops(*second_sum.sums)
        back_q = after(back_q, *second_sum.sums)
    back_x = own_rows(back_one, back_q, back_e, query_full, relative_full, other_part)

    if paired:
        third_sum.spread(back_x)
        first_sum.second_sums()
        first_sum.second_hops()
        second_sum.z_sums()
        second_sum.z_hops()
        second_sum.spread()
        first_sum.z_sums()
        first_sum.z_hops()
        first_sum.spread()
        third_grads = third_sum.grads()
        *second_grads, norm_sums = second_sum.grads()
        norm_sums = norm_sums.reshape(8, 16, 1024)[:, :norm_count, : norm_shard // 8]
        norm_grads = norm_sums.transpose(1, 0, 2).reshape(norm_count, norm_shard)
        first_grads = first_sum.grads()
        enc_sum = second_sum.extra_sum()
        main_sum = first_sum.extra_sum()
    else:
        norm_grads = lax.psum(norm_grads, ("fsdp", "ctx"))
        norm_grads = lax.dynamic_slice_in_dim(norm_grads, z_index * norm_shard, norm_shard, 1)

        def reduce(left, right):
            shard = lax.psum_scatter(outer_rows(left, right).astype(bf16), "fsdp", scatter_dimension=0, tiled=True)
            return lax.psum(shard, "ctx").astype(f32)

        def scatter(parts):
            whole = jnp.stack(parts, axis=1).reshape(ctx_count, -1, width)
            return lax.psum_scatter(whole, "ctx", scatter_dimension=0, tiled=True).astype(f32).reshape(-1, width)

        first_grads = [
            reduce(x_all, back_q), reduce(x_all, back_e), reduce(keyed_flat, back_k), reduce(keyed_flat, back_v),
        ]
        second_grads = [
            reduce(o_flat, back_self), reduce(normed_one_low, back_cq), reduce(enc_flat, back_ck),
            reduce(enc_flat, back_cv), reduce(oc_flat, back_cross),
        ]
        third_grads = [reduce(normed_two_low, back_pre), reduce(act_low, back_feed)]
        enc_sum = scatter(enc_part)
        main_sum = scatter(main_part)
    encoder_grad = enc_sum.reshape(slots, enc_rows, width)
    own_main = main_sum.shape[0]
    hidden_grad = jnp.concatenate([back_x[:own_main] + main_sum, back_x[own_main:]], axis=0)

    out_shape = hidden.shape
    return (
        layer_out.reshape(out_shape), hidden_grad.reshape(out_shape), encoder_grad,
        first_grads[0], first_grads[2], first_grads[3], first_grads[1], second_grads[0], norm_grads[0], norm_grads[1],
        second_grads[1], second_grads[2], second_grads[3], second_grads[4], norm_grads[2], norm_grads[3],
        third_grads[0], third_grads[1], norm_grads[4], norm_grads[5],
    )


def solution(mesh):
    rows = P("fsdp", None)
    vector = P("fsdp")
    slab = P(None, "fsdp", None, "ctx", None)
    encoder = P("fsdp", "ctx", None)
    weights = (rows,) * 5 + (vector,) * 2 + (rows,) * 4 + (vector,) * 2 + (rows,) * 2 + (vector,) * 2
    return jax.shard_map(
        on_device,
        mesh=mesh,
        in_specs=(slab, encoder, slab, vector, vector, P()) + weights,
        out_specs=(slab, slab, encoder) + weights,
        check_vma=False,
    )
```

time: 913 us -> 624 us (0.68)
  matrix products: 175 us -> 0 us
  local copies, waits for them, and re-layouts: 175 us -> 41 us
  blocking collectives: 92.9 us -> 0 us
  Pallas kernels: 187 us -> 268 us
  waiting for transfers between devices: 151 us -> 186 us
    dot_general x44 -> x0, matrix products: 175 us -> none  [the longest x11 66.1 us: matmul(): return jnp.dot(left_side, right_side, preferred_element_type=f32)]
    pallas_call x10 -> x23, Pallas kernels: 119 us -> 222 us  [the longest x1 42.5 us: feed_forward_backward(): pl.pallas_call(functools.partial(feed_kernel, steps if sending else 0, (l...]
    psum x1 -> x0, blocking collectives: 72.9 us -> none  [on_device(): norm_grads = lax.psum(norm_grads, ('fsdp', 'ctx'))]
    dynamic_slice x16 -> x0, local copies, waits for them, and re-layouts: 59.5 us -> none  [the longest x14 57.7 us: split_cores(): lax.dynamic_index_in_dim(parts, which, 2, keepdims=False)]
    ppermute x18, waiting for transfers between devices: 35.6 us -> 86.2 us  [z_hop(): lax.ppermute(array, 'fsdp', [(i, (i + step) % size) for i in range(size)])]
    unnamed x290 -> x130, local copies, waits for them, and re-layouts: 58.1 us -> 10 us
    pallas_call x1, Pallas kernels: 42.2 us -> 20.3 us  [self_forward(): pl.pallas_call(self_forward_kernel, grid=(slots, groups), in_specs=[SMEM_...]
    all_gather x1 -> x0, blocking collectives: 20 us -> none  [on_device(): norms = lax.all_gather(norms, 'fsdp', axis=1, tiled=True).astype(f32)]
  transfers between devices with their start and end apart: 106 -> 112, of which waited for: 19 -> 28; matrix products, arithmetic and copies ran while one was open for 34% -> 9% of each run, Pallas kernels for 13% -> 36%
where the time goes in v2:
time: 624 us; the launch traced here: 615 us
  Pallas kernels  268 us (43%)
  waiting for transfers between devices  186 us (30%)
  starting transfers between devices  84.1 us (13%)
  local copies, waits for them, and re-layouts  41 us (7%)
  other arithmetic  33.8 us (5%)
    ppermute x94, waiting for transfers between devices, ctx_hop(): return lax.ppermute(array, 'ctx', [(i, i ^ bit) for i in range(size)])  99.8 us
    ppermute x18, waiting for transfers between devices, z_hop(): lax.ppermute(array, 'fsdp', [(i, (i + step) % size) for i in range(size)])  86.2 us
    ppermute x94, starting transfers between devices, ctx_hop(): return lax.ppermute(array, 'ctx', [(i, i ^ bit) for i in range(size)])  51.6 us
    pallas_call x1, Pallas kernels, feed_forward_backward(): pl.pallas_call(functools.partial(feed_kernel, steps if sending else 0, (l...  42.5 us
    pallas_call x3, Pallas kernels, fold_grads(): pl.pallas_call(functools.partial(fold_grads_kernel, groups, steps, extra_...  38.4 us
    ppermute x18, starting transfers between devices, z_hop(): lax.ppermute(array, 'fsdp', [(i, (i + step) % size) for i in range(size)])  32.5 us
    pallas_call x2, Pallas kernels, self_backward(): pl.pallas_call(functools.partial(self_backward_kernel, len(made)), grid=(...  31.5 us
    pallas_call x2, Pallas kernels, project(): pl.pallas_call(functools.partial(project_kernel, layout, copies, cut, ste...  29.4 us
  transfers between devices with their start and end apart: 112, of which 28 were waited for; matrix products, arithmetic and copies ran while one was open for 9% of the time, Pallas kernels for 36%

profile of v2, /device:TPU:0, one launch (start us, length us, event | category | flops | bytes accessed | tf_op | source)
XLA Modules:
  0.0 615.4 jit_solution(10309779668133868184)
XLA Ops:
  19.7 13.6 %collective-permute-done.1.refs_1_ = bf16[112,1024]{1,0:T(8,128)(2,1)S(1)} collective-permute-done((bf16[112,1024]{1,0:T(8,128)(2,1)}, bf16[112,1024]{1,0:T(8,128)(2,1)S(1)}, u32[]{:S(2)}, u32[]{:S(2)}) %collective-permute-start.1) | collective-permute-done | bytes 229408 | tf_op jit(solution)/shard_map/ppermute | solution.py:773
  54.0 19.8 %collective-permute-done.4.refs_1_ = bf16[176,1024]{1,0:T(8,128)(2,1)S(1)} collective-permute-done((bf16[176,1024]{1,0:T(8,128)(2,1)}, bf16[176,1024]{1,0:T(8,128)(2,1)S(1)}, u32[]{:S(2)}, u32[]{:S(2)}) %collective-permute-start.4) | collective-permute-done | bytes 360480 | tf_op jit(solution)/shard_map/ppermute | solution.py:773
  93.3 19.0 %collective-permute-done.26.refs_16_ = bf16[3,176,1024]{2,1,0:T(8,128)(2,1)} collective-permute-done((bf16[3,176,1024]{2,1,0:T(8,128)(2,1)}, bf16[3,176,1024]{2,1,0:T(8,128)(2,1)}, u32[]{:S(2)}, u32[]{:S(2)}) %collective-permute-start.26) | collective-permute-done | bytes 1081376 | tf_op jit(solution)/shard_map/ppermute | solution.py:768
  117.2 14.6 %project.2 = (bf16[384,1024]{1,0:T(8,128)(2,1)}, bf16[384,512]{1,0:T(8,128)(2,1)}, bf16[1280,1024]{1,0:T(8,128)(2,1)}, bf16[1280,1024]{1,0:T(8,128)(2,1)}, bf16[...) custom-call(s32[12]{0:T(128)} %stack.146.place_ref, ...), custom_call_target="tpu_custom_call" | custom-call | flops 1000 | bytes 1000 | tf_op jit(solution)/shard_map/project/pallas_call | solution.py:922
  131.9 20.3 %self_forward.1 = (bf16[3,2,64,1024]{3,2,1,0:T(8,128)(2,1)}, bf16[2,16,192,512]{3,2,1,0:T(8,128)(2,1)}, f32[2,4,192,128]{3,2,1,0:T(8,128)}) custom-call(s32[2]{0:T(128)} %length_ref.2, s32[33]{0:T(128)} %convert_reduce_fusion.bounds_ref, s32[64,1]{1,0:T(8,128)} %copy.58.posq_ref, s32[1,512]{1,0:T(1,128)} %bitcast.232, bf16[3,2,64,1024]{3,2,1,0:T(8,128)(2,1)} %bitcast.196, ...), custom_call_target="tpu_custom_call" | custom-call | flops 1000 | bytes 1000 | tf_op jit(solution)/shard_map/self_forward/pallas_call | solution.py:397
  155.8 14.4 %collective-permute-done.22.refs_0_ = bf16[256,1024]{1,0:T(8,128)(2,1)S(1)} collective-permute-done((bf16[256,1024]{1,0:T(8,128)(2,1)}, bf16[256,1024]{1,0:T(8,128)(2,1)S(1)}, u32[]{:S(2)}, u32[]{:S(2)}) %collective-permute-start.22) | collective-permute-done | bytes 524320 | tf_op jit(solution)/shard_map/ppermute | solution.py:773
  188.3 14.8 %project.3 = (bf16[1024,1024]{1,0:T(8,128)(2,1)}, bf16[1024,1024]{1,0:T(8,128)(2,1)}, bf16[1024,1024]{1,0:T(8,128)(2,1)}, bf16[1024,1024]{1,0:T(8,128)(2,1)}, bf...) custom-call(s32[12]{0:T(128)} %stack.146.place_ref, ...), custom_call_target="tpu_custom_call" | custom-call | flops 1000 | bytes 1000 | tf_op jit(solution)/shard_map/project/pallas_call | solution.py:922
  210.1 11.8 %cross_forward.1 = (bf16[3,2,64,1024]{3,2,1,0:T(8,128)(2,1)}, bf16[2,16,192,512]{3,2,1,0:T(8,128)(2,1)}) custom-call(s32[2]{0:T(128)} %length_ref.3, s32[1,512]{1,0:T(1,128)} %add.335.posk_ref, bf16[3,2,64,1024]{3,2,1,0:T(8,128)(2,1)} %bitcast.211, bf16[8,2,64,1024]{3,2,1,0:T(8,128)(2,1)} %bitcast.192, bf16[8,2,64,1024]{3,2,1,0:T(8,128)(2,1)} %bitcast.194), custom_call_target="tpu_custom_call" | custom-call | flops 1000 | bytes 1000 | tf_op jit(solution)/shard_map/cross_forward/pallas_call | solution.py:475
  226.9 15.9 %collective-permute-done.43.refs_5_ = bf16[3,128,1024]{2,1,0:T(8,128)(2,1)S(1)} collective-permute-done((bf16[3,128,1024]{2,1,0:T(8,128)(2,1)S(1)}, bf16[3,128,1024]{2,1,0:T(8,128)(2,1)S(1)}, u32[]{:S(2)}, u32[]{:S(2)}) %collective-permute-start.43) | collective-permute-done | bytes 786464 | tf_op jit(solution)/shard_map/ppermute | solution.py:768
  248.8 42.5 %feed.1 = (bf16[384,1024]{1,0:T(8,128)(2,1)}, bf16[384,1024]{1,0:T(8,128)(2,1)}, bf16[384,4096]{1,0:T(8,128)(2,1)}, bf16[384,4096]{1,0:T(8,128)(2,1)}, bf16[384,...) custom-call(s32[13]{0:T(128)} %concatenate.28.core_ref, ...), custom_call_target="tpu_custom_call" | custom-call | flops 1000 | bytes 1000 | tf_op jit(solution)/shard_map/feed/pallas_call | solution.py:639
  292.9 13.6 %cross_backward.1 = (bf16[3,2,64,1024]{3,2,1,0:T(8,128)(2,1)}, bf16[8,2,64,1024]{3,2,1,0:T(8,128)(2,1)}, bf16[8,2,64,1024]{3,2,1,0:T(8,128)(2,1)}) custom-call(bf16[2,16,192,512]{3,2,1,0:T(8,128)(2,1)} %get-tuple-element.179.p_ref, bf16[3,2,64,1024]{3,2,1,0:T(8,128)(2,1)} %bitcast.223, bf16[3,2,64,1024]{3,2,1,0:T(8,128)(2,1)} %bitcast.212, ...), custom_call_target="tpu_custom_call" | custom-call | flops 1000 | bytes 1000 | tf_op jit(solution)/shard_map/cross_backward/pallas_call | solution.py:492
  306.5 13.3 %fold_grads.3 = (bf16[2,2,256,1024]{3,2,1,0:T(8,128)(2,1)}, bf16[2,2,256,1024]{3,2,1,0:T(8,128)(2,1)}, bf16[2,2,256,1024]{3,2,1,0:T(8,128)(2,1)}, bf16[2,2,256,1024]{3,2,1,0:T(8,128)(2,1)}) custom-call(s32[3]{0:T(128)} %pad_add_fusion.1.place_ref, bf16[384,1024]{1,0:T(8,128)(2,1)} %get-tuple-element.183.refs_0_, ...), custom_call_target="tpu_custom_call" | custom-call | flops 1000 | bytes 1000 | tf_op jit(solution)/shard_map/fold_grads/pallas_call | solution.py:1144
  319.8 8.3 %middle_backward.1 = (f32[384,1024]{1,0:T(8,128)}, bf16[384,1024]{1,0:T(8,128)(2,1)}, bf16[384,1024]{1,0:T(8,128)(2,1)}, f32[2,1024]{1,0:T(2,128)}, bf16[512,102...) custom-call(s32[1]{0:T(128)} %bitcast.core_ref, bf16[384,1024]{1,0:T(8,128)(2,1)} %bitcast.209, ...), custom_call_target="tpu_custom_call" | custom-call | flops 1000 | bytes 1000 | tf_op jit(solution)/shard_map/middle_backward/pallas_call | solution.py:690
  337.8 8.8 %pair_rows.2 = (bf16[4,128,1024]{2,1,0:T(8,128)(2,1)}, bf16[4,128,1024]{2,1,0:T(8,128)(2,1)}) custom-call(bf16[1024,1024]{1,0:T(8,128)(2,1)} %bitcast.180, bf16[1024,1024]{1,0:T(8,128)(2,1)} %bitcast.183, bf16[1024,1024]{1,0:T(8,128)(2,1)} %get-tuple-element.207.key_ref, bf16[1024,1024]{1,0:T(8,128)(2,1)} %get-tuple-element.208.value_ref), custom_call_target="tpu_custom_call" | custom-call | flops 1000 | bytes 1000 | tf_op jit(solution)/shard_map/pair_rows/pallas_call | solution.py:730
  347.7 15.8 %self_backward.2 = (bf16[3,2,64,1024]{3,2,1,0:T(8,128)(2,1)}, bf16[10,2,64,1024]{3,2,1,0:T(8,128)(2,1)}, bf16[10,2,64,1024]{3,2,1,0:T(8,128)(2,1)}, bf16[3,2,64,512]{3,2,1,0:T(8,128)(2,1)}) custom-call(s32[33]{0:T(128)} %convert_reduce_fusion.bounds_ref, s32[64,1]{1,0:T(8,128)} %copy.58.posq_ref, s32[1,512]{1,0:T(1,128)} %bitcast.233, ...), custom_call_target="tpu_custom_call" | custom-call | flops 1000 | bytes 1000 | tf_op jit(solution)/shard_map/self_backward/pallas_call | solution.py:438
  363.5 13.4 %fold_grads.4 = (bf16[2,2,208,1024]{3,2,1,0:T(8,128)(2,1)}, bf16[2,2,208,1024]{3,2,1,0:T(8,128)(2,1)}, bf16[2,2,208,1024]{3,2,1,0:T(8,128)(2,1)}, bf16[2,2,208,1024]{3,2,1,0:T(8,128)(2,1)}) custom-call(s32[3]{0:T(128)} %pad_add_fusion.1.place_ref, bf16[384,1024]{1,0:T(8,128)(2,1)} %bitcast.201, bf16[384,1024]{1,0:T(8,128)(2,1)} %get-tuple-element.197.refs_0_.refs_1_, ...), custom_call_target="tpu_custom_call" | custom-call | flops 1000 | bytes 1000 | tf_op jit(solution)/shard_map/fold_grads/pallas_call | solution.py:1144
  385.7 15.8 %self_backward.3 = (bf16[3,2,64,1024]{3,2,1,0:T(8,128)(2,1)}, bf16[10,2,64,1024]{3,2,1,0:T(8,128)(2,1)}, bf16[10,2,64,1024]{3,2,1,0:T(8,128)(2,1)}, bf16[3,2,64,512]{3,2,1,0:T(8,128)(2,1)}) custom-call(s32[33]{0:T(128)} %convert_reduce_fusion.bounds_ref, ...), custom_call_target="tpu_custom_call", output_to_operand_aliasing={{0}: (9, {}), {1}: (10, {}), {2}: (11, {}), {3}: (12, {})} | custom-call | flops 1000 | bytes 1000 | tf_op jit(solution)/shard_map/self_backward/pallas_call | solution.py:438
  415.2 10.6 %pair_rows.3 = (bf16[4,128,1024]{2,1,0:T(8,128)(2,1)}, bf16[4,128,1024]{2,1,0:T(8,128)(2,1)}, f32[256,1024]{1,0:T(8,128)}) custom-call(bf16[1280,1024]{1,0:T(8,128)(2,1)} %bitcast.168, bf16[1280,1024]{1,0:T(8,128)(2,1)} %bitcast.171, bf16[1024,1024]{1,0:T(8,128)(2,1)} %get-tuple-element.246.key_ref, bf16[1024,1024]{1,0:T(8,128)(2,1)} %get-tuple-element.247.value_ref), custom_call_target="tpu_custom_call" | custom-call | flops 1000 | bytes 1000 | tf_op jit(solution)/shard_map/pair_rows/pallas_call | solution.py:730
  437.4 11.7 %fold_grads.5 = (bf16[2,2,144,1024]{3,2,1,0:T(8,128)(2,1)}, bf16[2,2,144,1024]{3,2,1,0:T(8,128)(2,1)}, bf16[2,2,144,1024]{3,2,1,0:T(8,128)(2,1)}, bf16[2,2,144,1024]{3,2,1,0:T(8,128)(2,1)}) custom-call(s32[3]{0:T(128)} %pad_add_fusion.1.place_ref, bf16[384,1024]{1,0:T(8,128)(2,1)} %bitcast.188, bf16[1280,1024]{1,0:T(8,128)(2,1)} %get-tuple-element.231.left_ref.refs_1_, ...), custom_call_target="tpu_custom_call" | custom-call | flops 1000 | bytes 1000 | tf_op jit(solution)/shard_map/fold_grads/pallas_call | solution.py:1144
  462.1 20.3 %collective-permute-done.101 = bf16[256,1024]{1,0:T(8,128)(2,1)} collective-permute-done((bf16[256,1024]{1,0:T(8,128)(2,1)}, bf16[256,1024]{1,0:T(8,128)(2,1)}, u32[]{:S(2)}, u32[]{:S(2)}) %collective-permute-start.101) | collective-permute-done | bytes 524320 | tf_op jit(solution)/shard_map/ppermute | solution.py:773
  488.5 9.6 %collective-permute-done.104.refs_2_ = bf16[256,1024]{1,0:T(8,128)(2,1)S(1)} collective-permute-done((bf16[256,1024]{1,0:T(8,128)(2,1)S(1)}, bf16[256,1024]{1,0:T(8,128)(2,1)S(1)}, u32[]{:S(2)}, u32[]{:S(2)}) %collective-permute-start.104) | collective-permute-done | bytes 524320 | tf_op jit(solution)/shard_map/ppermute | solution.py:768
  507.2 12.4 %collective-permute-done.75 = bf16[2,208,1024]{2,1,0:T(8,128)(2,1)S(1)} collective-permute-done((bf16[2,208,1024]{2,1,0:T(8,128)(2,1)S(1)}, bf16[2,208,1024]{2,1,0:T(8,128)(2,1)S(1)}, u32[]{:S(2)}, u32[]{:S(2)}) %collective-permute-start.75) | collective-permute-done | bytes 852000 | tf_op jit(solution)/shard_map/ppermute | solution.py:768
  538.0 14.2 %collective-permute-start.76 = (bf16[112,1024]{1,0:T(8,128)(2,1)S(1)}, bf16[112,1024]{1,0:T(8,128)(2,1)S(1)}, u32[]{:S(2)}, u32[]{:S(2)}) collective-permute-start(bf16[112,1024]{1,0:T(8,128)(2,1)S(1)} %slice.526), channel_id=1, source_target_pairs={{0,1},{1,2},{2,3},{3,0},{4,5},{5,6},{6,7},{7,4},{8,9},{9,10},{10,1... | collective-permute-start | bytes 688136 | tf_op jit(solution)/shard_map/ppermute | solution.py:773
  552.2 8.8 %collective-permute-done.89 = bf16[176,1024]{1,0:T(8,128)(2,1)S(1)} collective-permute-done((bf16[176,1024]{1,0:T(8,128)(2,1)S(1)}, bf16[176,1024]{1,0:T(8,128)(2,1)S(1)}, u32[]{:S(2)}, u32[]{:S(2)}) %collective-permute-start.89) | collective-permute-done | bytes 360480 | tf_op jit(solution)/shard_map/ppermute | solution.py:773
  (450 shorter events, 250.0 us)
Async XLA Ops:
  36.7 37.1 %collective-permute-start.14 = (bf16[3,112,1024]{2,1,0:T(8,128)(2,1)}, bf16[3,112,1024]{2,1,0:T(8,128)(2,1)S(1)}, u32[]{:S(2)}, u32[]{:S(2)}) collective-permute-start(bf16[3,112,1024]{2,1,0:T(8,128)(2,1)} %stack_rows.3.refs_13_), channel_id=1, source_target_pairs={{0,16},{4,20},{8,24},{12,28},{16,0},{20,4},{24,8},{28,12},{1,17},{... | collective-permute-start | bytes 2064392 | tf_op jit(solution)/shard_map/ppermute | solution.py:768
  39.5 35.8 %collective-permute-start.13 = (bf16[3,112,1024]{2,1,0:T(8,128)(2,1)}, bf16[3,112,1024]{2,1,0:T(8,128)(2,1)S(1)}, u32[]{:S(2)}, u32[]{:S(2)}) collective-permute-start(bf16[3,112,1024]{2,1,0:T(8,128)(2,1)} %stack_rows.3.refs_13_), channel_id=1, source_target_pairs={{0,8},{4,12},{8,0},{12,4},{16,24},{20,28},{24,16},{28,20},{1,9},{5... | collective-permute-start | bytes 2064392 | tf_op jit(solution)/shard_map/ppermute | solution.py:768
  50.4 30.7 %collective-permute-start.17 = (bf16[3,112,1024]{2,1,0:T(8,128)(2,1)}, bf16[3,112,1024]{2,1,0:T(8,128)(2,1)}, u32[]{:S(2)}, u32[]{:S(2)}) collective-permute-start(bf16[3,112,1024]{2,1,0:T(8,128)(2,1)} %stack_rows.3.refs_13_), channel_id=1, source_target_pairs={{0,4},{4,0},{8,12},{12,8},{16,20},{20,16},{24,28},{28,24},{1,5},{5... | collective-permute-start | bytes 2064392 | tf_op jit(solution)/shard_map/ppermute | solution.py:768
  79.5 32.8 %collective-permute-start.26 = (bf16[3,176,1024]{2,1,0:T(8,128)(2,1)}, bf16[3,176,1024]{2,1,0:T(8,128)(2,1)}, u32[]{:S(2)}, u32[]{:S(2)}) collective-permute-start(bf16[3,176,1024]{2,1,0:T(8,128)(2,1)} %stack_rows.4.refs_14_), channel_id=1, source_target_pairs={{0,16},{4,20},{8,24},{12,28},{16,0},{20,4},{24,8},{28,12},{1,17},{... | collective-permute-start | bytes 3244040 | tf_op jit(solution)/shard_map/ppermute | solution.py:768
  81.1 50.7 %collective-permute-start.25 = (bf16[3,176,1024]{2,1,0:T(8,128)(2,1)}, bf16[3,176,1024]{2,1,0:T(8,128)(2,1)}, u32[]{:S(2)}, u32[]{:S(2)}) collective-permute-start(bf16[3,176,1024]{2,1,0:T(8,128)(2,1)} %stack_rows.4.refs_14_), channel_id=1, source_target_pairs={{0,8},{4,12},{8,0},{12,4},{16,24},{20,28},{24,16},{28,20},{1,9},{5... | collective-permute-start | bytes 3244040 | tf_op jit(solution)/shard_map/ppermute | solution.py:768
  91.0 64.2 %collective-permute-start.24 = (bf16[256,1024]{1,0:T(8,128)(2,1)}, bf16[256,1024]{1,0:T(8,128)(2,1)}, u32[]{:S(2)}, u32[]{:S(2)}) collective-permute-start(bf16[256,1024]{1,0:T(8,128)(2,1)} %get-tuple-element.159), channel_id=1, source_target_pairs={{0,3},{1,0},{2,1},{3,2},{4,7},{5,4},{6,5},{7,6},{8,11},{9,8},{10,9... | collective-permute-start | bytes 1572872 | tf_op jit(solution)/shard_map/ppermute | solution.py:773
  92.7 60.6 %collective-permute-start.32 = (bf16[128,1024]{1,0:T(8,128)(2,1)}, bf16[128,1024]{1,0:T(8,128)(2,1)}, u32[]{:S(2)}, u32[]{:S(2)}) collective-permute-start(bf16[128,1024]{1,0:T(8,128)(2,1)} %bitcast.227), channel_id=1, source_target_pairs={{0,16},{4,20},{8,24},{12,28},{16,0},{20,4},{24,8},{28,12},{1,17},{... | collective-permute-start | bytes 786440 | tf_op jit(solution)/shard_map/ppermute | solution.py:768
  112.3 41.7 %collective-permute-start.30 = (bf16[128,1024]{1,0:T(8,128)(2,1)}, bf16[128,1024]{1,0:T(8,128)(2,1)}, u32[]{:S(2)}, u32[]{:S(2)}) collective-permute-start(bf16[128,1024]{1,0:T(8,128)(2,1)} %bitcast.228), channel_id=1, source_target_pairs={{0,8},{4,12},{8,0},{12,4},{16,24},{20,28},{24,16},{28,20},{1,9},{5... | collective-permute-start | bytes 786440 | tf_op jit(solution)/shard_map/ppermute | solution.py:768
  115.1 40.7 %collective-permute-start.23 = (bf16[256,1024]{1,0:T(8,128)(2,1)}, bf16[256,1024]{1,0:T(8,128)(2,1)}, u32[]{:S(2)}, u32[]{:S(2)}) collective-permute-start(bf16[256,1024]{1,0:T(8,128)(2,1)} %get-tuple-element.159), channel_id=1, source_target_pairs={{0,2},{1,3},{2,0},{3,1},{4,6},{5,7},{6,4},{7,5},{8,10},{9,11},{10,... | collective-permute-start | bytes 1572872 | tf_op jit(solution)/shard_map/ppermute | solution.py:773
  131.8 50.5 %collective-permute-start.36 = (bf16[3,176,1024]{2,1,0:T(8,128)(2,1)}, bf16[3,176,1024]{2,1,0:T(8,128)(2,1)}, u32[]{:S(2)}, u32[]{:S(2)}) collective-permute-start(bf16[3,176,1024]{2,1,0:T(8,128)(2,1)} %stack_rows.4.refs_14_), channel_id=1, source_target_pairs={{0,4},{4,0},{8,12},{12,8},{16,20},{20,16},{24,28},{28,24},{1,5},{5... | collective-permute-start | bytes 3244040 | tf_op jit(solution)/shard_map/ppermute | solution.py:768
  174.5 47.4 %collective-permute-start.42 = (bf16[3,256,1024]{2,1,0:T(8,128)(2,1)}, bf16[3,256,1024]{2,1,0:T(8,128)(2,1)}, u32[]{:S(2)}, u32[]{:S(2)}) collective-permute-start(bf16[3,256,1024]{2,1,0:T(8,128)(2,1)} %stack_rows.5.refs_2_), channel_id=1, source_target_pairs={{0,16},{4,20},{8,24},{12,28},{16,0},{20,4},{24,8},{28,12},{1,17},{... | collective-permute-start | bytes 4718600 | tf_op jit(solution)/shard_map/ppermute | solution.py:768
  175.8 46.1 %collective-permute-start.41 = (bf16[3,256,1024]{2,1,0:T(8,128)(2,1)}, bf16[3,256,1024]{2,1,0:T(8,128)(2,1)}, u32[]{:S(2)}, u32[]{:S(2)}) collective-permute-start(bf16[3,256,1024]{2,1,0:T(8,128)(2,1)} %stack_rows.5.refs_2_), channel_id=1, source_target_pairs={{0,8},{4,12},{8,0},{12,4},{16,24},{20,28},{24,16},{28,20},{1,9},{5... | collective-permute-start | bytes 4718600 | tf_op jit(solution)/shard_map/ppermute | solution.py:768
  187.1 59.9 %collective-permute-start.45 = (bf16[3,256,1024]{2,1,0:T(8,128)(2,1)}, bf16[3,256,1024]{2,1,0:T(8,128)(2,1)}, u32[]{:S(2)}, u32[]{:S(2)}) collective-permute-start(bf16[3,256,1024]{2,1,0:T(8,128)(2,1)} %stack_rows.5.refs_2_), channel_id=1, source_target_pairs={{0,4},{4,0},{8,12},{12,8},{16,20},{20,16},{24,28},{28,24},{1,5},{5... | collective-permute-start | bytes 4718600 | tf_op jit(solution)/shard_map/ppermute | solution.py:768
  291.9 39.7 %collective-permute-start.56 = (bf16[512,1024]{1,0:T(8,128)(2,1)}, bf16[512,1024]{1,0:T(8,128)(2,1)}, u32[]{:S(2)}, u32[]{:S(2)}) collective-permute-start(bf16[512,1024]{1,0:T(8,128)(2,1)} %get-tuple-element.219), channel_id=1, source_target_pairs={{0,4},{4,0},{8,12},{12,8},{16,20},{20,16},{24,28},{28,24},{1,5},{5... | collective-permute-start | bytes 3145736 | tf_op jit(solution)/shard_map/ppermute | solution.py:768
  328.6 48.3 %collective-permute-start.60 = (bf16[2,2,256,1024]{3,2,1,0:T(8,128)(2,1)}, bf16[2,2,256,1024]{3,2,1,0:T(8,128)(2,1)}, u32[]{:S(2)}, u32[]{:S(2)}) collective-permute-start(bf16[2,2,256,1024]{3,2,1,0:T(8,128)(2,1)} %get-tuple-element.191), channel_id=1, source_target_pairs={{0,16},{4,20},{8,24},{12,28},{16,0},{20,4},{24,8},{28,12},{1,17},{... | collective-permute-start | bytes 6291464 | tf_op jit(solution)/shard_map/ppermute | solution.py:768
  329.1 47.9 %collective-permute-start.59 = (bf16[2,2,256,1024]{3,2,1,0:T(8,128)(2,1)}, bf16[2,2,256,1024]{3,2,1,0:T(8,128)(2,1)}, u32[]{:S(2)}, u32[]{:S(2)}) collective-permute-start(bf16[2,2,256,1024]{3,2,1,0:T(8,128)(2,1)} %get-tuple-element.189), channel_id=1, source_target_pairs={{0,8},{4,12},{8,0},{12,4},{16,24},{20,28},{24,16},{28,20},{1,9},{5... | collective-permute-start | bytes 6291464 | tf_op jit(solution)/shard_map/ppermute | solution.py:768
  408.7 40.4 %collective-permute-start.63 = (bf16[2,2,208,1024]{3,2,1,0:T(8,128)(2,1)}, bf16[2,2,208,1024]{3,2,1,0:T(8,128)(2,1)}, u32[]{:S(2)}, u32[]{:S(2)}) collective-permute-start(bf16[2,2,208,1024]{3,2,1,0:T(8,128)(2,1)} %get-tuple-element.225), channel_id=1, source_target_pairs={{0,8},{4,12},{8,0},{12,4},{16,24},{20,28},{24,16},{28,20},{1,9},{5... | collective-permute-start | bytes 5111816 | tf_op jit(solution)/shard_map/ppermute | solution.py:768
  409.2 39.9 %collective-permute-start.64 = (bf16[2,2,208,1024]{3,2,1,0:T(8,128)(2,1)}, bf16[2,2,208,1024]{3,2,1,0:T(8,128)(2,1)}, u32[]{:S(2)}, u32[]{:S(2)}) collective-permute-start(bf16[2,2,208,1024]{3,2,1,0:T(8,128)(2,1)} %get-tuple-element.240), channel_id=1, source_target_pairs={{0,16},{4,20},{8,24},{12,28},{16,0},{20,4},{24,8},{28,12},{1,17},{... | collective-permute-start | bytes 5111816 | tf_op jit(solution)/shard_map/ppermute | solution.py:768
  437.4 45.0 %collective-permute-start.101 = (bf16[256,1024]{1,0:T(8,128)(2,1)}, bf16[256,1024]{1,0:T(8,128)(2,1)}, u32[]{:S(2)}, u32[]{:S(2)}) collective-permute-start(bf16[256,1024]{1,0:T(8,128)(2,1)} %get-tuple-element.285), channel_id=1, source_target_pairs={{0,2},{1,3},{2,0},{3,1},{4,6},{5,7},{6,4},{7,5},{8,10},{9,11},{10,... | collective-permute-start | bytes 1572872 | tf_op jit(solution)/shard_map/ppermute | solution.py:773
  453.4 49.0 %collective-permute-start.70 = (bf16[2,2,144,1024]{3,2,1,0:T(8,128)(2,1)}, bf16[2,2,144,1024]{3,2,1,0:T(8,128)(2,1)}, u32[]{:S(2)}, u32[]{:S(2)}) collective-permute-start(bf16[2,2,144,1024]{3,2,1,0:T(8,128)(2,1)} %get-tuple-element.259), channel_id=1, source_target_pairs={{0,8},{4,12},{8,0},{12,4},{16,24},{20,28},{24,16},{28,20},{1,9},{5... | collective-permute-start | bytes 3538952 | tf_op jit(solution)/shard_map/ppermute | solution.py:768
  454.9 50.5 %collective-permute-start.72 = (bf16[2,2,144,1024]{3,2,1,0:T(8,128)(2,1)}, bf16[2,2,144,1024]{3,2,1,0:T(8,128)(2,1)}, u32[]{:S(2)}, u32[]{:S(2)}) collective-permute-start(bf16[2,2,144,1024]{3,2,1,0:T(8,128)(2,1)} %get-tuple-element.262), channel_id=1, source_target_pairs={{0,16},{4,20},{8,24},{12,28},{16,0},{20,4},{24,8},{28,12},{1,17},{... | collective-permute-start | bytes 3538952 | tf_op jit(solution)/shard_map/ppermute | solution.py:768
  487.9 31.6 %collective-permute-start.75 = (bf16[2,208,1024]{2,1,0:T(8,128)(2,1)S(1)}, bf16[2,208,1024]{2,1,0:T(8,128)(2,1)S(1)}, u32[]{:S(2)}, u32[]{:S(2)}) collective-permute-start(bf16[2,208,1024]{2,1,0:T(8,128)(2,1)S(1)} %copy-done.18), channel_id=1, source_target_pairs={{0,8},{4,12},{8,0},{12,4},{16,24},{20,28},{24,16},{28,20},{1,9},{5... | collective-permute-start | bytes 2555912 | tf_op jit(solution)/shard_map/ppermute | solution.py:768
  525.5 35.4 %collective-permute-start.89 = (bf16[176,1024]{1,0:T(8,128)(2,1)S(1)}, bf16[176,1024]{1,0:T(8,128)(2,1)S(1)}, u32[]{:S(2)}, u32[]{:S(2)}) collective-permute-start(bf16[176,1024]{1,0:T(8,128)(2,1)S(1)} %slice.522), channel_id=1, source_target_pairs={{0,2},{1,3},{2,0},{3,1},{4,6},{5,7},{6,4},{7,5},{8,10},{9,11},{10,... | collective-permute-start | bytes 1081352 | tf_op jit(solution)/shard_map/ppermute | solution.py:773
  530.1 31.2 %collective-permute-start.88 = (bf16[176,1024]{1,0:T(8,128)(2,1)S(1)}, bf16[176,1024]{1,0:T(8,128)(2,1)S(1)}, u32[]{:S(2)}, u32[]{:S(2)}) collective-permute-start(bf16[176,1024]{1,0:T(8,128)(2,1)S(1)} %slice.523), channel_id=1, source_target_pairs={{0,1},{1,2},{2,3},{3,0},{4,5},{5,6},{6,7},{7,4},{8,9},{9,10},{10,1... | collective-permute-start | bytes 1081352 | tf_op jit(solution)/shard_map/ppermute | solution.py:773
  (151 other events, 2003.4 us)

commit v3 on v2

--- a/solution.py
+++ b/solution.py
@@ -663,7 +663,9 @@
     sending, core_ref, back_cq_ref, query_ref, back_two_ref, unit_ref, scale_ref, norms_ref, outer_ref, *refs
 ):
     if sending:
-        normed_ref, mixed_ref, back_ref, low_ref, back_mixed_ref, grads_ref, query_send_ref, outer_send_ref = refs
+        normed_ref, mixed_ref, feed_norms_ref, enc_ref, back_k_ref, back_v_ref, key_ref, value_ref, *refs = refs
+        back_ref, low_ref, back_mixed_ref, grads_ref, query_send_ref, outer_send_ref, *refs = refs
+        norm_keep_ref, norm_send_ref, key_send_ref, value_send_ref, even_ref, odd_ref, pieces_ref = refs
     else:
         back_ref, low_ref, back_mixed_ref, grads_ref = refs
     total = back_two_ref[...] + dot_nt(back_cq_ref[...], query_ref[...])
@@ -676,22 +678,68 @@
     if sending:
         for left, right, out in ((normed_ref, back_cq_ref, query_send_ref), (mixed_ref, low_ref, outer_send_ref)):
             out[...] = dot_tn(core_columns(left, 1 - core_ref[0], sending), right[...]).astype(bf16)
-
-
-def middle_backward(back_cq, query, back_two, unit, scale, norms, outer, normed, mixed, core, steps, sending):
+        width = back.shape[1]
+        pieces = pieces_ref.shape[0] // 16
+        part = width // pieces
+        vectors = jnp.concatenate(
+            [gain_grad[None], shift_grad[None], feed_norms_ref[...], jnp.zeros((16 - 6, width), f32)], axis=0
+        )
+        pick_row = lax.broadcasted_iota(jnp.int32, (pieces * 16, 16), 0)
+        pick_col = lax.broadcasted_iota(jnp.int32, (pieces * 16, 16), 1)
+        pick = jnp.where(lax.rem(pick_row, 16) == pick_col, 1.0, 0.0).astype(bf16)
+        wide = dot_nn(pick, vectors.astype(bf16))
+        piece = lax.broadcasted_iota(jnp.int32, wide.shape, 0) // 16
+        column = lax.broadcasted_iota(jnp.int32, wide.shape, 1) // part
+        wide = jnp.where(piece == column, wide, 0.0).astype(bf16)
+        copy_row = lax.broadcasted_iota(jnp.int32, (width, LANE), 0)
+        copy_col = lax.broadcasted_iota(jnp.int32, (width, LANE), 1)
+        copy = jnp.where(lax.rem(copy_row, part) == copy_col, 1.0, 0.0).astype(bf16)
+        pieces_ref[...] = dot_nn(wide, copy).astype(bf16)
+        norm_keep_ref[...] = jnp.zeros(norm_keep_ref.shape, bf16)
+        norm_send_ref[...] = jnp.zeros(norm_send_ref.shape, bf16)
+        size = pieces * 16 // (2 * sending)
+        for step in range(sending):
+            for out, which in ((norm_keep_ref, core_ref[0]), (norm_send_ref, 1 - core_ref[0])):
+                start = pl.multiple_of((2 * step + which) * size, size)
+                out[step * size : (step + 1) * size, :LANE] = pieces_ref[pl.ds(start, size), :]
+        columns = core_columns(enc_ref, 1 - core_ref[0], sending)
+        key_send_ref[...] = dot_tn(columns, back_k_ref[...]).astype(bf16)
+        value_send_ref[...] = dot_tn(columns, back_v_ref[...]).astype(bf16)
+        pair_tiles(back_k_ref, back_v_ref, key_ref, value_ref, even_ref, odd_ref)
+
+
+def pair_tiles(back_k_ref, back_v_ref, key_ref, value_ref, even_ref, odd_ref):
+    half = even_ref.shape[1]
+
+    def fill(tile, carry):
+        rows = pl.ds(pl.multiple_of(tile * 2 * half, 2 * half), 2 * half)
+        total = dot_nt(back_k_ref[rows, :], key_ref[...]) + dot_nt(back_v_ref[rows, :], value_ref[...])
+        even_ref[tile] = total[:half].astype(bf16)
+        odd_ref[tile] = total[half:].astype(bf16)
+        return carry
+
+    lax.fori_loop(0, even_ref.shape[0], fill, 0)
+
+
+def middle_backward(
+    back_cq, query, back_two, unit, scale, norms, outer, core, steps, sending=()
+):
     rows, width = back_two.shape
     low = shaped((rows, width), bf16)
     out_shape = [shaped((rows, width), f32), low, low, shaped((2, width), f32)]
     inputs = [back_cq, query, back_two, unit, scale, norms, outer]
     if sending:
-        out_shape += [shaped((width // 2, width), bf16)] * 2
-        inputs += [normed, mixed]
+        half = shaped((width // 2, width), bf16)
+        pair = shaped((4, sending[3].shape[0] // 8, width), bf16)
+        out_shape += [half, half] + [shaped((16 * 4 * steps, width), bf16)] * 2 + [half, half, pair, pair]
+        inputs += sending
     vmem = pl.BlockSpec(memory_space=pltpu.VMEM)
     return pl.pallas_call(
         functools.partial(middle_kernel, steps if sending else 0),
         in_specs=[SMEM_SPEC] + [vmem] * len(inputs),
         out_specs=[vmem] * len(out_shape),
         out_shape=out_shape,
+        scratch_shapes=[pltpu.VMEM((16 * 8 * steps, LANE), bf16)] if sending else [],
         compiler_params=params(),
         cost_estimate=SMALL,
         name="middle_backward",
@@ -739,28 +787,49 @@
     )(back_k, back_v, key, value)
 
 
-def own_rows_kernel(back_ref, back_q_ref, back_e_ref, query_ref, relative_ref, other_ref, out_ref):
+def last_kernel(
+    steps, core_ref, x_ref, keyed_ref, back_ref, back_q_ref, back_e_ref, back_k_ref, back_v_ref,
+    query_ref, relative_ref, key_ref, value_ref,
+    key_send_ref, value_send_ref, query_send_ref, embed_send_ref, even_ref, odd_ref, out_ref,
+):
+    columns = core_columns(keyed_ref, 1 - core_ref[0], steps)
+    key_send_ref[...] = dot_tn(columns, back_k_ref[...]).astype(bf16)
+    value_send_ref[...] = dot_tn(columns, back_v_ref[...]).astype(bf16)
+    columns = core_columns(x_ref, 1 - core_ref[0], steps)
+    query_send_ref[...] = dot_tn(columns, back_q_ref[...]).astype(bf16)
+    embed_send_ref[...] = dot_tn(columns, back_e_ref[...]).astype(bf16)
+    pair_tiles(back_k_ref, back_v_ref, key_ref, value_ref, even_ref, odd_ref)
+    main = even_ref.shape[0] * 2 * even_ref.shape[1]
+    skip = out_ref.shape[0] - (back_k_ref.shape[0] - main)
     total = back_ref[...] + dot_nt(back_q_ref[...], query_ref[...]) + dot_nt(back_e_ref[...], relative_ref[...])
-    skip = total.shape[0] - other_ref.shape[0]
     out_ref[:skip, :] = total[:skip]
-    out_ref[skip:, :] = total[skip:] + other_ref[...]
-
-
-def own_rows(back, back_q, back_e, query, relative, other):
+    lanes = dot_nt(back_k_ref[main:, :], key_ref[...]) + dot_nt(back_v_ref[main:, :], value_ref[...])
+    out_ref[skip:, :] = total[skip:] + lanes
+
+
+def last_backward(x, keyed, back, back_q, back_e, back_k, back_v, query, relative, key, value, core, steps, pieces):
+    width = x.shape[1]
+    half = shaped((width // 2, width), bf16)
+    pair = shaped((pieces // 2, x.shape[0] // 3, width), bf16)
+    out_shape = [half, half, half, shaped((width // 2, back_e.shape[1]), bf16), pair, pair, shaped(back.shape, f32)]
     vmem = pl.BlockSpec(memory_space=pltpu.VMEM)
     return pl.pallas_call(
-        own_rows_kernel,
-        in_specs=[vmem] * 6,
-        out_specs=vmem,
-        out_shape=shaped(back.shape, f32),
+        functools.partial(last_kernel, steps),
+        in_specs=[SMEM_SPEC] + [vmem] * 11,
+        out_specs=[vmem] * len(out_shape),
+        out_shape=out_shape,
         compiler_params=params(),
         cost_estimate=SMALL,
-        name="own_rows",
-    )(back, back_q, back_e, query, relative, other)
+        name="last_backward",
+    )(core, x, keyed, back, back_q, back_e, back_k, back_v, query, relative, key, value)
 
 
 def after(value, *others):
     return lax.optimization_barrier((value,) + others)[0]
+
+
+def tie(*values):
+    return lax.optimization_barrier(values)
 
 
 def ctx_hop(array, bit):
@@ -785,14 +854,6 @@
     corner_one = ctx_hop(lax.slice_in_dim(from_y, 0, cut, axis=axis), XBIT)
     corner_two = ctx_hop(lax.slice_in_dim(from_x, cut, size, axis=axis), YBIT)
     return [array, from_x, from_y, corner_one, corner_two]
-
-
-def core_spread(near):
-    return near + [ctx_hop(item, CORE) for item in near]
-
-
-def ctx_spread(array, axis, cut):
-    return core_spread(corner_spread(first_spread(array), axis, cut))
 
 
 SPREAD_PLAN = tuple(
@@ -1042,25 +1103,6 @@
     return jnp.concatenate(parts, axis=1)
 
 
-def send_kernel(count, steps, core_ref, left_ref, *refs):
-    left = core_columns(left_ref, 1 - core_ref[0], steps)
-    for right, out in zip(refs[:count], refs[count:]):
-        out[...] = dot_tn(left, right[...]).astype(bf16)
-
-
-def send_grads(left, rights, core, steps):
-    vmem = pl.BlockSpec(memory_space=pltpu.VMEM)
-    return pl.pallas_call(
-        functools.partial(send_kernel, len(rights), steps),
-        in_specs=[SMEM_SPEC] + [vmem] * (1 + len(rights)),
-        out_specs=[vmem] * len(rights),
-        out_shape=[shaped((left.shape[1] // 2, right.shape[1]), bf16) for right in rights],
-        compiler_params=params(),
-        cost_estimate=SMALL,
-        name="send_grads",
-    )(core, left, *rights)
-
-
 def fold_grads_kernel(groups, steps, extra_rows, plain_rows, place_ref, *refs):
     count = len(groups)
     half = steps // 2
@@ -1070,7 +1112,7 @@
         extra_keep, extra_got, refs = refs[0], refs[1], refs[2:]
     if plain_rows:
         plain_keep, plain_got, refs = refs[0], refs[1], refs[2:]
-    outs, work = refs[:4], refs[4:]
+    outs, work = refs[:8], refs[8:]
     step = pl.program_id(0)
 
     for number, group in enumerate(groups):
@@ -1079,35 +1121,35 @@
 
         @pl.when((step < half) if first_x else (step >= half))
         def _(first_x=first_x):
-            send, keep = outs[:2] if first_x else outs[2:]
+            some = outs[:4] if first_x else outs[4:]
             for offset in range(4):
                 y_bit, x_bit = offset >> 1, offset & 1
                 on, other = (x_bit, y_bit) if first_x else (y_bit, x_bit)
-                out = send if on else keep
+                out = some[2 * (1 - on) + other]
                 yx = place_ref[1] ^ offset
                 row = extra_rows
                 if extra_rows:
                     total = extra_keep[offset, 0].astype(f32) + extra_got[offset, 0].astype(f32)
-                    out[other, 0, :extra_rows, :] = total.astype(bf16)
+                    out[0, :extra_rows, :] = total.astype(bf16)
                 for number in range(count):
                     piece, columns = arrivals[number].shape[1:]
                     total = work[number][pl.ds(pl.multiple_of(yx * piece, piece), piece), :]
                     total = (total + arrivals[number][yx].astype(f32)).astype(bf16)
                     if columns >= 1024:
                         for block in range(columns // 1024):
-                            out[other, 0, row : row + piece, :] = total[:, block * 1024 : (block + 1) * 1024]
+                            out[0, row : row + piece, :] = total[:, block * 1024 : (block + 1) * 1024]
                             row += piece
                     else:
                         parts = 1024 // columns
                         low = piece // parts
                         for part in range(parts):
-                            out[other, 0, row : row + low, part * columns : (part + 1) * columns] = total[
+                            out[0, row : row + low, part * columns : (part + 1) * columns] = total[
                                 part * low : (part + 1) * low
                             ]
                         row += low
                 if plain_rows:
                     total = plain_keep[yx].astype(f32) + plain_got[yx].astype(f32)
-                    out[other, 0, row : row + plain_rows, :] = total.astype(bf16)
+                    out[0, row : row + plain_rows, :] = total.astype(bf16)
 
 
 def fold_grads(pairs, arrivals, extra, plain, place, steps):
@@ -1139,21 +1181,21 @@
         plain_rows = plain[0].shape[1]
         in_specs += [by_z(item) for item in plain]
     total_rows += extra_rows + plain_rows
-    a_spec = pl.BlockSpec((2, 1, total_rows, 1024), lambda t, p: (0, jnp.minimum(t, half - 1), 0, 0))
-    b_spec = pl.BlockSpec((2, 1, total_rows, 1024), lambda t, p: (0, jnp.maximum(t - half, 0), 0, 0))
+    a_spec = pl.BlockSpec((1, total_rows, 1024), lambda t, p: (jnp.minimum(t, half - 1), 0, 0))
+    b_spec = pl.BlockSpec((1, total_rows, 1024), lambda t, p: (jnp.maximum(t - half, 0), 0, 0))
     return pl.pallas_call(
         functools.partial(fold_grads_kernel, groups, steps, extra_rows, plain_rows),
         grid_spec=pltpu.PrefetchScalarGridSpec(
             num_scalar_prefetch=1,
             grid=(steps,),
             in_specs=in_specs,
-            out_specs=[a_spec, a_spec, b_spec, b_spec],
+            out_specs=[a_spec] * 4 + [b_spec] * 4,
             scratch_shapes=[
                 pltpu.VMEM((lefts[group].shape[1] // (2 * steps), right.shape[1]), f32)
                 for group, right in zip(groups, rights)
             ],
         ),
-        out_shape=[shaped((2, half, total_rows, 1024), bf16)] * 4,
+        out_shape=[shaped((half, total_rows, 1024), bf16)] * 8,
         compiler_params=params(),
         cost_estimate=SMALL,
         name="fold_grads",
@@ -1176,77 +1218,69 @@
 
 
 class Reduction:
-    def __init__(self, pairs, sends, layout, cut, extra, plain, z_index, c_index):
-        self.pairs = pairs
-        self.layout, self.cut, self.c_index = layout, cut, c_index
-        self.steps = steps = lax.axis_size("fsdp")
-        self.half = steps // 2
+    def __init__(self, pairs, layout, cut, z_index, c_index):
+        self.pairs, self.layout, self.cut, self.c_index = pairs, layout, cut, c_index
+        self.steps = lax.axis_size("fsdp")
+        self.half = self.steps // 2
         self.copies, self.rows = block_copies(layout)
-        arrivals = [
-            ctx_hop(s, CORE).reshape(steps * 4, rows // 8, columns) for s, (rows, columns) in zip(sends, layout)
-        ]
+        self.place = jnp.stack([z_index, c_index >> 1, c_index & 1]).astype(jnp.int32)
+
+    def fold(self, arrivals, extra, plain, *held):
+        steps = self.steps
+        arrivals = [a.reshape(steps * 4, rows // 8, columns) for a, (rows, columns) in zip(arrivals, self.layout)]
         self.lead = 0
         if extra is not None:
-            keep, send = extra
-            self.lead = keep.shape[1] // steps
-            split = (4, steps, self.lead, 1024)
-            extra = (keep.reshape(split), ctx_hop(send, CORE).reshape(split))
-        if plain is not None:
-            plain = (plain[0], ctx_hop(plain[1], CORE))
-        self.inputs = arrivals, extra, plain
-        self.place = jnp.stack([z_index, c_index >> 1, c_index & 1]).astype(jnp.int32)
-
-    def fold(self, *held):
-        place = after(self.place, *held) if held else self.place
-        self.folded = list(fold_grads(self.pairs, *self.inputs, place, self.steps))
-
-    def first_hops(self, *held):
-        self.folded[0], self.folded[2] = after(self.folded[0], *held), after(self.folded[2], *held)
-        send_x, _, send_y, _ = self.folded
-        self.first = ctx_hop(send_x, XBIT), ctx_hop(send_y, YBIT)
-
-    def second_sums(self, *held):
-        _, keep_x, _, keep_y = self.folded
-        got_x, got_y = self.first
-        if held:
-            got_x, got_y, *_ = lax.optimization_barrier((got_x, got_y, *held))
-        self.sums = add_low(keep_x[1], got_x[1]), add_low(keep_y[1], got_y[1])
+            self.lead = extra[0].shape[1] // steps
+            extra = [item.reshape(4, steps, self.lead, 1024) for item in extra]
+        place = after(self.place, *held)
+        self.folded = list(fold_grads(self.pairs, arrivals, extra, plain, place, steps))
+
+    def first_hops(self, part):
+        return ctx_hop(self.folded[part], XBIT), ctx_hop(self.folded[4 + part], YBIT)
+
+    def second_sums(self, got_x, got_y):
+        self.sums = add_low(self.folded[3], got_x), add_low(self.folded[7], got_y)
 
     def second_hops(self):
-        self.second = ctx_hop(self.sums[0], YBIT), ctx_hop(self.sums[1], XBIT)
-
-    def z_sums(self, *held):
-        _, keep_x, _, keep_y = self.folded
-        second = lax.optimization_barrier((*self.second, *held))[:2] if held else self.second
+        return ctx_hop(self.sums[0], YBIT), ctx_hop(self.sums[1], XBIT)
+
+    def z_sums(self, got_x, got_y, late_x, late_y):
         done = []
-        for keep, got, late in ((keep_x, self.first[0], second[0]), (keep_y, self.first[1], second[1])):
+        for keep, got, late in ((self.folded[2], got_x, late_x), (self.folded[6], got_y, late_y)):
             for kk in range(self.half):
-                done.append(keep[0, kk].astype(f32) + got[0, kk].astype(f32) + late[kk].astype(f32))
+                done.append(keep[kk].astype(f32) + got[kk].astype(f32) + late[kk].astype(f32))
         self.extra = [item[: self.lead] for item in done]
-        self.mine = done[0][self.lead :]
-        self.sums = [item[self.lead :].astype(bf16) for item in done[1:]]
-
-    def z_hops(self):
-        self.third = tuple(z_hop(item, k + 1) for k, item in enumerate(self.sums))
-
-    def spread(self, *held):
-        total = self.mine
-        for item in (lax.optimization_barrier((*self.third, *held))[: len(self.third)] if held else self.third):
-            total = total + item.astype(f32)
-        self.arrivals = ctx_spread(total.astype(bf16), 0, self.cut)
-
-    def grads(self):
+        self.terms = [item[self.lead :] for item in done]
+        self.total = self.terms[-1].astype(bf16)
+
+    def z_step(self, step, got=None):
+        if got is not None:
+            self.total = (self.terms[self.steps - step].astype(f32) + got.astype(f32)).astype(bf16)
+        return z_hop(self.total, 1)
+
+    def z_end(self, got):
+        self.total = (self.terms[0] + got.astype(f32)).astype(bf16)
+
+    def spread(self):
+        self.near = list(first_spread(self.total))
+        return self.near[1:]
+
+    def corners(self, from_x, from_y):
+        self.near = corner_spread([self.near[0], from_x, from_y], 0, self.cut)
+        return self.near[3:]
+
+    def grads(self, arrivals):
         place = jnp.stack([piece_number(self.c_index ^ j) for j in range(8)]).astype(jnp.int32)
         vmem = pl.BlockSpec(memory_space=pltpu.VMEM)
         return pl.pallas_call(
             functools.partial(unpack_kernel, self.layout, self.copies, self.cut),
-            in_specs=[SMEM_SPEC] + [vmem] * len(self.arrivals),
+            in_specs=[SMEM_SPEC] + [vmem] * len(arrivals),
             out_specs=[vmem] * len(self.layout),
             out_shape=[shaped((rows, columns), f32) for rows, columns in self.layout],
             compiler_params=params(),
             cost_estimate=SMALL,
             name="unpack",
-        )(place, *self.arrivals)
+        )(place, *arrivals)
 
     def extra_sum(self):
         return jnp.concatenate(self.extra, axis=0)
@@ -1284,28 +1318,53 @@
     x_rows = hidden.reshape(slab)
     if paired:
         cuts = (48, 96, 128)
+        where = place_of(z_index, c_index, steps)
+        main, enc = x_all[: slots * rows], encoder_out.reshape(slots * rows, width)
+        (piece,) = own_pieces((self_set,), layouts[:1], c_index)
+        ring = [z_hop(piece, 1)]
+        main_x, enc_x = ctx_hop(main, XBIT), ctx_hop(enc, XBIT)
+        main_y, enc_y = ctx_hop(main, YBIT), ctx_hop(enc, YBIT)
         vectors = norms.reshape(norm_count, 8, norm_shard // 8).transpose(1, 0, 2)
         vectors = jnp.pad(vectors, ((0, 0), (0, 16 - norm_count), (0, 1024 - norm_shard // 8))).reshape(128, 1024)
         second_set = (*cross_set, vectors)
         second_layout = layouts[1] + (vectors.shape,)
-        where = place_of(z_index, c_index, steps)
-        main, enc = x_all[: slots * rows], encoder_out.reshape(slots * rows, width)
-        main_x, enc_x = ctx_hop(main, XBIT), ctx_hop(enc, XBIT)
-        main_y, enc_y = ctx_hop(main, YBIT), ctx_hop(enc, YBIT)
-        mine = own_pieces((self_set, second_set, feed_set), (layouts[0], second_layout, layouts[2]), c_index)
-        by_offset = lambda near: [item for pair in zip(near, [ctx_hop(n, CORE) for n in near]) for item in pair]
-        stack = stack_rows(z_spread(mine[0]))
-        main_near = [main, main_x, main_y, ctx_hop(main_y, XBIT)]
-        enc_near = [enc, enc_x, enc_y, ctx_hop(enc_x, YBIT)]
-        second_hops = z_spread(after(mine[1], stack))
-        arrivals = ctx_spread(stack, 1, cuts[0])
-        second_stack = stack_rows(second_hops)
-        second_first = first_spread(second_stack)
-        third_hops = z_spread(after(mine[2], second_stack))
+        second_piece, feed_piece = own_pieces((second_set, feed_set), (second_layout, layouts[2]), c_index)
+        held, main_x, main_y, enc_x, enc_y = tie(ring[0], main_x, main_y, enc_x, enc_y)
+        ring.append(z_hop(held, 1))
+        main_corner, enc_corner = ctx_hop(main_y, XBIT), ctx_hop(enc_x, YBIT)
+        main_far, enc_far = [ctx_hop(main, CORE)], [ctx_hop(enc, CORE)]
+        held, main_corner, enc_corner, main_far[0], enc_far[0] = tie(
+            ring[1], main_corner, enc_corner, main_far[0], enc_far[0]
+        )
+        ring.append(z_hop(held, 1))
+        main_far += [ctx_hop(main_x, CORE), ctx_hop(main_y, CORE)]
+        enc_far += [ctx_hop(enc_x, CORE), ctx_hop(enc_y, CORE)]
+        last, main_far[1], main_far[2], enc_far[1], enc_far[2] = tie(
+            ring[2], main_far[1], main_far[2], enc_far[1], enc_far[2]
+        )
+        first_stack = stack_rows([*ring[:2], last])
+        main_far.append(ctx_hop(main_corner, CORE))
+        enc_far.append(ctx_hop(enc_corner, CORE))
+        main_parts = [item for pair in zip([main, main_x, main_y, main_corner], main_far) for item in pair]
+        enc_parts = [item for pair in zip([enc, enc_x, enc_y, enc_corner], enc_far) for item in pair]
+
+        ring = [z_hop(after(second_piece, first_stack), 1)]
+        near = list(first_spread(first_stack))
+        held, near[1], near[2], main_parts[7], enc_parts[7] = tie(ring[0], near[1], near[2], main_parts[7], enc_parts[7])
+        ring.append(z_hop(held, 1))
+        near = corner_spread(near, 1, cuts[0])
+        far = [ctx_hop(near[0], CORE), ctx_hop(near[1], CORE)]
+        held, *near[2:], far[0], far[1] = tie(ring[1], *near[2:], far[0], far[1])
+        ring.append(z_hop(held, 1))
+        far += [ctx_hop(item, CORE) for item in near[2:]]
         (q, e, k, v), keyed_flat, first = project(
-            x_all, by_offset(main_near), self_set, arrivals, layouts[0], cuts[0],
-            ((False, 0), (False, 1), (True, 2), (True, 3)), after(where, second_stack), steps,
-        )
+            x_all, main_parts, self_set, near + far, layouts[0], cuts[0],
+            ((False, 0), (False, 1), (True, 2), (True, 3)), where, steps,
+        )
+        second_stack = stack_rows(tie(*ring, q)[: steps - 1])
+        second_near = list(first_spread(second_stack))
+        feed_hops = [z_hop(after(feed_piece, second_stack), step) for step in range(1, steps - 1)]
+        k = after(k, second_stack)
         peers = [c_index ^ j for j in range(8)]
     else:
         norms = lax.all_gather(norms, "fsdp", axis=1, tiled=True)
@@ -1337,11 +1396,20 @@
     o, probs, own = self_forward(slot_len, bounds, positions[:, None], key_positions[None], q, e, k, v)
     o_flat = o.reshape(all_rows, width)
     if paired:
-        second_near = corner_spread(second_first, 1, cuts[1], o)
-        third_stack = stack_rows(lax.optimization_barrier((*third_hops, *second_near[3:]))[: steps - 1])
-        third_first = first_spread(third_stack)
+        second_near[1], second_near[2], feed_hops[0], feed_piece, _ = tie(
+            second_near[1], second_near[2], feed_hops[0], feed_piece, o
+        )
+        feed_hops.append(z_hop(feed_piece, steps - 1))
+        second_near = corner_spread(second_near, 1, cuts[1])
+        second_far = [ctx_hop(second_near[0], CORE)]
+        *feed_hops, second_near[1], second_near[2], second_near[3], second_near[4], second_far[0] = tie(
+            *feed_hops, *second_near[1:], second_far[0]
+        )
+        second_far += [ctx_hop(item, CORE) for item in second_near[1:]]
+        third_stack = stack_rows(tie(*feed_hops, *second_far[2:])[: steps - 1])
+        third_near = list(first_spread(third_stack))
         (ck, cv), enc_flat, second = project(
-            None, by_offset(enc_near), second_set, core_spread(second_near), second_layout, cuts[1],
+            None, enc_parts, second_set, second_near + second_far, second_layout, cuts[1],
             ((True, 2), (True, 3)), after(where, third_stack), steps,
         )
         output_full, cquery_full, ckey_full, cvalue_full, coutput_full, vectors = second
@@ -1363,21 +1431,20 @@
 
     core = (c_index & 1).astype(jnp.int32).reshape(1)
 
-    def reduction(pairs, sent, index, extra=None, plain=None):
-        layout = layouts[index] + (((128, 1024),) if plain is not None else ())
-        return Reduction(pairs, sent, layout, cuts[index], extra, plain, z_index, c_index)
-
-    def norm_pieces(grads):
-        parts = grads.reshape(norm_count, steps, 2, 4, norm_shard // 8).transpose(2, 1, 3, 0, 4)
-        parts = parts.astype(bf16).reshape(2, steps * 4, norm_count, norm_shard // 8)
-        parts = jnp.where(core[0] == 0, parts, parts[::-1])
-        parts = jnp.pad(parts, ((0, 0), (0, 0), (0, 16 - norm_count), (0, 1024 - norm_shard // 8)))
-        return parts[0], parts[1]
+    def reduction(pairs, index, *more):
+        return Reduction(pairs, layouts[index] + more, cuts[index], z_index, c_index)
+
+    far = lambda *items: [ctx_hop(item, CORE) for item in items]
 
     row_valid = (positions[None, None, :] < slot_len[None, :, None]).astype(f32)
     row_valid = jnp.broadcast_to(row_valid, (lanes, slots, rows)).reshape(all_rows, 1)
     if paired:
-        third = core_spread(corner_spread(third_first, 1, cuts[2], oc_flat))
+        third_near[1], third_near[2], _ = tie(third_near[1], third_near[2], oc_flat)
+        third_near = corner_spread(third_near, 1, cuts[2])
+        third_far = [ctx_hop(item, CORE) for item in third_near[:3]]
+        third_near[3], third_near[4], *third_far = tie(third_near[3], third_near[4], *third_far)
+        third_far += [ctx_hop(item, CORE) for item in third_near[3:]]
+        third = third_near + third_far
         feed_inputs = (feed_set, third, layouts[2], cuts[2], jnp.concatenate([core, where]))
     else:
         feed_inputs = (third, (), tuple(w.shape for w in third), 0, core)
@@ -1388,39 +1455,57 @@
     )
     if paired:
         sent_up, sent_down, sent_coutput = sent
-        third_sum = reduction([(normed_two_low, [back_pre]), (act_low, [back_feed])], [sent_up, sent_down], 2)
+        third_sum = reduction([(normed_two_low, [back_pre]), (act_low, [back_feed])], 2)
+        far_feed = far(sent_up, sent_down, sent_coutput)
     back_cq, back_ck, back_cv = cross_backward(cprobs, back_oc.reshape(slab), cq, ck, cv)
     back_cq = back_cq.reshape(all_rows, width)
     back_ck = back_ck.reshape(-1, width)
     back_cv = back_cv.reshape(-1, width)
+    sending = ()
     if paired:
-        third_sum.fold(back_cq)
-        third_sum.first_hops()
-        back_cq, back_ck = after(back_cq, *third_sum.folded), after(back_ck, *third_sum.folded)
-        sent_ckey, sent_cvalue = send_grads(enc_flat, (back_ck, back_cv), core, steps)
-    enc_part = pair_rows(back_ck, back_cv, ckey_full, cvalue_full, ctx_count, slots * enc_rows)
+        *far_feed, back_cq = tie(*far_feed, back_cq)
+        third_sum.fold(far_feed[:2], None, None, back_cq)
+        third_first = third_sum.first_hops(1)
+        back_cq = after(back_cq, third_sum.folded[0])
+        sending = (normed_one_low, o_flat, feed_norms, enc_flat, back_ck, back_cv, ckey_full, cvalue_full)
     back_one, back_self, back_o, norm_grads, *sent = middle_backward(
-        back_cq, cquery_full, back_two, unit_one, scale_one, norms, output_full, normed_one_low, o_flat, core, steps, paired
+        back_cq, cquery_full, back_two, unit_one, scale_one, norms, output_full, core, steps, sending
     )
-    norm_grads = jnp.concatenate([norm_grads, feed_norms], axis=0)
     if paired:
-        sent_cquery, sent_output = sent
         second_sum = reduction(
             [(o_flat, [back_self]), (normed_one_low, [back_cq]), (enc_flat, [back_ck, back_cv]), (oc_flat, [back_cross])],
-            [sent_output, sent_cquery, sent_ckey, sent_cvalue, sent_coutput],
             1,
-            enc_part,
-            norm_pieces(norm_grads),
-        )
-        back_o = after(back_o, sent_ckey, *enc_part)
+            (128, 1024),
+        )
+        got_x, got_y, back_o, *sent = tie(*third_first, back_o, *sent)
+        sent_cquery, sent_output, norm_keep, norm_send, sent_ckey, sent_cvalue, enc_keep, enc_send = sent
+        third_sum.second_sums(got_x, got_y)
+        third_late = third_sum.second_hops()
+        far_some = far(sent_cquery, sent_output, sent_ckey)
+        back_o = after(back_o, *third_sum.sums)
+    else:
+        enc_part = pair_rows(back_ck, back_cv, ckey_full, cvalue_full, ctx_count, slots * enc_rows)
     self_inputs = (bounds, positions[:, None], key_positions[None], probs, own)
     part_one = self_backward(*self_inputs, back_o.reshape(slab), q, k, v, 0, 2)
     if paired:
-        second_sum.fold(part_one[0])
-        third_sum.second_sums(second_sum.folded[0])
-        third_sum.second_hops()
-        second_sum.first_hops(*third_sum.sums)
-        back_o = after(back_o, second_sum.folded[0], *third_sum.sums)
+        late_x, late_y, *far_some, sent_cvalue, norm_send, enc_send, third_sum.folded[0], third_sum.folded[4], _ = tie(
+            *third_late, *far_some, sent_cvalue, norm_send, enc_send, third_sum.folded[0], third_sum.folded[4], part_one[0]
+        )
+        third_got = third_sum.first_hops(0)
+        norm_shape = (4 * steps, 16, width)
+        far_rest = far(sent_cvalue, norm_send.reshape(norm_shape), enc_send)
+        second_sum.fold(
+            [far_some[1], far_some[0], far_some[2], far_rest[0], far_feed[2]],
+            [enc_keep, far_rest[2]],
+            [norm_keep.reshape(norm_shape), far_rest[1]],
+        )
+        *third_got, second_sum.folded[1], second_sum.folded[5] = tie(
+            *third_got, second_sum.folded[1], second_sum.folded[5]
+        )
+        third_sum.z_sums(*third_got, late_x, late_y)
+        hop = third_sum.z_step(1)
+        second_first = second_sum.first_hops(1)
+        back_o = after(back_o, second_sum.folded[1], third_sum.total)
     back_q, back_k, back_v, back_e = self_backward(*self_inputs, back_o.reshape(slab), q, k, v, 1, 2, part_one)
     back_q = back_q.reshape(all_rows, width)
     back_e = back_e.reshape(all_rows, -1)
@@ -1428,46 +1513,82 @@
     back_v = back_v.reshape(-1, width)
 
     if paired:
-        sent_keyed = send_grads(keyed_flat, (back_k, back_v), core, steps)
-        third_sum.z_sums(sent_keyed[0])
-        third_sum.z_hops()
-        back_q = after(back_q, *third_sum.sums)
-        sent_query, sent_relative = send_grads(x_all, (back_q, back_e), core, steps)
-        back_k = after(back_k, *third_sum.sums)
-    *main_part, other_part = pair_rows(back_k, back_v, key_full, value_full, ctx_count, slots * rows)
-    if paired:
-        first_sum = reduction(
-            [(x_all, [back_q, back_e]), (keyed_flat, [back_k, back_v])],
-            [sent_query, sent_relative, *sent_keyed],
-            0,
-            main_part,
-        )
-        first_sum.fold()
-        second_sum.second_sums(first_sum.folded[0])
-        second_sum.second_hops()
-        first_sum.first_hops(*second_sum.sums)
-        back_q = after(back_q, *second_sum.sums)
-    back_x = own_rows(back_one, back_q, back_e, query_full, relative_full, other_part)
-
-    if paired:
-        third_sum.spread(back_x)
-        first_sum.second_sums()
-        first_sum.second_hops()
-        second_sum.z_sums()
-        second_sum.z_hops()
-        second_sum.spread()
-        first_sum.z_sums()
-        first_sum.z_hops()
-        first_sum.spread()
-        third_grads = third_sum.grads()
-        *second_grads, norm_sums = second_sum.grads()
+        first_sum = reduction([(x_all, [back_q, back_e]), (keyed_flat, [back_k, back_v])], 0)
+        hop, got_x, got_y, back_q, back_k = tie(hop, *second_first, back_q, back_k)
+        hop = third_sum.z_step(2, hop)
+        second_sum.second_sums(got_x, got_y)
+        second_late = second_sum.second_hops()
+        back_q = after(back_q, third_sum.total, *second_sum.sums)
+        *sent_first, main_keep, main_send, back_x = last_backward(
+            x_all, keyed_flat, back_one, back_q, back_e, back_k, back_v, query_full, relative_full, key_full, value_full,
+            core, steps, ctx_count,
+        )
+        hop, late_x, late_y, main_send, second_sum.folded[0], second_sum.folded[4], *sent_first = tie(
+            hop, *second_late, main_send, second_sum.folded[0], second_sum.folded[4], *sent_first
+        )
+        far_keys, far_values, far_query, far_main = far(*sent_first[:3], main_send)
+        far_embed, hop, far_keys = tie(*far(sent_first[3]), hop, far_keys)
+        hop = third_sum.z_step(3, hop)
+        second_got = second_sum.first_hops(0)
+        first_sum.fold([far_query, far_embed, far_keys, far_values], [main_keep, far_main], None, third_sum.total)
+        got_x, got_y, hop, first_sum.folded[1], first_sum.folded[5] = tie(
+            *second_got, hop, first_sum.folded[1], first_sum.folded[5]
+        )
+        first_first = first_sum.first_hops(1)
+        third_sum.z_end(hop)
+        second_sum.z_sums(got_x, got_y, late_x, late_y)
+        hop = second_sum.z_step(1)
+        hop, got_x, got_y = tie(hop, *first_first)
+        first_sum.second_sums(got_x, got_y)
+        first_late = first_sum.second_hops()
+        first_sum.folded[0], first_sum.folded[4], hop, _ = tie(
+            first_sum.folded[0], first_sum.folded[4], hop, first_sum.sums[0]
+        )
+        first_got = first_sum.first_hops(0)
+        hop = second_sum.z_step(2, hop)
+        hop, *rest, third_total = tie(hop, *first_got, *first_late, third_sum.total)
+        third_sum.total = third_total
+        first_sum.z_sums(*rest)
+        first_hop = first_sum.z_step(1)
+        hop = second_sum.z_step(3, hop)
+        main_sum = jnp.concatenate(first_sum.extra, axis=0)
+        hidden_grad = jnp.concatenate([back_x[: main_sum.shape[0]] + main_sum, back_x[main_sum.shape[0] :]], axis=0)
+        encoder_grad = jnp.concatenate(second_sum.extra, axis=0)
+        hop, first_hop, third_x, third_y = tie(hop, first_hop, *third_sum.spread())
+        second_sum.z_end(hop)
+        first_hop = first_sum.z_step(2, first_hop)
+        corners = third_sum.corners(third_x, third_y)
+        spread = second_sum.spread()
+        first_hop, second_x, second_y, *third_sum.near[1:], hidden_grad = tie(
+            first_hop, *spread, third_x, third_y, *corners, hidden_grad
+        )
+        first_hop = first_sum.z_step(3, first_hop)
+        corners = second_sum.corners(second_x, second_y)
+        third_far = far(*third_sum.near[1:3])
+        first_hop, *second_sum.near[1:], third_far[0], third_far[1], encoder_grad = tie(
+            first_hop, second_x, second_y, *corners, *third_far, encoder_grad
+        )
+        first_sum.z_end(first_hop)
+        spread = first_sum.spread()
+        more = far(third_sum.near[0], *third_sum.near[3:])
+        *more, held = tie(*more, second_sum.near[0])
+        third_far = [more[0], *third_far, *more[1:]]
+        second_sum.near[0] = held
+        second_far = far(*second_sum.near[:3])
+        third_grads = third_sum.grads(third_sum.near + third_far)
+        first_x, first_y, *second_far, _ = tie(*spread, *second_far, third_grads[0])
+        corners = first_sum.corners(first_x, first_y)
+        second_far += far(*second_sum.near[3:])
+        *second_grads, norm_sums = second_sum.grads(second_sum.near + second_far)
         norm_sums = norm_sums.reshape(8, 16, 1024)[:, :norm_count, : norm_shard // 8]
-        norm_grads = norm_sums.transpose(1, 0, 2).reshape(norm_count, norm_shard)
-        first_grads = first_sum.grads()
-        enc_sum = second_sum.extra_sum()
-        main_sum = first_sum.extra_sum()
+        norm_grads = [item for item in norm_sums.transpose(1, 0, 2).reshape(norm_count, norm_shard)]
+        *first_sum.near[1:], second_grads[0], norm_grads = tie(first_x, first_y, *corners, second_grads[0], norm_grads)
+        first_grads = first_sum.grads(first_sum.near + far(*first_sum.near))
     else:
-        norm_grads = lax.psum(norm_grads, ("fsdp", "ctx"))
+        *main_part, other_part = pair_rows(back_k, back_v, key_full, value_full, ctx_count, slots * rows)
+        back_x = back_one + matmul_back(back_q, query_full) + matmul_back(back_e, relative_full)
+        back_x = jnp.concatenate([back_x[: slots * rows], back_x[slots * rows :] + other_part], axis=0)
+        norm_grads = lax.psum(jnp.concatenate([norm_grads, feed_norms], axis=0), ("fsdp", "ctx"))
         norm_grads = lax.dynamic_slice_in_dim(norm_grads, z_index * norm_shard, norm_shard, 1)
 
         def reduce(left, right):
@@ -1486,15 +1607,12 @@
             reduce(enc_flat, back_cv), reduce(oc_flat, back_cross),
         ]
         third_grads = [reduce(normed_two_low, back_pre), reduce(act_low, back_feed)]
-        enc_sum = scatter(enc_part)
+        encoder_grad = scatter(enc_part)
         main_sum = scatter(main_part)
-    encoder_grad = enc_sum.reshape(slots, enc_rows, width)
-    own_main = main_sum.shape[0]
-    hidden_grad = jnp.concatenate([back_x[:own_main] + main_sum, back_x[own_main:]], axis=0)
-
+        hidden_grad = jnp.concatenate([back_x[: main_sum.shape[0]] + main_sum, back_x[main_sum.shape[0] :]], axis=0)
     out_shape = hidden.shape
     return (
-        layer_out.reshape(out_shape), hidden_grad.reshape(out_shape), encoder_grad,
+        layer_out.reshape(out_shape), hidden_grad.reshape(out_shape), encoder_grad.reshape(encoder_out.shape),
         first_grads[0], first_grads[2], first_grads[3], first_grads[1], second_grads[0], norm_grads[0], norm_grads[1],
         second_grads[1], second_grads[2], second_grads[3], second_grads[4], norm_grads[2], norm_grads[3],
         third_grads[0], third_grads[1], norm_grads[4], norm_grads[5],

time: 624 us -> 596 us (0.955)
  waiting for transfers between devices: 186 us -> 175 us
  Pallas kernels: 268 us -> 260 us
  local copies, waits for them, and re-layouts: 41 us -> 34.3 us
    pallas_call x6 -> x1, Pallas kernels: 41.7 us -> 19.2 us  [last_backward(): pl.pallas_call(functools.partial(last_kernel, steps), in_specs=[SMEM_SPEC...]
    pallas_call x1, Pallas kernels: 8.26 us -> 21.3 us  [middle_backward(): pl.pallas_call(functools.partial(middle_kernel, steps if sending else 0),...]
    ppermute x94 -> x100, starting transfers between devices: 51.6 us -> 59.2 us  [ctx_hop(): return lax.ppermute(array, 'ctx', [(i, i ^ bit) for i in range(size)])]
    ppermute x94 -> x100, waiting for transfers between devices: 99.8 us -> 92.7 us  [ctx_hop(): return lax.ppermute(array, 'ctx', [(i, i ^ bit) for i in range(size)])]
    unnamed x130 -> x174, local copies, waits for them, and re-layouts: 10 us -> 12.8 us
  transfers between devices with their start and end apart: 112 -> 118, of which waited for: 28 -> 48; matrix products, arithmetic and copies ran while one was open for 9% -> 7% of each run, Pallas kernels for 36% -> 33%
where the time goes in v3:
time: 596 us; the launch traced here: 588 us
  Pallas kernels  260 us (44%)
  waiting for transfers between devices  175 us (29%)
  starting transfers between devices  87.3 us (15%)
  local copies, waits for them, and re-layouts  34.3 us (6%)
  other arithmetic  28.9 us (5%)
    ppermute x100, waiting for transfers between devices, ctx_hop(): return lax.ppermute(array, 'ctx', [(i, i ^ bit) for i in range(size)])  92.7 us
    ppermute x18, waiting for transfers between devices, z_hop(): lax.ppermute(array, 'fsdp', [(i, (i + step) % size) for i in range(size)])  82.3 us
    ppermute x100, starting transfers between devices, ctx_hop(): return lax.ppermute(array, 'ctx', [(i, i ^ bit) for i in range(size)])  59.2 us
    pallas_call x1, Pallas kernels, feed_forward_backward(): pl.pallas_call(functools.partial(feed_kernel, steps if sending else 0, (l...  42.5 us
    pallas_call x3, Pallas kernels, fold_grads(): pl.pallas_call(functools.partial(fold_grads_kernel, groups, steps, extra_...  38.5 us
    pallas_call x2, Pallas kernels, self_backward(): pl.pallas_call(functools.partial(self_backward_kernel, len(made)), grid=(...  31.6 us
    pallas_call x2, Pallas kernels, project(): pl.pallas_call(functools.partial(project_kernel, layout, copies, cut, ste...  29.4 us
    ppermute x18, starting transfers between devices, z_hop(): lax.ppermute(array, 'fsdp', [(i, (i + step) % size) for i in range(size)])  28.1 us
  transfers between devices with their start and end apart: 118, of which 48 were waited for; matrix products, arithmetic and copies ran while one was open for 7% of the time, Pallas kernels for 33%

profile of v3, /device:TPU:0, one launch (start us, length us, event | category | flops | bytes accessed | tf_op | source)
XLA Modules:
  0.0 587.9 jit_solution(15863293761940693495)
XLA Ops:
  10.7 6.7 %collective-permute-done.refs_0_ = bf16[112,1024]{1,0:T(8,128)(2,1)S(1)} collective-permute-done((bf16[112,1024]{1,0:T(8,128)(2,1)}, bf16[112,1024]{1,0:T(8,128)(2,1)S(1)}, u32[]{:S(2)}, u32[]{:S(2)}) %collective-permute-start) | collective-permute-done | bytes 229408 | tf_op jit(solution)/shard_map/ppermute | solution.py:842
  22.7 7.1 %collective-permute-done.5.refs_1_ = bf16[112,1024]{1,0:T(8,128)(2,1)S(1)} collective-permute-done((bf16[112,1024]{1,0:T(8,128)(2,1)S(1)}, bf16[112,1024]{1,0:T(8,128)(2,1)S(1)}, u32[]{:S(2)}, u32[]{:S(2)}) %collective-permute-start.5) | collective-permute-done | bytes 229408 | tf_op jit(solution)/shard_map/ppermute | solution.py:842
  48.8 8.8 %collective-permute-done.15.refs_0_ = bf16[176,1024]{1,0:T(8,128)(2,1)S(1)} collective-permute-done((bf16[176,1024]{1,0:T(8,128)(2,1)}, bf16[176,1024]{1,0:T(8,128)(2,1)S(1)}, u32[]{:S(2)}, u32[]{:S(2)}) %collective-permute-start.15) | collective-permute-done | bytes 360480 | tf_op jit(solution)/shard_map/ppermute | solution.py:842
  64.7 7.8 %collective-permute-done.21.refs_16_ = bf16[3,48,1024]{2,1,0:T(8,128)(2,1)S(1)} collective-permute-done((bf16[3,48,1024]{2,1,0:T(8,128)(2,1)S(1)}, bf16[3,48,1024]{2,1,0:T(8,128)(2,1)S(1)}, u32[]{:S(2)}, u32[]{:S(2)}) %collective-permute-start.21) | collective-permute-done | bytes 294944 | tf_op jit(solution)/shard_map/ppermute | solution.py:837
  79.6 14.5 %project.2 = (bf16[384,1024]{1,0:T(8,128)(2,1)}, bf16[384,512]{1,0:T(8,128)(2,1)}, bf16[1280,1024]{1,0:T(8,128)(2,1)}, bf16[1280,1024]{1,0:T(8,128)(2,1)}, bf16[...) custom-call(s32[12]{0:T(128)} %stack.146.place_ref, ...), custom_call_target="tpu_custom_call" | custom-call | flops 1000 | bytes 1000 | tf_op jit(solution)/shard_map/project/pallas_call | solution.py:983
  99.8 20.2 %self_forward.1 = (bf16[3,2,64,1024]{3,2,1,0:T(8,128)(2,1)}, bf16[2,16,192,512]{3,2,1,0:T(8,128)(2,1)}, f32[2,4,192,128]{3,2,1,0:T(8,128)}) custom-call(s32[2]{0:T(128)} %length_ref.2, s32[33]{0:T(128)} %convert_reduce_fusion.bounds_ref, s32[64,1]{1,0:T(8,128)} %copy.56.posq_ref, s32[1,512]{1,0:T(1,128)} %bitcast.207, bf16[3,2,64,1024]{3,2,1,0:T(8,128)(2,1)} %bitcast.171, ...), custom_call_target="tpu_custom_call" | custom-call | flops 1000 | bytes 1000 | tf_op jit(solution)/shard_map/self_forward/pallas_call | solution.py:397
  130.2 20.7 %collective-permute-done.32.refs_1_ = bf16[256,1024]{1,0:T(8,128)(2,1)S(1)} collective-permute-done((bf16[256,1024]{1,0:T(8,128)(2,1)}, bf16[256,1024]{1,0:T(8,128)(2,1)S(1)}, u32[]{:S(2)}, u32[]{:S(2)}) %collective-permute-start.32) | collective-permute-done | bytes 524320 | tf_op jit(solution)/shard_map/ppermute | solution.py:842
  165.1 14.9 %project.3 = (bf16[1024,1024]{1,0:T(8,128)(2,1)}, bf16[1024,1024]{1,0:T(8,128)(2,1)}, bf16[1024,1024]{1,0:T(8,128)(2,1)}, bf16[1024,1024]{1,0:T(8,128)(2,1)}, bf...) custom-call(s32[12]{0:T(128)} %stack.146.place_ref, ...), custom_call_target="tpu_custom_call" | custom-call | flops 1000 | bytes 1000 | tf_op jit(solution)/shard_map/project/pallas_call | solution.py:983
  180.0 7.0 %query_rows.1 = (f32[384,1024]{1,0:T(8,128)}, f32[384,1024]{1,0:T(8,128)}, f32[384,1]{1,0:T(8,128)}, bf16[384,1024]{1,0:T(8,128)(2,1)}, bf16[384,1024]{1,0:T(8,128)(2,1)}, /*index=5*/f32[16,1024]{1,0:T(8,128)}) custom-call(bf16[384,1024]{1,0:T(8,128)(2,1)} %bitcast.155, bf16[384,1024]{1,0:T(8,128)(2,1)} %bitcast.168, ...), custom_call_target="tpu_custom_call" | custom-call | flops 1000 | bytes 1000 | tf_op jit(solution)/shard_map/query_rows/pallas_call | solution.py:1030
  187.0 11.9 %cross_forward.1 = (bf16[3,2,64,1024]{3,2,1,0:T(8,128)(2,1)}, bf16[2,16,192,512]{3,2,1,0:T(8,128)(2,1)}) custom-call(s32[2]{0:T(128)} %length_ref.3, s32[1,512]{1,0:T(1,128)} %add.322.posk_ref, bf16[3,2,64,1024]{3,2,1,0:T(8,128)(2,1)} %bitcast.182, bf16[8,2,64,1024]{3,2,1,0:T(8,128)(2,1)} %bitcast.158, bf16[8,2,64,1024]{3,2,1,0:T(8,128)(2,1)} %bitcast.160), custom_call_target="tpu_custom_call" | custom-call | flops 1000 | bytes 1000 | tf_op jit(solution)/shard_map/cross_forward/pallas_call | solution.py:475
  203.7 17.8 %collective-permute-done.43.refs_5_ = bf16[3,128,1024]{2,1,0:T(8,128)(2,1)S(1)} collective-permute-done((bf16[3,128,1024]{2,1,0:T(8,128)(2,1)S(1)}, bf16[3,128,1024]{2,1,0:T(8,128)(2,1)S(1)}, u32[]{:S(2)}, u32[]{:S(2)}) %collective-permute-start.43) | collective-permute-done | bytes 786464 | tf_op jit(solution)/shard_map/ppermute | solution.py:837
  226.9 42.5 %feed.1 = (bf16[384,1024]{1,0:T(8,128)(2,1)}, bf16[384,1024]{1,0:T(8,128)(2,1)}, bf16[384,4096]{1,0:T(8,128)(2,1)}, bf16[384,4096]{1,0:T(8,128)(2,1)}, bf16[384,...) custom-call(s32[13]{0:T(128)} %concatenate.24.core_ref, ...), custom_call_target="tpu_custom_call" | custom-call | flops 1000 | bytes 1000 | tf_op jit(solution)/shard_map/feed/pallas_call | solution.py:639
  270.7 13.6 %cross_backward.1 = (bf16[3,2,64,1024]{3,2,1,0:T(8,128)(2,1)}, bf16[8,2,64,1024]{3,2,1,0:T(8,128)(2,1)}, bf16[8,2,64,1024]{3,2,1,0:T(8,128)(2,1)}) custom-call(bf16[2,16,192,512]{3,2,1,0:T(8,128)(2,1)} %get-tuple-element.369.p_ref, bf16[3,2,64,1024]{3,2,1,0:T(8,128)(2,1)} %bitcast.198, bf16[3,2,64,1024]{3,2,1,0:T(8,128)(2,1)} %bitcast.183, ...), custom_call_target="tpu_custom_call" | custom-call | flops 1000 | bytes 1000 | tf_op jit(solution)/shard_map/cross_backward/pallas_call | solution.py:492
  284.5 13.3 %fold_grads.3 = (bf16[2,256,1024]{2,1,0:T(8,128)(2,1)}, bf16[2,256,1024]{2,1,0:T(8,128)(2,1)}, bf16[2,256,1024]{2,1,0:T(8,128)(2,1)}, bf16[2,256,1024]{2,1,0:T(8...) custom-call(s32[3]{0:T(128)} %pad_add_fusion.1.place_ref, ...), custom_call_target="tpu_custom_call" | custom-call | flops 1000 | bytes 1000 | tf_op jit(solution)/shard_map/fold_grads/pallas_call | solution.py:1186
  299.2 21.3 %middle_backward.1 = (f32[384,1024]{1,0:T(8,128)}, bf16[384,1024]{1,0:T(8,128)(2,1)}, bf16[384,1024]{1,0:T(8,128)(2,1)}, f32[2,1024]{1,0:T(2,128)}, bf16[512,102...) custom-call(s32[1]{0:T(128)} %bitcast.core_ref, ...), custom_call_target="tpu_custom_call" | custom-call | flops 1000 | bytes 1000 | tf_op jit(solution)/shard_map/middle_backward/pallas_call | solution.py:737
  331.8 15.8 %self_backward.2 = (bf16[3,2,64,1024]{3,2,1,0:T(8,128)(2,1)}, bf16[10,2,64,1024]{3,2,1,0:T(8,128)(2,1)}, bf16[10,2,64,1024]{3,2,1,0:T(8,128)(2,1)}, bf16[3,2,64,512]{3,2,1,0:T(8,128)(2,1)}) custom-call(s32[33]{0:T(128)} %convert_reduce_fusion.bounds_ref, s32[64,1]{1,0:T(8,128)} %copy.56.posq_ref, s32[1,512]{1,0:T(1,128)} %bitcast.208, ...), custom_call_target="tpu_custom_call" | custom-call | flops 1000 | bytes 1000 | tf_op jit(solution)/shard_map/self_backward/pallas_call | solution.py:438
  361.0 13.4 %fold_grads.4 = (bf16[2,208,1024]{2,1,0:T(8,128)(2,1)}, bf16[2,208,1024]{2,1,0:T(8,128)(2,1)}, bf16[2,208,1024]{2,1,0:T(8,128)(2,1)}, bf16[2,208,1024]{2,1,0:T(8...) custom-call(s32[3]{0:T(128)} %pad_add_fusion.1.place_ref, ...), custom_call_target="tpu_custom_call" | custom-call | flops 1000 | bytes 1000 | tf_op jit(solution)/shard_map/fold_grads/pallas_call | solution.py:1186
  385.7 10.8 %collective-permute-start.65 = (bf16[256,1024]{1,0:T(8,128)(2,1)}, bf16[256,1024]{1,0:T(8,128)(2,1)}, u32[]{:S(2)}, u32[]{:S(2)}) collective-permute-start(bf16[256,1024]{1,0:T(8,128)(2,1)} %fusion.9), channel_id=1, source_target_pairs={{0,1},{1,2},{2,3},{3,0},{4,5},{5,6},{6,7},{7,4},{8,9},{9,10},{10,1... | collective-permute-start | bytes 1572872 | tf_op jit(solution)/shard_map/ppermute | solution.py:842
  396.5 15.8 %self_backward.3 = (bf16[3,2,64,1024]{3,2,1,0:T(8,128)(2,1)}, bf16[10,2,64,1024]{3,2,1,0:T(8,128)(2,1)}, bf16[10,2,64,1024]{3,2,1,0:T(8,128)(2,1)}, bf16[3,2,64,512]{3,2,1,0:T(8,128)(2,1)}) custom-call(s32[33]{0:T(128)} %convert_reduce_fusion.bounds_ref, ...), custom_call_target="tpu_custom_call", output_to_operand_aliasing={{0}: (9, {}), {1}: (10, {}), {2}: (11, {}), {3}: (12, {})} | custom-call | flops 1000 | bytes 1000 | tf_op jit(solution)/shard_map/self_backward/pallas_call | solution.py:438
  421.9 19.2 %last_backward.1 = (bf16[512,1024]{1,0:T(8,128)(2,1)}, bf16[512,1024]{1,0:T(8,128)(2,1)}, bf16[512,1024]{1,0:T(8,128)(2,1)}, bf16[512,512]{1,0:T(8,128)(2,1)}, b...) custom-call(s32[1]{0:T(128)} %bitcast.core_ref, bf16[384,1024]{1,0:T(8,128)(2,1)} %bitcast.156, ...), custom_call_target="tpu_custom_call" | custom-call | flops 1000 | bytes 1000 | tf_op jit(solution)/shard_map/last_backward/pallas_call | solution.py:816
  456.8 11.8 %fold_grads.5 = (bf16[2,144,1024]{2,1,0:T(8,128)(2,1)}, bf16[2,144,1024]{2,1,0:T(8,128)(2,1)}, bf16[2,144,1024]{2,1,0:T(8,128)(2,1)}, bf16[2,144,1024]{2,1,0:T(8...) custom-call(s32[3]{0:T(128)} %pad_add_fusion.1.place_ref, ...), custom_call_target="tpu_custom_call" | custom-call | flops 1000 | bytes 1000 | tf_op jit(solution)/shard_map/fold_grads/pallas_call | solution.py:1186
  476.8 6.9 %collective-permute-done.79 = bf16[176,1024]{1,0:T(8,128)(2,1)S(1)} collective-permute-done((bf16[176,1024]{1,0:T(8,128)(2,1)S(1)}, bf16[176,1024]{1,0:T(8,128)(2,1)S(1)}, u32[]{:S(2)}, u32[]{:S(2)}) %collective-permute-start.79) | collective-permute-done | bytes 360480 | tf_op jit(solution)/shard_map/ppermute | solution.py:842
  501.8 8.4 %collective-permute-done.84 = bf16[2,144,1024]{2,1,0:T(8,128)(2,1)S(1)} collective-permute-done((bf16[2,144,1024]{2,1,0:T(8,128)(2,1)S(1)}, bf16[2,144,1024]{2,1,0:T(8,128)(2,1)S(1)}, u32[]{:S(2)}, u32[]{:S(2)}) %collective-permute-start.84) | collective-permute-done | bytes 589856 | tf_op jit(solution)/shard_map/ppermute | solution.py:837
  516.6 7.2 %collective-permute-done.88 = bf16[112,1024]{1,0:T(8,128)(2,1)S(1)} collective-permute-done((bf16[112,1024]{1,0:T(8,128)(2,1)S(1)}, bf16[112,1024]{1,0:T(8,128)(2,1)S(1)}, u32[]{:S(2)}, u32[]{:S(2)}) %collective-permute-start.88) | collective-permute-done | bytes 229408 | tf_op jit(solution)/shard_map/ppermute | solution.py:842
  (495 shorter events, 248.2 us)
Async XLA Ops:
  96.3 26.3 %collective-permute-start.30 = (bf16[3,176,1024]{2,1,0:T(8,128)(2,1)}, bf16[3,176,1024]{2,1,0:T(8,128)(2,1)}, u32[]{:S(2)}, u32[]{:S(2)}) collective-permute-start(bf16[3,176,1024]{2,1,0:T(8,128)(2,1)} %stack_rows.4.refs_14_), channel_id=1, source_target_pairs={{0,16},{4,20},{8,24},{12,28},{16,0},{20,4},{24,8},{28,12},{1,17},{... | collective-permute-start | bytes 3244040 | tf_op jit(solution)/shard_map/ppermute | solution.py:837
  96.9 25.9 %collective-permute-start.29 = (bf16[3,176,1024]{2,1,0:T(8,128)(2,1)}, bf16[3,176,1024]{2,1,0:T(8,128)(2,1)}, u32[]{:S(2)}, u32[]{:S(2)}) collective-permute-start(bf16[3,176,1024]{2,1,0:T(8,128)(2,1)} %stack_rows.4.refs_14_), channel_id=1, source_target_pairs={{0,8},{4,12},{8,0},{12,4},{16,24},{20,28},{24,16},{28,20},{1,9},{5... | collective-permute-start | bytes 3244040 | tf_op jit(solution)/shard_map/ppermute | solution.py:837
  97.5 53.4 %collective-permute-start.36 = (bf16[3,176,1024]{2,1,0:T(8,128)(2,1)}, bf16[3,176,1024]{2,1,0:T(8,128)(2,1)}, u32[]{:S(2)}, u32[]{:S(2)}) collective-permute-start(bf16[3,176,1024]{2,1,0:T(8,128)(2,1)} %stack_rows.4.refs_14_), channel_id=1, source_target_pairs={{0,4},{4,0},{8,12},{12,8},{16,20},{20,16},{24,28},{28,24},{1,5},{5... | collective-permute-start | bytes 3244040 | tf_op jit(solution)/shard_map/ppermute | solution.py:837
  123.9 27.3 %collective-permute-start.34 = (bf16[3,96,1024]{2,1,0:T(8,128)(2,1)S(1)}, bf16[3,96,1024]{2,1,0:T(8,128)(2,1)S(1)}, u32[]{:S(2)}, u32[]{:S(2)}) collective-permute-start(bf16[3,96,1024]{2,1,0:T(8,128)(2,1)S(1)} %slice.263), channel_id=1, source_target_pairs={{0,8},{4,12},{8,0},{12,4},{16,24},{20,28},{24,16},{28,20},{1,9},{5... | collective-permute-start | bytes 1769480 | tf_op jit(solution)/shard_map/ppermute | solution.py:837
  124.5 26.3 %collective-permute-start.32 = (bf16[256,1024]{1,0:T(8,128)(2,1)}, bf16[256,1024]{1,0:T(8,128)(2,1)S(1)}, u32[]{:S(2)}, u32[]{:S(2)}) collective-permute-start(bf16[256,1024]{1,0:T(8,128)(2,1)} %get-tuple-element.329), channel_id=1, source_target_pairs={{0,2},{1,3},{2,0},{3,1},{4,6},{5,7},{6,4},{7,5},{8,10},{9,11},{10,... | collective-permute-start | bytes 1572872 | tf_op jit(solution)/shard_map/ppermute | solution.py:842
  126.8 24.5 %collective-permute-start.33 = (bf16[256,1024]{1,0:T(8,128)(2,1)}, bf16[256,1024]{1,0:T(8,128)(2,1)S(1)}, u32[]{:S(2)}, u32[]{:S(2)}) collective-permute-start(bf16[256,1024]{1,0:T(8,128)(2,1)} %get-tuple-element.329), channel_id=1, source_target_pairs={{0,3},{1,0},{2,1},{3,2},{4,7},{5,4},{6,5},{7,6},{8,11},{9,8},{10,9... | collective-permute-start | bytes 1572872 | tf_op jit(solution)/shard_map/ppermute | solution.py:842
  159.8 39.1 %collective-permute-start.42 = (bf16[3,256,1024]{2,1,0:T(8,128)(2,1)}, bf16[3,256,1024]{2,1,0:T(8,128)(2,1)}, u32[]{:S(2)}, u32[]{:S(2)}) collective-permute-start(bf16[3,256,1024]{2,1,0:T(8,128)(2,1)} %stack_rows.5.refs_2_), channel_id=1, source_target_pairs={{0,16},{4,20},{8,24},{12,28},{16,0},{20,4},{24,8},{28,12},{1,17},{... | collective-permute-start | bytes 4718600 | tf_op jit(solution)/shard_map/ppermute | solution.py:837
  161.4 37.5 %collective-permute-start.41 = (bf16[3,256,1024]{2,1,0:T(8,128)(2,1)}, bf16[3,256,1024]{2,1,0:T(8,128)(2,1)}, u32[]{:S(2)}, u32[]{:S(2)}) collective-permute-start(bf16[3,256,1024]{2,1,0:T(8,128)(2,1)} %stack_rows.5.refs_2_), channel_id=1, source_target_pairs={{0,8},{4,12},{8,0},{12,4},{16,24},{20,28},{24,16},{28,20},{1,9},{5... | collective-permute-start | bytes 4718600 | tf_op jit(solution)/shard_map/ppermute | solution.py:837
  162.9 40.8 %collective-permute-start.45 = (bf16[3,256,1024]{2,1,0:T(8,128)(2,1)}, bf16[3,256,1024]{2,1,0:T(8,128)(2,1)}, u32[]{:S(2)}, u32[]{:S(2)}) collective-permute-start(bf16[3,256,1024]{2,1,0:T(8,128)(2,1)} %stack_rows.5.refs_2_), channel_id=1, source_target_pairs={{0,4},{4,0},{8,12},{12,8},{16,20},{20,16},{24,28},{28,24},{1,5},{5... | collective-permute-start | bytes 4718600 | tf_op jit(solution)/shard_map/ppermute | solution.py:837
  198.9 23.6 %collective-permute-start.46 = (bf16[3,256,1024]{2,1,0:T(8,128)(2,1)}, bf16[3,256,1024]{2,1,0:T(8,128)(2,1)}, u32[]{:S(2)}, u32[]{:S(2)}) collective-permute-start(bf16[3,256,1024]{2,1,0:T(8,128)(2,1)} %collective-permute-done.41.refs_3_), channel_id=1, source_target_pairs={{0,4},{4,0},{8,12},{12,8},{16,20},{20,16},{24,28},{28,24},{1,5},{5... | collective-permute-start | bytes 4718600 | tf_op jit(solution)/shard_map/ppermute | solution.py:837
  199.1 23.4 %collective-permute-start.47 = (bf16[3,256,1024]{2,1,0:T(8,128)(2,1)}, bf16[3,256,1024]{2,1,0:T(8,128)(2,1)}, u32[]{:S(2)}, u32[]{:S(2)}) collective-permute-start(bf16[3,256,1024]{2,1,0:T(8,128)(2,1)} %collective-permute-done.42.refs_4_), channel_id=1, source_target_pairs={{0,4},{4,0},{8,12},{12,8},{16,20},{20,16},{24,28},{28,24},{1,5},{5... | collective-permute-start | bytes 4718600 | tf_op jit(solution)/shard_map/ppermute | solution.py:837
  297.8 25.7 %collective-permute-start.53 = (bf16[2,256,1024]{2,1,0:T(8,128)(2,1)}, bf16[2,256,1024]{2,1,0:T(8,128)(2,1)}, u32[]{:S(2)}, u32[]{:S(2)}) collective-permute-start(bf16[2,256,1024]{2,1,0:T(8,128)(2,1)} %get-tuple-element.382), channel_id=1, source_target_pairs={{0,8},{4,12},{8,0},{12,4},{16,24},{20,28},{24,16},{28,20},{1,9},{5... | collective-permute-start | bytes 3145736 | tf_op jit(solution)/shard_map/ppermute | solution.py:837
  298.6 25.3 %collective-permute-start.54 = (bf16[2,256,1024]{2,1,0:T(8,128)(2,1)}, bf16[2,256,1024]{2,1,0:T(8,128)(2,1)}, u32[]{:S(2)}, u32[]{:S(2)}) collective-permute-start(bf16[2,256,1024]{2,1,0:T(8,128)(2,1)} %get-tuple-element.383), channel_id=1, source_target_pairs={{0,16},{4,20},{8,24},{12,28},{16,0},{20,4},{24,8},{28,12},{1,17},{... | collective-permute-start | bytes 3145736 | tf_op jit(solution)/shard_map/ppermute | solution.py:837
  326.9 24.5 %collective-permute-start.56 = (bf16[2,256,1024]{2,1,0:T(8,128)(2,1)}, bf16[2,256,1024]{2,1,0:T(8,128)(2,1)}, u32[]{:S(2)}, u32[]{:S(2)}) collective-permute-start(bf16[2,256,1024]{2,1,0:T(8,128)(2,1)} %add_convert_fusion), channel_id=1, source_target_pairs={{0,8},{4,12},{8,0},{12,4},{16,24},{20,28},{24,16},{28,20},{1,9},{5... | collective-permute-start | bytes 3145736 | tf_op jit(solution)/shard_map/ppermute | solution.py:837
  330.8 24.2 %collective-permute-start.55 = (bf16[2,256,1024]{2,1,0:T(8,128)(2,1)}, bf16[2,256,1024]{2,1,0:T(8,128)(2,1)}, u32[]{:S(2)}, u32[]{:S(2)}) collective-permute-start(bf16[2,256,1024]{2,1,0:T(8,128)(2,1)} %add_convert_fusion.1), channel_id=1, source_target_pairs={{0,16},{4,20},{8,24},{12,28},{16,0},{20,4},{24,8},{28,12},{1,17},{... | collective-permute-start | bytes 3145736 | tf_op jit(solution)/shard_map/ppermute | solution.py:837
  331.3 23.7 %collective-permute-start.57 = (bf16[512,1024]{1,0:T(8,128)(2,1)}, bf16[512,1024]{1,0:T(8,128)(2,1)}, u32[]{:S(2)}, u32[]{:S(2)}) collective-permute-start(bf16[512,1024]{1,0:T(8,128)(2,1)} %get-tuple-element.408), channel_id=1, source_target_pairs={{0,4},{4,0},{8,12},{12,8},{16,20},{20,16},{24,28},{28,24},{1,5},{5... | collective-permute-start | bytes 3145736 | tf_op jit(solution)/shard_map/ppermute | solution.py:837
  331.3 23.7 %collective-permute-start.58 = (bf16[512,1024]{1,0:T(8,128)(2,1)}, bf16[512,1024]{1,0:T(8,128)(2,1)}, u32[]{:S(2)}, u32[]{:S(2)}) collective-permute-start(bf16[512,1024]{1,0:T(8,128)(2,1)} %get-tuple-element.409), channel_id=1, source_target_pairs={{0,4},{4,0},{8,12},{12,8},{16,20},{20,16},{24,28},{28,24},{1,5},{5... | collective-permute-start | bytes 3145736 | tf_op jit(solution)/shard_map/ppermute | solution.py:837
  355.6 25.5 %collective-permute-start.60 = (bf16[2,256,1024]{2,1,0:T(8,128)(2,1)}, bf16[2,256,1024]{2,1,0:T(8,128)(2,1)}, u32[]{:S(2)}, u32[]{:S(2)}) collective-permute-start(bf16[2,256,1024]{2,1,0:T(8,128)(2,1)} %get-tuple-element.420), channel_id=1, source_target_pairs={{0,8},{4,12},{8,0},{12,4},{16,24},{20,28},{24,16},{28,20},{1,9},{5... | collective-permute-start | bytes 3145736 | tf_op jit(solution)/shard_map/ppermute | solution.py:837
  356.3 25.2 %collective-permute-start.61 = (bf16[2,256,1024]{2,1,0:T(8,128)(2,1)}, bf16[2,256,1024]{2,1,0:T(8,128)(2,1)}, u32[]{:S(2)}, u32[]{:S(2)}) collective-permute-start(bf16[2,256,1024]{2,1,0:T(8,128)(2,1)} %get-tuple-element.421), channel_id=1, source_target_pairs={{0,16},{4,20},{8,24},{12,28},{16,0},{20,4},{24,8},{28,12},{1,17},{... | collective-permute-start | bytes 3145736 | tf_op jit(solution)/shard_map/ppermute | solution.py:837
  381.5 30.8 %collective-permute-start.67 = (bf16[2,208,1024]{2,1,0:T(8,128)(2,1)}, bf16[2,208,1024]{2,1,0:T(8,128)(2,1)}, u32[]{:S(2)}, u32[]{:S(2)}) collective-permute-start(bf16[2,208,1024]{2,1,0:T(8,128)(2,1)} %get-tuple-element.441), channel_id=1, source_target_pairs={{0,16},{4,20},{8,24},{12,28},{16,0},{20,4},{24,8},{28,12},{1,17},{... | collective-permute-start | bytes 2555912 | tf_op jit(solution)/shard_map/ppermute | solution.py:837
  382.1 30.3 %collective-permute-start.66 = (bf16[2,208,1024]{2,1,0:T(8,128)(2,1)}, bf16[2,208,1024]{2,1,0:T(8,128)(2,1)}, u32[]{:S(2)}, u32[]{:S(2)}) collective-permute-start(bf16[2,208,1024]{2,1,0:T(8,128)(2,1)} %get-tuple-element.440), channel_id=1, source_target_pairs={{0,8},{4,12},{8,0},{12,4},{16,24},{20,28},{24,16},{28,20},{1,9},{5... | collective-permute-start | bytes 2555912 | tf_op jit(solution)/shard_map/ppermute | solution.py:837
  385.7 26.6 %collective-permute-start.65 = (bf16[256,1024]{1,0:T(8,128)(2,1)}, bf16[256,1024]{1,0:T(8,128)(2,1)}, u32[]{:S(2)}, u32[]{:S(2)}) collective-permute-start(bf16[256,1024]{1,0:T(8,128)(2,1)} %fusion.9), channel_id=1, source_target_pairs={{0,1},{1,2},{2,3},{3,0},{4,5},{5,6},{6,7},{7,4},{8,9},{9,10},{10,1... | collective-permute-start | bytes 1572872 | tf_op jit(solution)/shard_map/ppermute | solution.py:842
  414.9 26.3 %collective-permute-start.69 = (bf16[2,208,1024]{2,1,0:T(8,128)(2,1)}, bf16[2,208,1024]{2,1,0:T(8,128)(2,1)}, u32[]{:S(2)}, u32[]{:S(2)}) collective-permute-start(bf16[2,208,1024]{2,1,0:T(8,128)(2,1)} %add_convert_fusion.3), channel_id=1, source_target_pairs={{0,16},{4,20},{8,24},{12,28},{16,0},{20,4},{24,8},{28,12},{1,17},{... | collective-permute-start | bytes 2555912 | tf_op jit(solution)/shard_map/ppermute | solution.py:837
  484.1 26.2 %collective-permute-start.85 = (bf16[2,144,1024]{2,1,0:T(8,128)(2,1)S(1)}, bf16[2,144,1024]{2,1,0:T(8,128)(2,1)S(1)}, u32[]{:S(2)}, u32[]{:S(2)}) collective-permute-start(bf16[2,144,1024]{2,1,0:T(8,128)(2,1)S(1)} %add_convert_fusion.5), channel_id=1, source_target_pairs={{0,16},{4,20},{8,24},{12,28},{16,0},{20,4},{24,8},{28,12},{1,17},{... | collective-permute-start | bytes 1769480 | tf_op jit(solution)/shard_map/ppermute | solution.py:837
  (178 other events, 1886.8 us)

commit v4 on v3

--- a/solution.py
+++ b/solution.py
@@ -100,9 +100,9 @@
 
 
 def self_forward_kernel(
-    length_ref, bounds_ref, posq_ref, posk_ref, q_ref, e_ref, k_ref, v_ref, o_ref, p_ref, own_ref,
-    bucket_ref, one_hot_ref, spread_ref, bias_ref,
+    held, base, length_ref, bounds_ref, posq_ref, posk_ref, q_ref, e_ref, k_ref, v_ref, *refs,
 ):
+    o_ref, p_ref, own_ref, bucket_ref, one_hot_ref, spread_ref, bias_ref = refs[held:]
     slot = pl.program_id(0)
     group = pl.program_id(1)
     lanes, _, rows, _ = q_ref.shape
@@ -124,7 +124,8 @@
         for part in range(LANE // BUCKETS):
             copy = jnp.where(source == target + part * BUCKETS, 1.0, 0.0).astype(bf16)
             for block in range(heads * BUCKETS // LANE):
-                rows_e = rows_of(e_ref, 0, lanes, slice(block * LANE, (block + 1) * LANE))
+                column = base * GROUP * BUCKETS + block * LANE
+                rows_e = rows_of(e_ref, 0, lanes, slice(column, column + LANE))
                 head = block * (LANE // BUCKETS) + part
                 spread_ref[head] = jnp.where(keep, dot_nn(rows_e, copy), 0.0)
         distance = posq_ref[...] - posk_ref[...]
@@ -142,7 +143,7 @@
     low_half = lax.broadcasted_iota(jnp.int32, (1, LANE), 1) < HEAD_DIM
     lane_id = lax.broadcasted_iota(jnp.int32, (1, LANE), 1)
     own_all = [jnp.zeros((rows, LANE), f32) for _ in range(lanes)]
-    e_cols = pl.ds(pl.multiple_of(group * (GROUP * BUCKETS), LANE), GROUP * BUCKETS)
+    e_cols = pl.ds(pl.multiple_of((base + group) * (GROUP * BUCKETS), LANE), GROUP * BUCKETS)
     tables = [None] + [e_ref[lane, 0, :, e_cols].astype(f32) for lane in range(1, lanes)]
     for pair in range(GROUP // 2):
         cols = slice(pair * LANE, (pair + 1) * LANE)
@@ -388,28 +389,34 @@
     return jax.ShapeDtypeStruct(shape, dtype)
 
 
-def self_forward(length, bounds, posq, posk, q, e, k, v):
+def self_forward(length, bounds, posq, posk, q, e, k, v, part, parts, made=()):
     lanes, slots, rows, width = q.shape
-    heads = width // HEAD_DIM
+    all_heads = width // HEAD_DIM
+    heads = all_heads // parts
     keys = posk.shape[1]
     count = lanes * rows
     groups = heads // GROUP
+    base = part * groups
+
+    def block(array):
+        return pl.BlockSpec((array.shape[0], 1, array.shape[2], GROUP * HEAD_DIM), lambda s, g: (0, s, 0, base + g))
+
+    inputs = [length, bounds, posq, posk, q, e, k, v]
     return pl.pallas_call(
-        self_forward_kernel,
+        functools.partial(self_forward_kernel, len(made), base),
         grid=(slots, groups),
         in_specs=[
-            SMEM_SPEC, SMEM_SPEC, whole_block(posq), whole_block(posk),
-            head_block(q), slot_block(e), head_block(k), head_block(v),
-        ],
+            SMEM_SPEC, SMEM_SPEC, whole_block(posq), whole_block(posk), block(q), slot_block(e), block(k), block(v),
+        ] + [pl.BlockSpec(memory_space=pl.ANY)] * len(made),
         out_specs=[
-            head_block(q),
-            pl.BlockSpec((1, GROUP, count, keys), lambda s, g: (s, g, 0, 0)),
-            pl.BlockSpec((1, 1, count, LANE), lambda s, g: (s, g, 0, 0)),
+            block(q),
+            pl.BlockSpec((1, GROUP, count, keys), lambda s, g: (s, base + g, 0, 0)),
+            pl.BlockSpec((1, 1, count, LANE), lambda s, g: (s, base + g, 0, 0)),
         ],
         out_shape=[
             shaped(q.shape, bf16),
-            shaped((slots, heads, count, keys), bf16),
-            shaped((slots, groups, count, LANE), f32),
+            shaped((slots, all_heads, count, keys), bf16),
+            shaped((slots, all_heads // GROUP, count, LANE), f32),
         ],
         scratch_shapes=[
             pltpu.VMEM((rows, keys), jnp.int32),
@@ -417,10 +424,11 @@
             pltpu.VMEM((heads, count, SUB * BUCKETS), f32),
             pltpu.VMEM((heads, count, keys), f32),
         ],
+        input_output_aliases={len(inputs) + i: i for i in range(len(made))},
         compiler_params=params(),
         cost_estimate=SMALL,
         name="self_forward",
-    )(length, bounds, posq, posk, q, e, k, v)
+    )(*inputs, *made)
 
 
 def self_backward(bounds, posq, posk, p, own, do, q, k, v, part, parts, made=()):
@@ -1202,15 +1210,37 @@
     )(place, *lefts, *rights, *arrivals, *(extra or ()), *(plain or ()))
 
 
-def unpack_kernel(layout, copies, cut, place_ref, *refs):
+def unpack_kernel(layout, copies, cut, vectors, place_ref, *refs):
     arrivals = refs[: len(SPREAD_PLAN)]
     outs = refs[len(SPREAD_PLAN) :]
+    weights = len(layout) - (1 if vectors else 0)
     chosen = place_copies(copies, cut)
     for arrival, (offset, part) in zip(arrivals, SPREAD_PLAN):
         for row, rows, col, cols, number, prow, wcol in chosen(part):
             piece_rows = layout[number][0] // 8
-            start = pl.multiple_of(place_ref[offset] * piece_rows + prow, 8)
-            outs[number][pl.ds(start, rows), wcol : wcol + cols] = arrival[row : row + rows, col : col + cols].astype(f32)
+            if number < weights:
+                start = pl.multiple_of(place_ref[offset] * piece_rows + prow, 8)
+                target = outs[number]
+                target[pl.ds(start, rows), wcol : wcol + cols] = arrival[row : row + rows, col : col + cols].astype(f32)
+            else:
+                start = pl.multiple_of(place_ref[offset] * piece_rows, 16)
+                outs[-1][pl.ds(start, rows), :] = arrival[row : row + rows, :LANE]
+    if vectors:
+        pieces, width = 8, outs[weights].shape[1]
+        part = width // pieces
+        copy_row = lax.broadcasted_iota(jnp.int32, (LANE, width), 0)
+        copy_col = lax.broadcasted_iota(jnp.int32, (LANE, width), 1)
+        copy = jnp.where(copy_row == lax.rem(copy_col, part), 1.0, 0.0).astype(bf16)
+        wide = dot_nn(outs[-1][...], copy)
+        piece = lax.broadcasted_iota(jnp.int32, wide.shape, 0) // 16
+        column = lax.broadcasted_iota(jnp.int32, wide.shape, 1) // part
+        wide = jnp.where(piece == column, wide, 0.0).astype(bf16)
+        pick_row = lax.broadcasted_iota(jnp.int32, (16, pieces * 16), 0)
+        pick_col = lax.broadcasted_iota(jnp.int32, (16, pieces * 16), 1)
+        pick = jnp.where(pick_row == lax.rem(pick_col, 16), 1.0, 0.0).astype(bf16)
+        whole = dot_nn(pick, wide)
+        for index in range(vectors):
+            outs[weights + index][...] = whole[index : index + 1, :]
 
 
 def add_low(a, b):
@@ -1269,14 +1299,18 @@
         self.near = corner_spread([self.near[0], from_x, from_y], 0, self.cut)
         return self.near[3:]
 
-    def grads(self, arrivals):
+    def grads(self, arrivals, vectors=0):
         place = jnp.stack([piece_number(self.c_index ^ j) for j in range(8)]).astype(jnp.int32)
         vmem = pl.BlockSpec(memory_space=pltpu.VMEM)
+        out_shape = [shaped((rows, columns), f32) for rows, columns in self.layout]
+        if vectors:
+            out_shape[-1:] = [shaped((1, self.layout[0][0]), f32)] * vectors
         return pl.pallas_call(
-            functools.partial(unpack_kernel, self.layout, self.copies, self.cut),
+            functools.partial(unpack_kernel, self.layout, self.copies, self.cut, vectors),
             in_specs=[SMEM_SPEC] + [vmem] * len(arrivals),
-            out_specs=[vmem] * len(self.layout),
-            out_shape=[shaped((rows, columns), f32) for rows, columns in self.layout],
+            out_specs=[vmem] * len(out_shape),
+            out_shape=out_shape,
+            scratch_shapes=[pltpu.VMEM((128, LANE), bf16)] if vectors else [],
             compiler_params=params(),
             cost_estimate=SMALL,
             name="unpack",
@@ -1302,7 +1336,7 @@
     seq_len = ctx_count * rows
     all_rows = lanes * slots * rows
     slab = (lanes, slots, rows, width)
-    paired = ctx_count == 8 and steps % 2 == 0 and query_weight.shape[0] % 256 == 0 and width == 1024
+    paired = ctx_count == 8 and steps == 4 and query_weight.shape[0] % 256 == 0 and width == 1024
     paired = paired and enc_rows == rows
 
     norms = jnp.stack(
@@ -1363,7 +1397,7 @@
         )
         second_stack = stack_rows(tie(*ring, q)[: steps - 1])
         second_near = list(first_spread(second_stack))
-        feed_hops = [z_hop(after(feed_piece, second_stack), step) for step in range(1, steps - 1)]
+        feed_ring = [z_hop(after(feed_piece, second_stack), 1)]
         k = after(k, second_stack)
         peers = [c_index ^ j for j in range(8)]
     else:
@@ -1393,20 +1427,22 @@
 
     q, e = q.reshape(slab), e.reshape(lanes, slots, rows, -1)
     k, v = k.reshape(-1, slots, rows, width), v.reshape(-1, slots, rows, width)
-    o, probs, own = self_forward(slot_len, bounds, positions[:, None], key_positions[None], q, e, k, v)
+    self_inputs = (slot_len, bounds, positions[:, None], key_positions[None])
+    made = self_forward(*self_inputs, q, e, k, v, 0, 2)
+    q_late = q
+    if paired:
+        held, q_late, _ = tie(feed_ring[0], q, made[0])
+        feed_ring.append(z_hop(held, 1))
+    o, probs, own = self_forward(*self_inputs, q_late, e, k, v, 1, 2, made)
     o_flat = o.reshape(all_rows, width)
     if paired:
-        second_near[1], second_near[2], feed_hops[0], feed_piece, _ = tie(
-            second_near[1], second_near[2], feed_hops[0], feed_piece, o
-        )
-        feed_hops.append(z_hop(feed_piece, steps - 1))
+        second_near[1], second_near[2], held, _ = tie(second_near[1], second_near[2], feed_ring[1], o)
+        feed_ring.append(z_hop(held, 1))
         second_near = corner_spread(second_near, 1, cuts[1])
         second_far = [ctx_hop(second_near[0], CORE)]
-        *feed_hops, second_near[1], second_near[2], second_near[3], second_near[4], second_far[0] = tie(
-            *feed_hops, *second_near[1:], second_far[0]
-        )
+        feed_ring[2], *second_near[1:], second_far[0] = tie(feed_ring[2], *second_near[1:], second_far[0])
         second_far += [ctx_hop(item, CORE) for item in second_near[1:]]
-        third_stack = stack_rows(tie(*feed_hops, *second_far[2:])[: steps - 1])
+        third_stack = stack_rows(tie(*feed_ring, *second_far[2:])[: steps - 1])
         third_near = list(first_spread(third_stack))
         (ck, cv), enc_flat, second = project(
             None, enc_parts, second_set, second_near + second_far, second_layout, cuts[1],
@@ -1576,14 +1612,14 @@
         second_sum.near[0] = held
         second_far = far(*second_sum.near[:3])
         third_grads = third_sum.grads(third_sum.near + third_far)
-        first_x, first_y, *second_far, _ = tie(*spread, *second_far, third_grads[0])
+        first_x, first_y, *second_far = tie(*spread, *second_far)
         corners = first_sum.corners(first_x, first_y)
         second_far += far(*second_sum.near[3:])
-        *second_grads, norm_sums = second_sum.grads(second_sum.near + second_far)
-        norm_sums = norm_sums.reshape(8, 16, 1024)[:, :norm_count, : norm_shard // 8]
-        norm_grads = [item for item in norm_sums.transpose(1, 0, 2).reshape(norm_count, norm_shard)]
-        *first_sum.near[1:], second_grads[0], norm_grads = tie(first_x, first_y, *corners, second_grads[0], norm_grads)
-        first_grads = first_sum.grads(first_sum.near + far(*first_sum.near))
+        *first_sum.near[1:], second_far[3], second_far[4], _ = tie(first_x, first_y, *corners, *second_far[3:], third_grads[0])
+        first_far = far(*first_sum.near)
+        outs = second_sum.grads(second_sum.near + second_far, norm_count)
+        second_grads, norm_grads = outs[:-norm_count], [item.reshape(norm_shard) for item in outs[-norm_count:]]
+        first_grads = first_sum.grads(first_sum.near + first_far)
     else:
         *main_part, other_part = pair_rows(back_k, back_v, key_full, value_full, ctx_count, slots * rows)
         back_x = back_one + matmul_back(back_q, query_full) + matmul_back(back_e, relative_full)

time: 596 us -> 575 us (0.965)
  starting transfers between devices: 87.3 us -> 70.3 us
  local copies, waits for them, and re-layouts: 34.3 us -> 27.8 us
    ppermute x18, starting transfers between devices: 28.1 us -> 10.4 us  [z_hop(): lax.ppermute(array, 'fsdp', [(i, (i + step) % size) for i in range(size)])]
    ppermute x18, waiting for transfers between devices: 82.3 us -> 67.5 us  [z_hop(): lax.ppermute(array, 'fsdp', [(i, (i + step) % size) for i in range(size)])]
    ppermute x100, waiting for transfers between devices: 92.7 us -> 103 us  [ctx_hop(): return lax.ppermute(array, 'ctx', [(i, i ^ bit) for i in range(size)])]
    pallas_call x1 -> x2, Pallas kernels: 20.2 us -> 24.1 us  [self_forward(): pl.pallas_call(functools.partial(self_forward_kernel, len(made), base), g...]
    unnamed x174 -> x194, local copies, waits for them, and re-layouts: 12.8 us -> 11.5 us
  transfers between devices with their start and end apart: 118 -> 118, of which waited for: 48 -> 49; matrix products, arithmetic and copies ran while one was open for 7% -> 7% of each run, Pallas kernels for 33% -> 35%
where the time goes in v4:
time: 575 us; the launch traced here: 566 us
  Pallas kernels  264 us (46%)
  waiting for transfers between devices  171 us (30%)
  starting transfers between devices  70.3 us (12%)
  other arithmetic  30.7 us (5%)
  local copies, waits for them, and re-layouts  27.8 us (5%)
    ppermute x100, waiting for transfers between devices, ctx_hop(): return lax.ppermute(array, 'ctx', [(i, i ^ bit) for i in range(size)])  103 us
    ppermute x18, waiting for transfers between devices, z_hop(): lax.ppermute(array, 'fsdp', [(i, (i + step) % size) for i in range(size)])  67.5 us
    ppermute x100, starting transfers between devices, ctx_hop(): return lax.ppermute(array, 'ctx', [(i, i ^ bit) for i in range(size)])  59.9 us
    pallas_call x1, Pallas kernels, feed_forward_backward(): pl.pallas_call(functools.partial(feed_kernel, steps if sending else 0, (l...  42.5 us
    pallas_call x3, Pallas kernels, fold_grads(): pl.pallas_call(functools.partial(fold_grads_kernel, groups, steps, extra_...  38.6 us
    pallas_call x2, Pallas kernels, self_backward(): pl.pallas_call(functools.partial(self_backward_kernel, len(made)), grid=(...  31.6 us
    pallas_call x2, Pallas kernels, project(): pl.pallas_call(functools.partial(project_kernel, layout, copies, cut, ste...  29.3 us
    pallas_call x2, Pallas kernels, self_forward(): pl.pallas_call(functools.partial(self_forward_kernel, len(made), base), g...  24.1 us
  transfers between devices with their start and end apart: 118, of which 49 were waited for; matrix products, arithmetic and copies ran while one was open for 7% of the time, Pallas kernels for 35%

profile of v4, /device:TPU:0, one launch (start us, length us, event | category | flops | bytes accessed | tf_op | source)
XLA Modules:
  0.0 565.7 jit_solution(13091400974778390330)
XLA Ops:
  10.7 6.7 %collective-permute-done.refs_0_ = bf16[112,1024]{1,0:T(8,128)(2,1)S(1)} collective-permute-done((bf16[112,1024]{1,0:T(8,128)(2,1)}, bf16[112,1024]{1,0:T(8,128)(2,1)S(1)}, u32[]{:S(2)}, u32[]{:S(2)}) %collective-permute-start) | collective-permute-done | bytes 229408 | tf_op jit(solution)/shard_map/ppermute | solution.py:850
  22.7 7.1 %collective-permute-done.5.refs_1_ = bf16[112,1024]{1,0:T(8,128)(2,1)S(1)} collective-permute-done((bf16[112,1024]{1,0:T(8,128)(2,1)S(1)}, bf16[112,1024]{1,0:T(8,128)(2,1)S(1)}, u32[]{:S(2)}, u32[]{:S(2)}) %collective-permute-start.5) | collective-permute-done | bytes 229408 | tf_op jit(solution)/shard_map/ppermute | solution.py:850
  48.8 8.8 %collective-permute-done.15.refs_0_ = bf16[176,1024]{1,0:T(8,128)(2,1)S(1)} collective-permute-done((bf16[176,1024]{1,0:T(8,128)(2,1)}, bf16[176,1024]{1,0:T(8,128)(2,1)S(1)}, u32[]{:S(2)}, u32[]{:S(2)}) %collective-permute-start.15) | collective-permute-done | bytes 360480 | tf_op jit(solution)/shard_map/ppermute | solution.py:850
  64.7 7.8 %collective-permute-done.21.refs_16_ = bf16[3,48,1024]{2,1,0:T(8,128)(2,1)S(1)} collective-permute-done((bf16[3,48,1024]{2,1,0:T(8,128)(2,1)S(1)}, bf16[3,48,1024]{2,1,0:T(8,128)(2,1)S(1)}, u32[]{:S(2)}, u32[]{:S(2)}) %collective-permute-start.21) | collective-permute-done | bytes 294944 | tf_op jit(solution)/shard_map/ppermute | solution.py:845
  80.4 14.5 %project.2 = (bf16[384,1024]{1,0:T(8,128)(2,1)}, bf16[384,512]{1,0:T(8,128)(2,1)}, bf16[1280,1024]{1,0:T(8,128)(2,1)}, bf16[1280,1024]{1,0:T(8,128)(2,1)}, bf16[...) custom-call(s32[12]{0:T(128)} %stack.153.place_ref, ...), custom_call_target="tpu_custom_call" | custom-call | flops 1000 | bytes 1000 | tf_op jit(solution)/shard_map/project/pallas_call | solution.py:991
  99.7 12.0 %self_forward.2 = (bf16[3,2,64,1024]{3,2,1,0:T(8,128)(2,1)}, bf16[2,16,192,512]{3,2,1,0:T(8,128)(2,1)}, f32[2,4,192,128]{3,2,1,0:T(8,128)}) custom-call(s32[2]{0:T(128)} %length_ref.4, s32[33]{0:T(128)} %convert_reduce_fusion.bounds_ref, s32[64,1]{1,0:T(8,128)} %copy.62.posq_ref, s32[1,512]{1,0:T(1,128)} %bitcast.214, bf16[3,2,64,1024]{3,2,1,0:T(8,128)(2,1)} %bitcast.166, ...), custom_call_target="tpu_custom_call" | custom-call | flops 1000 | bytes 1000 | tf_op jit(solution)/shard_map/self_forward/pallas_call | solution.py:405
  114.1 12.1 %self_forward.3 = (bf16[3,2,64,1024]{3,2,1,0:T(8,128)(2,1)}, bf16[2,16,192,512]{3,2,1,0:T(8,128)(2,1)}, f32[2,4,192,128]{3,2,1,0:T(8,128)}) custom-call(s32[2]{0:T(128)} %length_ref.4, s32[33]{0:T(128)} %convert_reduce_fusion.bounds_ref, s32[64,1]{1,0:T(8,128)} %copy.62.posq_ref, ...), custom_call_target="tpu_custom_call", output_to_operand_aliasing={{0}: (8, {}), {1}: (9, {}), {2}: (10, {})} | custom-call | flops 1000 | bytes 1000 | tf_op jit(solution)/shard_map/self_forward/pallas_call | solution.py:405
  134.3 11.5 %collective-permute-done.35.refs_18_ = bf16[3,80,1024]{2,1,0:T(8,128)(2,1)S(1)} collective-permute-done((bf16[3,80,1024]{2,1,0:T(8,128)(2,1)S(1)}, bf16[3,80,1024]{2,1,0:T(8,128)(2,1)S(1)}, u32[]{:S(2)}, u32[]{:S(2)}) %collective-permute-start.35) | collective-permute-done | bytes 491552 | tf_op jit(solution)/shard_map/ppermute | solution.py:845
  159.5 14.8 %project.3 = (bf16[1024,1024]{1,0:T(8,128)(2,1)}, bf16[1024,1024]{1,0:T(8,128)(2,1)}, bf16[1024,1024]{1,0:T(8,128)(2,1)}, bf16[1024,1024]{1,0:T(8,128)(2,1)}, bf...) custom-call(s32[12]{0:T(128)} %stack.153.place_ref, ...), custom_call_target="tpu_custom_call" | custom-call | flops 1000 | bytes 1000 | tf_op jit(solution)/shard_map/project/pallas_call | solution.py:991
  174.3 7.0 %query_rows.1 = (f32[384,1024]{1,0:T(8,128)}, f32[384,1024]{1,0:T(8,128)}, f32[384,1]{1,0:T(8,128)}, bf16[384,1024]{1,0:T(8,128)(2,1)}, bf16[384,1024]{1,0:T(8,128)(2,1)}, /*index=5*/f32[16,1024]{1,0:T(8,128)}) custom-call(bf16[384,1024]{1,0:T(8,128)(2,1)} %bitcast.160, bf16[384,1024]{1,0:T(8,128)(2,1)} %bitcast.163, ...), custom_call_target="tpu_custom_call" | custom-call | flops 1000 | bytes 1000 | tf_op jit(solution)/shard_map/query_rows/pallas_call | solution.py:1038
  181.3 11.8 %cross_forward.1 = (bf16[3,2,64,1024]{3,2,1,0:T(8,128)(2,1)}, bf16[2,16,192,512]{3,2,1,0:T(8,128)(2,1)}) custom-call(s32[2]{0:T(128)} %length_ref.5, s32[1,512]{1,0:T(1,128)} %add.322.posk_ref, bf16[3,2,64,1024]{3,2,1,0:T(8,128)(2,1)} %bitcast.188, bf16[8,2,64,1024]{3,2,1,0:T(8,128)(2,1)} %bitcast.170, bf16[8,2,64,1024]{3,2,1,0:T(8,128)(2,1)} %bitcast.172), custom_call_target="tpu_custom_call" | custom-call | flops 1000 | bytes 1000 | tf_op jit(solution)/shard_map/cross_forward/pallas_call | solution.py:483
  198.2 17.6 %collective-permute-done.43.refs_5_ = bf16[3,128,1024]{2,1,0:T(8,128)(2,1)S(1)} collective-permute-done((bf16[3,128,1024]{2,1,0:T(8,128)(2,1)S(1)}, bf16[3,128,1024]{2,1,0:T(8,128)(2,1)S(1)}, u32[]{:S(2)}, u32[]{:S(2)}) %collective-permute-start.43) | collective-permute-done | bytes 786464 | tf_op jit(solution)/shard_map/ppermute | solution.py:845
  221.4 42.5 %feed.1 = (bf16[384,1024]{1,0:T(8,128)(2,1)}, bf16[384,1024]{1,0:T(8,128)(2,1)}, bf16[384,4096]{1,0:T(8,128)(2,1)}, bf16[384,4096]{1,0:T(8,128)(2,1)}, bf16[384,...) custom-call(s32[13]{0:T(128)} %concatenate.24.core_ref, ...), custom_call_target="tpu_custom_call" | custom-call | flops 1000 | bytes 1000 | tf_op jit(solution)/shard_map/feed/pallas_call | solution.py:647
  265.2 13.6 %cross_backward.1 = (bf16[3,2,64,1024]{3,2,1,0:T(8,128)(2,1)}, bf16[8,2,64,1024]{3,2,1,0:T(8,128)(2,1)}, bf16[8,2,64,1024]{3,2,1,0:T(8,128)(2,1)}) custom-call(bf16[2,16,192,512]{3,2,1,0:T(8,128)(2,1)} %get-tuple-element.373.p_ref, bf16[3,2,64,1024]{3,2,1,0:T(8,128)(2,1)} %bitcast.206, bf16[3,2,64,1024]{3,2,1,0:T(8,128)(2,1)} %bitcast.189, ...), custom_call_target="tpu_custom_call" | custom-call | flops 1000 | bytes 1000 | tf_op jit(solution)/shard_map/cross_backward/pallas_call | solution.py:500
  279.0 13.4 %fold_grads.3 = (bf16[2,256,1024]{2,1,0:T(8,128)(2,1)}, bf16[2,256,1024]{2,1,0:T(8,128)(2,1)}, bf16[2,256,1024]{2,1,0:T(8,128)(2,1)}, bf16[2,256,1024]{2,1,0:T(8...) custom-call(s32[3]{0:T(128)} %pad_add_fusion.1.place_ref, ...), custom_call_target="tpu_custom_call" | custom-call | flops 1000 | bytes 1000 | tf_op jit(solution)/shard_map/fold_grads/pallas_call | solution.py:1194
  293.5 21.2 %middle_backward.1 = (f32[384,1024]{1,0:T(8,128)}, bf16[384,1024]{1,0:T(8,128)(2,1)}, bf16[384,1024]{1,0:T(8,128)(2,1)}, f32[2,1024]{1,0:T(2,128)}, bf16[512,102...) custom-call(s32[1]{0:T(128)} %bitcast.core_ref, ...), custom_call_target="tpu_custom_call" | custom-call | flops 1000 | bytes 1000 | tf_op jit(solution)/shard_map/middle_backward/pallas_call | solution.py:745
  326.4 15.8 %self_backward.2 = (bf16[3,2,64,1024]{3,2,1,0:T(8,128)(2,1)}, bf16[10,2,64,1024]{3,2,1,0:T(8,128)(2,1)}, bf16[10,2,64,1024]{3,2,1,0:T(8,128)(2,1)}, bf16[3,2,64,512]{3,2,1,0:T(8,128)(2,1)}) custom-call(s32[33]{0:T(128)} %convert_reduce_fusion.bounds_ref, s32[64,1]{1,0:T(8,128)} %copy.62.posq_ref, s32[1,512]{1,0:T(1,128)} %bitcast.216, ...), custom_call_target="tpu_custom_call" | custom-call | flops 1000 | bytes 1000 | tf_op jit(solution)/shard_map/self_backward/pallas_call | solution.py:446
  355.6 13.5 %fold_grads.4 = (bf16[2,208,1024]{2,1,0:T(8,128)(2,1)}, bf16[2,208,1024]{2,1,0:T(8,128)(2,1)}, bf16[2,208,1024]{2,1,0:T(8,128)(2,1)}, bf16[2,208,1024]{2,1,0:T(8...) custom-call(s32[3]{0:T(128)} %pad_add_fusion.1.place_ref, ...), custom_call_target="tpu_custom_call" | custom-call | flops 1000 | bytes 1000 | tf_op jit(solution)/shard_map/fold_grads/pallas_call | solution.py:1194
  380.6 15.8 %self_backward.3 = (bf16[3,2,64,1024]{3,2,1,0:T(8,128)(2,1)}, bf16[10,2,64,1024]{3,2,1,0:T(8,128)(2,1)}, bf16[10,2,64,1024]{3,2,1,0:T(8,128)(2,1)}, bf16[3,2,64,512]{3,2,1,0:T(8,128)(2,1)}) custom-call(s32[33]{0:T(128)} %convert_reduce_fusion.bounds_ref, ...), custom_call_target="tpu_custom_call", output_to_operand_aliasing={{0}: (9, {}), {1}: (10, {}), {2}: (11, {}), {3}: (12, {})} | custom-call | flops 1000 | bytes 1000 | tf_op jit(solution)/shard_map/self_backward/pallas_call | solution.py:446
  407.2 19.2 %last_backward.1 = (bf16[512,1024]{1,0:T(8,128)(2,1)}, bf16[512,1024]{1,0:T(8,128)(2,1)}, bf16[512,1024]{1,0:T(8,128)(2,1)}, bf16[512,512]{1,0:T(8,128)(2,1)}, b...) custom-call(s32[1]{0:T(128)} %bitcast.core_ref, bf16[384,1024]{1,0:T(8,128)(2,1)} %bitcast.161, ...), custom_call_target="tpu_custom_call" | custom-call | flops 1000 | bytes 1000 | tf_op jit(solution)/shard_map/last_backward/pallas_call | solution.py:824
  439.5 11.8 %fold_grads.5 = (bf16[2,144,1024]{2,1,0:T(8,128)(2,1)}, bf16[2,144,1024]{2,1,0:T(8,128)(2,1)}, bf16[2,144,1024]{2,1,0:T(8,128)(2,1)}, bf16[2,144,1024]{2,1,0:T(8...) custom-call(s32[3]{0:T(128)} %pad_add_fusion.1.place_ref, ...), custom_call_target="tpu_custom_call" | custom-call | flops 1000 | bytes 1000 | tf_op jit(solution)/shard_map/fold_grads/pallas_call | solution.py:1194
  460.0 7.7 %collective-permute-done.79 = bf16[176,1024]{1,0:T(8,128)(2,1)S(1)} collective-permute-done((bf16[176,1024]{1,0:T(8,128)(2,1)S(1)}, bf16[176,1024]{1,0:T(8,128)(2,1)S(1)}, u32[]{:S(2)}, u32[]{:S(2)}) %collective-permute-start.79) | collective-permute-done | bytes 360480 | tf_op jit(solution)/shard_map/ppermute | solution.py:850
  476.2 6.6 %collective-permute-done.82 = bf16[176,1024]{1,0:T(8,128)(2,1)S(1)} collective-permute-done((bf16[176,1024]{1,0:T(8,128)(2,1)S(1)}, bf16[176,1024]{1,0:T(8,128)(2,1)S(1)}, u32[]{:S(2)}, u32[]{:S(2)}) %collective-permute-start.82) | collective-permute-done | bytes 360480 | tf_op jit(solution)/shard_map/ppermute | solution.py:850
  485.9 8.9 %collective-permute-done.84 = bf16[2,144,1024]{2,1,0:T(8,128)(2,1)S(1)} collective-permute-done((bf16[2,144,1024]{2,1,0:T(8,128)(2,1)S(1)}, bf16[2,144,1024]{2,1,0:T(8,128)(2,1)S(1)}, u32[]{:S(2)}, u32[]{:S(2)}) %collective-permute-start.84) | collective-permute-done | bytes 589856 | tf_op jit(solution)/shard_map/ppermute | solution.py:845
  (508 shorter events, 241.4 us)
Async XLA Ops:
  97.2 31.6 %collective-permute-start.32 = (bf16[3,176,1024]{2,1,0:T(8,128)(2,1)}, bf16[3,176,1024]{2,1,0:T(8,128)(2,1)}, u32[]{:S(2)}, u32[]{:S(2)}) collective-permute-start(bf16[3,176,1024]{2,1,0:T(8,128)(2,1)} %stack_rows.4.refs_14_), channel_id=1, source_target_pairs={{0,16},{4,20},{8,24},{12,28},{16,0},{20,4},{24,8},{28,12},{1,17},{... | collective-permute-start | bytes 3244040 | tf_op jit(solution)/shard_map/ppermute | solution.py:845
  97.7 31.0 %collective-permute-start.31 = (bf16[3,176,1024]{2,1,0:T(8,128)(2,1)}, bf16[3,176,1024]{2,1,0:T(8,128)(2,1)}, u32[]{:S(2)}, u32[]{:S(2)}) collective-permute-start(bf16[3,176,1024]{2,1,0:T(8,128)(2,1)} %stack_rows.4.refs_14_), channel_id=1, source_target_pairs={{0,8},{4,12},{8,0},{12,4},{16,24},{20,28},{24,16},{28,20},{1,9},{5... | collective-permute-start | bytes 3244040 | tf_op jit(solution)/shard_map/ppermute | solution.py:845
  154.3 38.8 %collective-permute-start.42 = (bf16[3,256,1024]{2,1,0:T(8,128)(2,1)}, bf16[3,256,1024]{2,1,0:T(8,128)(2,1)}, u32[]{:S(2)}, u32[]{:S(2)}) collective-permute-start(bf16[3,256,1024]{2,1,0:T(8,128)(2,1)} %stack_rows.5.refs_2_), channel_id=1, source_target_pairs={{0,16},{4,20},{8,24},{12,28},{16,0},{20,4},{24,8},{28,12},{1,17},{... | collective-permute-start | bytes 4718600 | tf_op jit(solution)/shard_map/ppermute | solution.py:845
  155.9 37.2 %collective-permute-start.41 = (bf16[3,256,1024]{2,1,0:T(8,128)(2,1)}, bf16[3,256,1024]{2,1,0:T(8,128)(2,1)}, u32[]{:S(2)}, u32[]{:S(2)}) collective-permute-start(bf16[3,256,1024]{2,1,0:T(8,128)(2,1)} %stack_rows.5.refs_2_), channel_id=1, source_target_pairs={{0,8},{4,12},{8,0},{12,4},{16,24},{20,28},{24,16},{28,20},{1,9},{5... | collective-permute-start | bytes 4718600 | tf_op jit(solution)/shard_map/ppermute | solution.py:845
  157.3 40.9 %collective-permute-start.45 = (bf16[3,256,1024]{2,1,0:T(8,128)(2,1)}, bf16[3,256,1024]{2,1,0:T(8,128)(2,1)}, u32[]{:S(2)}, u32[]{:S(2)}) collective-permute-start(bf16[3,256,1024]{2,1,0:T(8,128)(2,1)} %stack_rows.5.refs_2_), channel_id=1, source_target_pairs={{0,4},{4,0},{8,12},{12,8},{16,20},{20,16},{24,28},{28,24},{1,5},{5... | collective-permute-start | bytes 4718600 | tf_op jit(solution)/shard_map/ppermute | solution.py:845
  193.2 23.8 %collective-permute-start.46 = (bf16[3,256,1024]{2,1,0:T(8,128)(2,1)}, bf16[3,256,1024]{2,1,0:T(8,128)(2,1)}, u32[]{:S(2)}, u32[]{:S(2)}) collective-permute-start(bf16[3,256,1024]{2,1,0:T(8,128)(2,1)} %collective-permute-done.41.refs_3_), channel_id=1, source_target_pairs={{0,4},{4,0},{8,12},{12,8},{16,20},{20,16},{24,28},{28,24},{1,5},{5... | collective-permute-start | bytes 4718600 | tf_op jit(solution)/shard_map/ppermute | solution.py:845
  193.4 23.6 %collective-permute-start.47 = (bf16[3,256,1024]{2,1,0:T(8,128)(2,1)}, bf16[3,256,1024]{2,1,0:T(8,128)(2,1)}, u32[]{:S(2)}, u32[]{:S(2)}) collective-permute-start(bf16[3,256,1024]{2,1,0:T(8,128)(2,1)} %collective-permute-done.42.refs_4_), channel_id=1, source_target_pairs={{0,4},{4,0},{8,12},{12,8},{16,20},{20,16},{24,28},{28,24},{1,5},{5... | collective-permute-start | bytes 4718600 | tf_op jit(solution)/shard_map/ppermute | solution.py:845
  292.3 25.7 %collective-permute-start.53 = (bf16[2,256,1024]{2,1,0:T(8,128)(2,1)}, bf16[2,256,1024]{2,1,0:T(8,128)(2,1)}, u32[]{:S(2)}, u32[]{:S(2)}) collective-permute-start(bf16[2,256,1024]{2,1,0:T(8,128)(2,1)} %get-tuple-element.386), channel_id=1, source_target_pairs={{0,8},{4,12},{8,0},{12,4},{16,24},{20,28},{24,16},{28,20},{1,9},{5... | collective-permute-start | bytes 3145736 | tf_op jit(solution)/shard_map/ppermute | solution.py:845
  292.9 25.3 %collective-permute-start.54 = (bf16[2,256,1024]{2,1,0:T(8,128)(2,1)}, bf16[2,256,1024]{2,1,0:T(8,128)(2,1)}, u32[]{:S(2)}, u32[]{:S(2)}) collective-permute-start(bf16[2,256,1024]{2,1,0:T(8,128)(2,1)} %get-tuple-element.387), channel_id=1, source_target_pairs={{0,16},{4,20},{8,24},{12,28},{16,0},{20,4},{24,8},{28,12},{1,17},{... | collective-permute-start | bytes 3145736 | tf_op jit(solution)/shard_map/ppermute | solution.py:845
  321.2 24.6 %collective-permute-start.56 = (bf16[2,256,1024]{2,1,0:T(8,128)(2,1)}, bf16[2,256,1024]{2,1,0:T(8,128)(2,1)}, u32[]{:S(2)}, u32[]{:S(2)}) collective-permute-start(bf16[2,256,1024]{2,1,0:T(8,128)(2,1)} %add_convert_fusion), channel_id=1, source_target_pairs={{0,8},{4,12},{8,0},{12,4},{16,24},{20,28},{24,16},{28,20},{1,9},{5... | collective-permute-start | bytes 3145736 | tf_op jit(solution)/shard_map/ppermute | solution.py:845
  325.4 24.2 %collective-permute-start.55 = (bf16[2,256,1024]{2,1,0:T(8,128)(2,1)}, bf16[2,256,1024]{2,1,0:T(8,128)(2,1)}, u32[]{:S(2)}, u32[]{:S(2)}) collective-permute-start(bf16[2,256,1024]{2,1,0:T(8,128)(2,1)} %add_convert_fusion.1), channel_id=1, source_target_pairs={{0,16},{4,20},{8,24},{12,28},{16,0},{20,4},{24,8},{28,12},{1,17},{... | collective-permute-start | bytes 3145736 | tf_op jit(solution)/shard_map/ppermute | solution.py:845
  325.9 23.7 %collective-permute-start.57 = (bf16[512,1024]{1,0:T(8,128)(2,1)}, bf16[512,1024]{1,0:T(8,128)(2,1)}, u32[]{:S(2)}, u32[]{:S(2)}) collective-permute-start(bf16[512,1024]{1,0:T(8,128)(2,1)} %get-tuple-element.412), channel_id=1, source_target_pairs={{0,4},{4,0},{8,12},{12,8},{16,20},{20,16},{24,28},{28,24},{1,5},{5... | collective-permute-start | bytes 3145736 | tf_op jit(solution)/shard_map/ppermute | solution.py:845
  325.9 23.7 %collective-permute-start.58 = (bf16[512,1024]{1,0:T(8,128)(2,1)}, bf16[512,1024]{1,0:T(8,128)(2,1)}, u32[]{:S(2)}, u32[]{:S(2)}) collective-permute-start(bf16[512,1024]{1,0:T(8,128)(2,1)} %get-tuple-element.413), channel_id=1, source_target_pairs={{0,4},{4,0},{8,12},{12,8},{16,20},{20,16},{24,28},{28,24},{1,5},{5... | collective-permute-start | bytes 3145736 | tf_op jit(solution)/shard_map/ppermute | solution.py:845
  326.4 23.2 %collective-permute-start.59 = (bf16[512,1024]{1,0:T(8,128)(2,1)}, bf16[512,1024]{1,0:T(8,128)(2,1)}, u32[]{:S(2)}, u32[]{:S(2)}) collective-permute-start(bf16[512,1024]{1,0:T(8,128)(2,1)} %get-tuple-element.414), channel_id=1, source_target_pairs={{0,4},{4,0},{8,12},{12,8},{16,20},{20,16},{24,28},{28,24},{1,5},{5... | collective-permute-start | bytes 3145736 | tf_op jit(solution)/shard_map/ppermute | solution.py:845
  350.2 25.5 %collective-permute-start.60 = (bf16[2,256,1024]{2,1,0:T(8,128)(2,1)}, bf16[2,256,1024]{2,1,0:T(8,128)(2,1)}, u32[]{:S(2)}, u32[]{:S(2)}) collective-permute-start(bf16[2,256,1024]{2,1,0:T(8,128)(2,1)} %get-tuple-element.424), channel_id=1, source_target_pairs={{0,8},{4,12},{8,0},{12,4},{16,24},{20,28},{24,16},{28,20},{1,9},{5... | collective-permute-start | bytes 3145736 | tf_op jit(solution)/shard_map/ppermute | solution.py:845
  350.8 25.2 %collective-permute-start.61 = (bf16[2,256,1024]{2,1,0:T(8,128)(2,1)}, bf16[2,256,1024]{2,1,0:T(8,128)(2,1)}, u32[]{:S(2)}, u32[]{:S(2)}) collective-permute-start(bf16[2,256,1024]{2,1,0:T(8,128)(2,1)} %get-tuple-element.425), channel_id=1, source_target_pairs={{0,16},{4,20},{8,24},{12,28},{16,0},{20,4},{24,8},{28,12},{1,17},{... | collective-permute-start | bytes 3145736 | tf_op jit(solution)/shard_map/ppermute | solution.py:845
  399.0 27.3 %collective-permute-start.69 = (bf16[2,208,1024]{2,1,0:T(8,128)(2,1)}, bf16[2,208,1024]{2,1,0:T(8,128)(2,1)}, u32[]{:S(2)}, u32[]{:S(2)}) collective-permute-start(bf16[2,208,1024]{2,1,0:T(8,128)(2,1)} %add_convert_fusion.3), channel_id=1, source_target_pairs={{0,16},{4,20},{8,24},{12,28},{16,0},{20,4},{24,8},{28,12},{1,17},{... | collective-permute-start | bytes 2555912 | tf_op jit(solution)/shard_map/ppermute | solution.py:845
  402.0 24.3 %collective-permute-start.70 = (bf16[2,208,1024]{2,1,0:T(8,128)(2,1)S(1)}, bf16[2,208,1024]{2,1,0:T(8,128)(2,1)}, u32[]{:S(2)}, u32[]{:S(2)}) collective-permute-start(bf16[2,208,1024]{2,1,0:T(8,128)(2,1)S(1)} %add_convert_fusion.2), channel_id=1, source_target_pairs={{0,8},{4,12},{8,0},{12,4},{16,24},{20,28},{24,16},{28,20},{1,9},{5... | collective-permute-start | bytes 2555912 | tf_op jit(solution)/shard_map/ppermute | solution.py:845
  405.7 20.6 %collective-permute-start.68 = (bf16[256,1024]{1,0:T(8,128)(2,1)}, bf16[256,1024]{1,0:T(8,128)(2,1)}, u32[]{:S(2)}, u32[]{:S(2)}) collective-permute-start(bf16[256,1024]{1,0:T(8,128)(2,1)} %fusion.1), channel_id=1, source_target_pairs={{0,1},{1,2},{2,3},{3,0},{4,5},{5,6},{6,7},{7,4},{8,9},{9,10},{10,1... | collective-permute-start | bytes 1572872 | tf_op jit(solution)/shard_map/ppermute | solution.py:850
  431.5 21.3 %collective-permute-start.76 = (bf16[2,208,1024]{2,1,0:T(8,128)(2,1)}, bf16[2,208,1024]{2,1,0:T(8,128)(2,1)}, u32[]{:S(2)}, u32[]{:S(2)}) collective-permute-start(bf16[2,208,1024]{2,1,0:T(8,128)(2,1)} %get-tuple-element.488), channel_id=1, source_target_pairs={{0,8},{4,12},{8,0},{12,4},{16,24},{20,28},{24,16},{28,20},{1,9},{5... | collective-permute-start | bytes 2555912 | tf_op jit(solution)/shard_map/ppermute | solution.py:845
  433.0 21.0 %collective-permute-start.77 = (bf16[2,208,1024]{2,1,0:T(8,128)(2,1)}, bf16[2,208,1024]{2,1,0:T(8,128)(2,1)}, u32[]{:S(2)}, u32[]{:S(2)}) collective-permute-start(bf16[2,208,1024]{2,1,0:T(8,128)(2,1)} %get-tuple-element.489), channel_id=1, source_target_pairs={{0,16},{4,20},{8,24},{12,28},{16,0},{20,4},{24,8},{28,12},{1,17},{... | collective-permute-start | bytes 2555912 | tf_op jit(solution)/shard_map/ppermute | solution.py:845
  469.0 25.8 %collective-permute-start.85 = (bf16[2,144,1024]{2,1,0:T(8,128)(2,1)S(1)}, bf16[2,144,1024]{2,1,0:T(8,128)(2,1)S(1)}, u32[]{:S(2)}, u32[]{:S(2)}) collective-permute-start(bf16[2,144,1024]{2,1,0:T(8,128)(2,1)S(1)} %add_convert_fusion.5), channel_id=1, source_target_pairs={{0,16},{4,20},{8,24},{12,28},{16,0},{20,4},{24,8},{28,12},{1,17},{... | collective-permute-start | bytes 1769480 | tf_op jit(solution)/shard_map/ppermute | solution.py:845
  471.0 23.8 %collective-permute-start.84 = (bf16[2,144,1024]{2,1,0:T(8,128)(2,1)S(1)}, bf16[2,144,1024]{2,1,0:T(8,128)(2,1)S(1)}, u32[]{:S(2)}, u32[]{:S(2)}) collective-permute-start(bf16[2,144,1024]{2,1,0:T(8,128)(2,1)S(1)} %copy-done.92), channel_id=1, source_target_pairs={{0,16},{4,20},{8,24},{12,28},{16,0},{20,4},{24,8},{28,12},{1,17},{... | collective-permute-start | bytes 1769480 | tf_op jit(solution)/shard_map/ppermute | solution.py:845
  472.8 22.2 %collective-permute-start.86 = (bf16[2,144,1024]{2,1,0:T(8,128)(2,1)S(1)}, bf16[2,144,1024]{2,1,0:T(8,128)(2,1)S(1)}, u32[]{:S(2)}, u32[]{:S(2)}) collective-permute-start(bf16[2,144,1024]{2,1,0:T(8,128)(2,1)S(1)} %add_convert_fusion.4), channel_id=1, source_target_pairs={{0,8},{4,12},{8,0},{12,4},{16,24},{20,28},{24,16},{28,20},{1,9},{5... | collective-permute-start | bytes 1769480 | tf_op jit(solution)/shard_map/ppermute | solution.py:845
  (188 other events, 1896.3 us)

commit v5 on v4

--- a/solution.py
+++ b/solution.py
@@ -1522,12 +1522,8 @@
     else:
         enc_part = pair_rows(back_ck, back_cv, ckey_full, cvalue_full, ctx_count, slots * enc_rows)
     self_inputs = (bounds, positions[:, None], key_positions[None], probs, own)
-    part_one = self_backward(*self_inputs, back_o.reshape(slab), q, k, v, 0, 2)
     if paired:
-        late_x, late_y, *far_some, sent_cvalue, norm_send, enc_send, third_sum.folded[0], third_sum.folded[4], _ = tie(
-            *third_late, *far_some, sent_cvalue, norm_send, enc_send, third_sum.folded[0], third_sum.folded[4], part_one[0]
-        )
-        third_got = third_sum.first_hops(0)
+        *far_some, sent_cvalue, norm_send, enc_send = tie(*far_some, sent_cvalue, norm_send, enc_send)
         norm_shape = (4 * steps, 16, width)
         far_rest = far(sent_cvalue, norm_send.reshape(norm_shape), enc_send)
         second_sum.fold(
@@ -1535,14 +1531,12 @@
             [enc_keep, far_rest[2]],
             [norm_keep.reshape(norm_shape), far_rest[1]],
         )
-        *third_got, second_sum.folded[1], second_sum.folded[5] = tie(
-            *third_got, second_sum.folded[1], second_sum.folded[5]
+        late_x, late_y, third_sum.folded[0], third_sum.folded[4], _ = tie(
+            *third_late, third_sum.folded[0], third_sum.folded[4], second_sum.folded[0]
         )
-        third_sum.z_sums(*third_got, late_x, late_y)
-        hop = third_sum.z_step(1)
-        second_first = second_sum.first_hops(1)
-        back_o = after(back_o, second_sum.folded[1], third_sum.total)
-    back_q, back_k, back_v, back_e = self_backward(*self_inputs, back_o.reshape(slab), q, k, v, 1, 2, part_one)
+        third_got = third_sum.first_hops(0)
+        back_o = after(back_o, third_sum.folded[0])
+    back_q, back_k, back_v, back_e = self_backward(*self_inputs, back_o.reshape(slab), q, k, v, 0, 1)
     back_q = back_q.reshape(all_rows, width)
     back_e = back_e.reshape(all_rows, -1)
     back_k = back_k.reshape(-1, width)
@@ -1550,40 +1544,44 @@
 
     if paired:
         first_sum = reduction([(x_all, [back_q, back_e]), (keyed_flat, [back_k, back_v])], 0)
-        hop, got_x, got_y, back_q, back_k = tie(hop, *second_first, back_q, back_k)
-        hop = third_sum.z_step(2, hop)
-        second_sum.second_sums(got_x, got_y)
-        second_late = second_sum.second_hops()
-        back_q = after(back_q, third_sum.total, *second_sum.sums)
+        got_x, got_y, second_sum.folded[1], second_sum.folded[5], back_q, back_k = tie(
+            *third_got, second_sum.folded[1], second_sum.folded[5], back_q, back_k
+        )
+        third_sum.z_sums(got_x, got_y, late_x, late_y)
+        hop = third_sum.z_step(1)
+        second_first = second_sum.first_hops(1)
+        back_q = after(back_q, third_sum.total, second_sum.folded[1])
         *sent_first, main_keep, main_send, back_x = last_backward(
             x_all, keyed_flat, back_one, back_q, back_e, back_k, back_v, query_full, relative_full, key_full, value_full,
             core, steps, ctx_count,
         )
-        hop, late_x, late_y, main_send, second_sum.folded[0], second_sum.folded[4], *sent_first = tie(
-            hop, *second_late, main_send, second_sum.folded[0], second_sum.folded[4], *sent_first
-        )
+        hop, got_x, got_y, main_send, *sent_first = tie(hop, *second_first, main_send, *sent_first)
         far_keys, far_values, far_query, far_main = far(*sent_first[:3], main_send)
         far_embed, hop, far_keys = tie(*far(sent_first[3]), hop, far_keys)
-        hop = third_sum.z_step(3, hop)
-        second_got = second_sum.first_hops(0)
-        first_sum.fold([far_query, far_embed, far_keys, far_values], [main_keep, far_main], None, third_sum.total)
-        got_x, got_y, hop, first_sum.folded[1], first_sum.folded[5] = tie(
-            *second_got, hop, first_sum.folded[1], first_sum.folded[5]
+        hop = third_sum.z_step(2, hop)
+        second_sum.second_sums(got_x, got_y)
+        second_late = second_sum.second_hops()
+        first_sum.fold(
+            [far_query, far_embed, far_keys, far_values], [main_keep, far_main], None, third_sum.total, *second_sum.sums
+        )
+        hop, late_x, late_y, first_sum.folded[1], first_sum.folded[5], second_sum.folded[0], second_sum.folded[4] = tie(
+            hop, *second_late, first_sum.folded[1], first_sum.folded[5], second_sum.folded[0], second_sum.folded[4]
         )
         first_first = first_sum.first_hops(1)
+        second_got = second_sum.first_hops(0)
+        hop = third_sum.z_step(3, hop)
+        hop, got_x, got_y = tie(hop, *first_first)
         third_sum.z_end(hop)
+        first_sum.second_sums(got_x, got_y)
+        first_late = first_sum.second_hops()
+        got_x, got_y, third_sum.total, _ = tie(*second_got, third_sum.total, first_sum.sums[0])
         second_sum.z_sums(got_x, got_y, late_x, late_y)
         hop = second_sum.z_step(1)
-        hop, got_x, got_y = tie(hop, *first_first)
-        first_sum.second_sums(got_x, got_y)
-        first_late = first_sum.second_hops()
-        first_sum.folded[0], first_sum.folded[4], hop, _ = tie(
-            first_sum.folded[0], first_sum.folded[4], hop, first_sum.sums[0]
-        )
+        first_sum.folded[0], first_sum.folded[4], _ = tie(first_sum.folded[0], first_sum.folded[4], second_sum.total)
         first_got = first_sum.first_hops(0)
+        hop, *first_late = tie(hop, *first_late)
         hop = second_sum.z_step(2, hop)
-        hop, *rest, third_total = tie(hop, *first_got, *first_late, third_sum.total)
-        third_sum.total = third_total
+        hop, *rest, third_sum.total = tie(hop, *first_got, *first_late, third_sum.total)
         first_sum.z_sums(*rest)
         first_hop = first_sum.z_step(1)
         hop = second_sum.z_step(3, hop)

time: 575 us -> 574 us (level)
  Pallas kernels: 264 us -> 257 us
  waiting for transfers between devices: 171 us -> 177 us
    pallas_call x2 -> x1, Pallas kernels: 31.6 us -> 25.8 us  [self_backward(): pl.pallas_call(functools.partial(self_backward_kernel, len(made)), grid=(...]
  transfers between devices with their start and end apart: 118 -> 118, of which waited for: 49 -> 46; matrix products, arithmetic and copies ran while one was open for 7% -> 7% of each run, Pallas kernels for 35% -> 34%
where the time goes in v5:
time: 574 us; the launch traced here: 564 us
  Pallas kernels  257 us (45%)
  waiting for transfers between devices  177 us (31%)
  starting transfers between devices  74.6 us (13%)
  other arithmetic  28.2 us (5%)
  local copies, waits for them, and re-layouts  25.1 us (4%)
    ppermute x100, waiting for transfers between devices, ctx_hop(): return lax.ppermute(array, 'ctx', [(i, i ^ bit) for i in range(size)])  109 us
    ppermute x18, waiting for transfers between devices, z_hop(): lax.ppermute(array, 'fsdp', [(i, (i + step) % size) for i in range(size)])  67.8 us
    ppermute x100, starting transfers between devices, ctx_hop(): return lax.ppermute(array, 'ctx', [(i, i ^ bit) for i in range(size)])  59.7 us
    pallas_call x1, Pallas kernels, feed_forward_backward(): pl.pallas_call(functools.partial(feed_kernel, steps if sending else 0, (l...  42.5 us
    pallas_call x3, Pallas kernels, fold_grads(): pl.pallas_call(functools.partial(fold_grads_kernel, groups, steps, extra_...  38.2 us
    pallas_call x2, Pallas kernels, project(): pl.pallas_call(functools.partial(project_kernel, layout, copies, cut, ste...  29.3 us
    pallas_call x1, Pallas kernels, self_backward(): pl.pallas_call(functools.partial(self_backward_kernel, len(made)), grid=(...  25.8 us
    pallas_call x2, Pallas kernels, self_forward(): pl.pallas_call(functools.partial(self_forward_kernel, len(made), base), g...  24.1 us
  transfers between devices with their start and end apart: 118, of which 46 were waited for; matrix products, arithmetic and copies ran while one was open for 7% of the time, Pallas kernels for 34%

profile of v5, /device:TPU:0, one launch (start us, length us, event | category | flops | bytes accessed | tf_op | source)
XLA Modules:
  0.0 564.3 jit_solution(2647554458114974074)
XLA Ops:
  10.7 6.7 %collective-permute-done.refs_0_ = bf16[112,1024]{1,0:T(8,128)(2,1)S(1)} collective-permute-done((bf16[112,1024]{1,0:T(8,128)(2,1)}, bf16[112,1024]{1,0:T(8,128)(2,1)S(1)}, u32[]{:S(2)}, u32[]{:S(2)}) %collective-permute-start) | collective-permute-done | bytes 229408 | tf_op jit(solution)/shard_map/ppermute | solution.py:850
  22.7 7.1 %collective-permute-done.5.refs_1_ = bf16[112,1024]{1,0:T(8,128)(2,1)S(1)} collective-permute-done((bf16[112,1024]{1,0:T(8,128)(2,1)S(1)}, bf16[112,1024]{1,0:T(8,128)(2,1)S(1)}, u32[]{:S(2)}, u32[]{:S(2)}) %collective-permute-start.5) | collective-permute-done | bytes 229408 | tf_op jit(solution)/shard_map/ppermute | solution.py:850
  48.8 8.8 %collective-permute-done.15.refs_0_ = bf16[176,1024]{1,0:T(8,128)(2,1)S(1)} collective-permute-done((bf16[176,1024]{1,0:T(8,128)(2,1)}, bf16[176,1024]{1,0:T(8,128)(2,1)S(1)}, u32[]{:S(2)}, u32[]{:S(2)}) %collective-permute-start.15) | collective-permute-done | bytes 360480 | tf_op jit(solution)/shard_map/ppermute | solution.py:850
  64.7 7.8 %collective-permute-done.21.refs_16_ = bf16[3,48,1024]{2,1,0:T(8,128)(2,1)S(1)} collective-permute-done((bf16[3,48,1024]{2,1,0:T(8,128)(2,1)S(1)}, bf16[3,48,1024]{2,1,0:T(8,128)(2,1)S(1)}, u32[]{:S(2)}, u32[]{:S(2)}) %collective-permute-start.21) | collective-permute-done | bytes 294944 | tf_op jit(solution)/shard_map/ppermute | solution.py:845
  80.4 14.5 %project.2 = (bf16[384,1024]{1,0:T(8,128)(2,1)}, bf16[384,512]{1,0:T(8,128)(2,1)}, bf16[1280,1024]{1,0:T(8,128)(2,1)}, bf16[1280,1024]{1,0:T(8,128)(2,1)}, bf16[...) custom-call(s32[12]{0:T(128)} %stack.153.place_ref, ...), custom_call_target="tpu_custom_call" | custom-call | flops 1000 | bytes 1000 | tf_op jit(solution)/shard_map/project/pallas_call | solution.py:991
  99.8 12.0 %self_forward.2 = (bf16[3,2,64,1024]{3,2,1,0:T(8,128)(2,1)}, bf16[2,16,192,512]{3,2,1,0:T(8,128)(2,1)}, f32[2,4,192,128]{3,2,1,0:T(8,128)}) custom-call(s32[2]{0:T(128)} %length_ref.4, s32[33]{0:T(128)} %convert_reduce_fusion.bounds_ref, s32[64,1]{1,0:T(8,128)} %copy.56.posq_ref, s32[1,512]{1,0:T(1,128)} %bitcast.208, bf16[3,2,64,1024]{3,2,1,0:T(8,128)(2,1)} %bitcast.171, ...), custom_call_target="tpu_custom_call" | custom-call | flops 1000 | bytes 1000 | tf_op jit(solution)/shard_map/self_forward/pallas_call | solution.py:405
  114.2 12.1 %self_forward.3 = (bf16[3,2,64,1024]{3,2,1,0:T(8,128)(2,1)}, bf16[2,16,192,512]{3,2,1,0:T(8,128)(2,1)}, f32[2,4,192,128]{3,2,1,0:T(8,128)}) custom-call(s32[2]{0:T(128)} %length_ref.4, s32[33]{0:T(128)} %convert_reduce_fusion.bounds_ref, s32[64,1]{1,0:T(8,128)} %copy.56.posq_ref, ...), custom_call_target="tpu_custom_call", output_to_operand_aliasing={{0}: (8, {}), {1}: (9, {}), {2}: (10, {})} | custom-call | flops 1000 | bytes 1000 | tf_op jit(solution)/shard_map/self_forward/pallas_call | solution.py:405
  134.4 11.5 %collective-permute-done.35.refs_18_ = bf16[3,80,1024]{2,1,0:T(8,128)(2,1)S(1)} collective-permute-done((bf16[3,80,1024]{2,1,0:T(8,128)(2,1)S(1)}, bf16[3,80,1024]{2,1,0:T(8,128)(2,1)S(1)}, u32[]{:S(2)}, u32[]{:S(2)}) %collective-permute-start.35) | collective-permute-done | bytes 491552 | tf_op jit(solution)/shard_map/ppermute | solution.py:845
  159.6 14.8 %project.3 = (bf16[1024,1024]{1,0:T(8,128)(2,1)}, bf16[1024,1024]{1,0:T(8,128)(2,1)}, bf16[1024,1024]{1,0:T(8,128)(2,1)}, bf16[1024,1024]{1,0:T(8,128)(2,1)}, bf...) custom-call(s32[12]{0:T(128)} %stack.153.place_ref, ...), custom_call_target="tpu_custom_call" | custom-call | flops 1000 | bytes 1000 | tf_op jit(solution)/shard_map/project/pallas_call | solution.py:991
  174.4 7.0 %query_rows.1 = (f32[384,1024]{1,0:T(8,128)}, f32[384,1024]{1,0:T(8,128)}, f32[384,1]{1,0:T(8,128)}, bf16[384,1024]{1,0:T(8,128)(2,1)}, bf16[384,1024]{1,0:T(8,128)(2,1)}, /*index=5*/f32[16,1024]{1,0:T(8,128)}) custom-call(bf16[384,1024]{1,0:T(8,128)(2,1)} %bitcast.153, bf16[384,1024]{1,0:T(8,128)(2,1)} %bitcast.156, ...), custom_call_target="tpu_custom_call" | custom-call | flops 1000 | bytes 1000 | tf_op jit(solution)/shard_map/query_rows/pallas_call | solution.py:1038
  181.4 11.8 %cross_forward.1 = (bf16[3,2,64,1024]{3,2,1,0:T(8,128)(2,1)}, bf16[2,16,192,512]{3,2,1,0:T(8,128)(2,1)}) custom-call(s32[2]{0:T(128)} %length_ref.5, s32[1,512]{1,0:T(1,128)} %add.322.posk_ref, bf16[3,2,64,1024]{3,2,1,0:T(8,128)(2,1)} %bitcast.180, bf16[8,2,64,1024]{3,2,1,0:T(8,128)(2,1)} %bitcast.163, bf16[8,2,64,1024]{3,2,1,0:T(8,128)(2,1)} %bitcast.165), custom_call_target="tpu_custom_call" | custom-call | flops 1000 | bytes 1000 | tf_op jit(solution)/shard_map/cross_forward/pallas_call | solution.py:483
  198.3 17.6 %collective-permute-done.43.refs_5_ = bf16[3,128,1024]{2,1,0:T(8,128)(2,1)S(1)} collective-permute-done((bf16[3,128,1024]{2,1,0:T(8,128)(2,1)S(1)}, bf16[3,128,1024]{2,1,0:T(8,128)(2,1)S(1)}, u32[]{:S(2)}, u32[]{:S(2)}) %collective-permute-start.43) | collective-permute-done | bytes 786464 | tf_op jit(solution)/shard_map/ppermute | solution.py:845
  221.4 42.5 %feed.1 = (bf16[384,1024]{1,0:T(8,128)(2,1)}, bf16[384,1024]{1,0:T(8,128)(2,1)}, bf16[384,4096]{1,0:T(8,128)(2,1)}, bf16[384,4096]{1,0:T(8,128)(2,1)}, bf16[384,...) custom-call(s32[13]{0:T(128)} %concatenate.24.core_ref, ...), custom_call_target="tpu_custom_call" | custom-call | flops 1000 | bytes 1000 | tf_op jit(solution)/shard_map/feed/pallas_call | solution.py:647
  265.3 13.6 %cross_backward.1 = (bf16[3,2,64,1024]{3,2,1,0:T(8,128)(2,1)}, bf16[8,2,64,1024]{3,2,1,0:T(8,128)(2,1)}, bf16[8,2,64,1024]{3,2,1,0:T(8,128)(2,1)}) custom-call(bf16[2,16,192,512]{3,2,1,0:T(8,128)(2,1)} %get-tuple-element.371.p_ref, bf16[3,2,64,1024]{3,2,1,0:T(8,128)(2,1)} %bitcast.200, bf16[3,2,64,1024]{3,2,1,0:T(8,128)(2,1)} %bitcast.181, ...), custom_call_target="tpu_custom_call" | custom-call | flops 1000 | bytes 1000 | tf_op jit(solution)/shard_map/cross_backward/pallas_call | solution.py:500
  279.0 13.4 %fold_grads.3 = (bf16[2,256,1024]{2,1,0:T(8,128)(2,1)}, bf16[2,256,1024]{2,1,0:T(8,128)(2,1)}, bf16[2,256,1024]{2,1,0:T(8,128)(2,1)}, bf16[2,256,1024]{2,1,0:T(8...) custom-call(s32[3]{0:T(128)} %pad_add_fusion.1.place_ref, ...), custom_call_target="tpu_custom_call" | custom-call | flops 1000 | bytes 1000 | tf_op jit(solution)/shard_map/fold_grads/pallas_call | solution.py:1194
  293.5 21.3 %middle_backward.1 = (f32[384,1024]{1,0:T(8,128)}, bf16[384,1024]{1,0:T(8,128)(2,1)}, bf16[384,1024]{1,0:T(8,128)(2,1)}, f32[2,1024]{1,0:T(2,128)}, bf16[512,102...) custom-call(s32[1]{0:T(128)} %bitcast.core_ref, ...), custom_call_target="tpu_custom_call" | custom-call | flops 1000 | bytes 1000 | tf_op jit(solution)/shard_map/middle_backward/pallas_call | solution.py:745
  330.6 13.2 %fold_grads.4 = (bf16[2,208,1024]{2,1,0:T(8,128)(2,1)}, bf16[2,208,1024]{2,1,0:T(8,128)(2,1)}, bf16[2,208,1024]{2,1,0:T(8,128)(2,1)}, bf16[2,208,1024]{2,1,0:T(8...) custom-call(s32[3]{0:T(128)} %pad_add_fusion.1.place_ref, ...), custom_call_target="tpu_custom_call" | custom-call | flops 1000 | bytes 1000 | tf_op jit(solution)/shard_map/fold_grads/pallas_call | solution.py:1194
  354.9 25.8 %self_backward.1 = (bf16[3,2,64,1024]{3,2,1,0:T(8,128)(2,1)}, bf16[10,2,64,1024]{3,2,1,0:T(8,128)(2,1)}, bf16[10,2,64,1024]{3,2,1,0:T(8,128)(2,1)}, bf16[3,2,64,512]{3,2,1,0:T(8,128)(2,1)}) custom-call(s32[33]{0:T(128)} %convert_reduce_fusion.bounds_ref, s32[64,1]{1,0:T(8,128)} %copy.56.posq_ref, s32[1,512]{1,0:T(1,128)} %bitcast.210, ...), custom_call_target="tpu_custom_call" | custom-call | flops 1000 | bytes 1000 | tf_op jit(solution)/shard_map/self_backward/pallas_call | solution.py:446
  386.0 19.0 %last_backward.1 = (bf16[512,1024]{1,0:T(8,128)(2,1)}, bf16[512,1024]{1,0:T(8,128)(2,1)}, bf16[512,1024]{1,0:T(8,128)(2,1)}, bf16[512,512]{1,0:T(8,128)(2,1)}, b...) custom-call(s32[1]{0:T(128)} %bitcast.core_ref, bf16[384,1024]{1,0:T(8,128)(2,1)} %bitcast.154, ...), custom_call_target="tpu_custom_call" | custom-call | flops 1000 | bytes 1000 | tf_op jit(solution)/shard_map/last_backward/pallas_call | solution.py:824
  416.5 11.7 %fold_grads.5 = (bf16[2,144,1024]{2,1,0:T(8,128)(2,1)}, bf16[2,144,1024]{2,1,0:T(8,128)(2,1)}, bf16[2,144,1024]{2,1,0:T(8,128)(2,1)}, bf16[2,144,1024]{2,1,0:T(8...) custom-call(s32[3]{0:T(128)} %pad_add_fusion.1.place_ref, ...), custom_call_target="tpu_custom_call" | custom-call | flops 1000 | bytes 1000 | tf_op jit(solution)/shard_map/fold_grads/pallas_call | solution.py:1194
  439.6 11.4 %collective-permute-done.78 = bf16[256,1024]{1,0:T(8,128)(2,1)S(1)} collective-permute-done((bf16[256,1024]{1,0:T(8,128)(2,1)S(1)}, bf16[256,1024]{1,0:T(8,128)(2,1)S(1)}, u32[]{:S(2)}, u32[]{:S(2)}) %collective-permute-start.78) | collective-permute-done | bytes 524320 | tf_op jit(solution)/shard_map/ppermute | solution.py:850
  454.7 12.1 %collective-permute-done.76 = bf16[2,208,1024]{2,1,0:T(8,128)(2,1)S(1)} collective-permute-done((bf16[2,208,1024]{2,1,0:T(8,128)(2,1)S(1)}, bf16[2,208,1024]{2,1,0:T(8,128)(2,1)S(1)}, u32[]{:S(2)}, u32[]{:S(2)}) %collective-permute-start.76) | collective-permute-done | bytes 852000 | tf_op jit(solution)/shard_map/ppermute | solution.py:845
  482.6 7.8 %collective-permute-done.85 = bf16[2,144,1024]{2,1,0:T(8,128)(2,1)S(1)} collective-permute-done((bf16[2,144,1024]{2,1,0:T(8,128)(2,1)S(1)}, bf16[2,144,1024]{2,1,0:T(8,128)(2,1)S(1)}, u32[]{:S(2)}, u32[]{:S(2)}) %collective-permute-start.85) | collective-permute-done | bytes 589856 | tf_op jit(solution)/shard_map/ppermute | solution.py:845
  496.8 7.8 %collective-permute-done.88 = bf16[112,1024]{1,0:T(8,128)(2,1)S(1)} collective-permute-done((bf16[112,1024]{1,0:T(8,128)(2,1)S(1)}, bf16[112,1024]{1,0:T(8,128)(2,1)S(1)}, u32[]{:S(2)}, u32[]{:S(2)}) %collective-permute-start.88) | collective-permute-done | bytes 229408 | tf_op jit(solution)/shard_map/ppermute | solution.py:850
  (513 shorter events, 230.5 us)
Async XLA Ops:
  74.8 20.2 %collective-permute-start.25 = (bf16[176,1024]{1,0:T(8,128)(2,1)}, bf16[176,1024]{1,0:T(8,128)(2,1)}, u32[]{:S(2)}, u32[]{:S(2)}) collective-permute-start(bf16[176,1024]{1,0:T(8,128)(2,1)} %collective-permute-done.20.refs_1_), channel_id=1, source_target_pairs={{0,1},{1,2},{2,3},{3,0},{4,5},{5,6},{6,7},{7,4},{8,9},{9,10},{10,1... | collective-permute-start | bytes 1081352 | tf_op jit(solution)/shard_map/ppermute | solution.py:850
  97.2 31.6 %collective-permute-start.32 = (bf16[3,176,1024]{2,1,0:T(8,128)(2,1)}, bf16[3,176,1024]{2,1,0:T(8,128)(2,1)}, u32[]{:S(2)}, u32[]{:S(2)}) collective-permute-start(bf16[3,176,1024]{2,1,0:T(8,128)(2,1)} %stack_rows.4.refs_14_), channel_id=1, source_target_pairs={{0,16},{4,20},{8,24},{12,28},{16,0},{20,4},{24,8},{28,12},{1,17},{... | collective-permute-start | bytes 3244040 | tf_op jit(solution)/shard_map/ppermute | solution.py:845
  97.7 31.0 %collective-permute-start.31 = (bf16[3,176,1024]{2,1,0:T(8,128)(2,1)}, bf16[3,176,1024]{2,1,0:T(8,128)(2,1)}, u32[]{:S(2)}, u32[]{:S(2)}) collective-permute-start(bf16[3,176,1024]{2,1,0:T(8,128)(2,1)} %stack_rows.4.refs_14_), channel_id=1, source_target_pairs={{0,8},{4,12},{8,0},{12,4},{16,24},{20,28},{24,16},{28,20},{1,9},{5... | collective-permute-start | bytes 3244040 | tf_op jit(solution)/shard_map/ppermute | solution.py:845
  114.2 20.1 %collective-permute-start.36 = (bf16[3,176,1024]{2,1,0:T(8,128)(2,1)}, bf16[3,176,1024]{2,1,0:T(8,128)(2,1)}, u32[]{:S(2)}, u32[]{:S(2)}) collective-permute-start(bf16[3,176,1024]{2,1,0:T(8,128)(2,1)} %stack_rows.4.refs_14_), channel_id=1, source_target_pairs={{0,4},{4,0},{8,12},{12,8},{16,20},{20,16},{24,28},{28,24},{1,5},{5... | collective-permute-start | bytes 3244040 | tf_op jit(solution)/shard_map/ppermute | solution.py:845
  154.4 38.8 %collective-permute-start.42 = (bf16[3,256,1024]{2,1,0:T(8,128)(2,1)}, bf16[3,256,1024]{2,1,0:T(8,128)(2,1)}, u32[]{:S(2)}, u32[]{:S(2)}) collective-permute-start(bf16[3,256,1024]{2,1,0:T(8,128)(2,1)} %stack_rows.5.refs_2_), channel_id=1, source_target_pairs={{0,16},{4,20},{8,24},{12,28},{16,0},{20,4},{24,8},{28,12},{1,17},{... | collective-permute-start | bytes 4718600 | tf_op jit(solution)/shard_map/ppermute | solution.py:845
  156.0 37.2 %collective-permute-start.41 = (bf16[3,256,1024]{2,1,0:T(8,128)(2,1)}, bf16[3,256,1024]{2,1,0:T(8,128)(2,1)}, u32[]{:S(2)}, u32[]{:S(2)}) collective-permute-start(bf16[3,256,1024]{2,1,0:T(8,128)(2,1)} %stack_rows.5.refs_2_), channel_id=1, source_target_pairs={{0,8},{4,12},{8,0},{12,4},{16,24},{20,28},{24,16},{28,20},{1,9},{5... | collective-permute-start | bytes 4718600 | tf_op jit(solution)/shard_map/ppermute | solution.py:845
  157.4 40.9 %collective-permute-start.45 = (bf16[3,256,1024]{2,1,0:T(8,128)(2,1)}, bf16[3,256,1024]{2,1,0:T(8,128)(2,1)}, u32[]{:S(2)}, u32[]{:S(2)}) collective-permute-start(bf16[3,256,1024]{2,1,0:T(8,128)(2,1)} %stack_rows.5.refs_2_), channel_id=1, source_target_pairs={{0,4},{4,0},{8,12},{12,8},{16,20},{20,16},{24,28},{28,24},{1,5},{5... | collective-permute-start | bytes 4718600 | tf_op jit(solution)/shard_map/ppermute | solution.py:845
  193.2 23.8 %collective-permute-start.46 = (bf16[3,256,1024]{2,1,0:T(8,128)(2,1)}, bf16[3,256,1024]{2,1,0:T(8,128)(2,1)}, u32[]{:S(2)}, u32[]{:S(2)}) collective-permute-start(bf16[3,256,1024]{2,1,0:T(8,128)(2,1)} %collective-permute-done.41.refs_3_), channel_id=1, source_target_pairs={{0,4},{4,0},{8,12},{12,8},{16,20},{20,16},{24,28},{28,24},{1,5},{5... | collective-permute-start | bytes 4718600 | tf_op jit(solution)/shard_map/ppermute | solution.py:845
  193.5 23.6 %collective-permute-start.47 = (bf16[3,256,1024]{2,1,0:T(8,128)(2,1)}, bf16[3,256,1024]{2,1,0:T(8,128)(2,1)}, u32[]{:S(2)}, u32[]{:S(2)}) collective-permute-start(bf16[3,256,1024]{2,1,0:T(8,128)(2,1)} %collective-permute-done.42.refs_4_), channel_id=1, source_target_pairs={{0,4},{4,0},{8,12},{12,8},{16,20},{20,16},{24,28},{28,24},{1,5},{5... | collective-permute-start | bytes 4718600 | tf_op jit(solution)/shard_map/ppermute | solution.py:845
  292.4 25.7 %collective-permute-start.53 = (bf16[2,256,1024]{2,1,0:T(8,128)(2,1)}, bf16[2,256,1024]{2,1,0:T(8,128)(2,1)}, u32[]{:S(2)}, u32[]{:S(2)}) collective-permute-start(bf16[2,256,1024]{2,1,0:T(8,128)(2,1)} %get-tuple-element.384), channel_id=1, source_target_pairs={{0,8},{4,12},{8,0},{12,4},{16,24},{20,28},{24,16},{28,20},{1,9},{5... | collective-permute-start | bytes 3145736 | tf_op jit(solution)/shard_map/ppermute | solution.py:845
  293.0 25.3 %collective-permute-start.54 = (bf16[2,256,1024]{2,1,0:T(8,128)(2,1)}, bf16[2,256,1024]{2,1,0:T(8,128)(2,1)}, u32[]{:S(2)}, u32[]{:S(2)}) collective-permute-start(bf16[2,256,1024]{2,1,0:T(8,128)(2,1)} %get-tuple-element.385), channel_id=1, source_target_pairs={{0,16},{4,20},{8,24},{12,28},{16,0},{20,4},{24,8},{28,12},{1,17},{... | collective-permute-start | bytes 3145736 | tf_op jit(solution)/shard_map/ppermute | solution.py:845
  321.8 25.9 %collective-permute-start.56 = (bf16[2,256,1024]{2,1,0:T(8,128)(2,1)}, bf16[2,256,1024]{2,1,0:T(8,128)(2,1)}, u32[]{:S(2)}, u32[]{:S(2)}) collective-permute-start(bf16[2,256,1024]{2,1,0:T(8,128)(2,1)} %add_convert_fusion), channel_id=1, source_target_pairs={{0,8},{4,12},{8,0},{12,4},{16,24},{20,28},{24,16},{28,20},{1,9},{5... | collective-permute-start | bytes 3145736 | tf_op jit(solution)/shard_map/ppermute | solution.py:845
  327.4 25.5 %collective-permute-start.55 = (bf16[2,256,1024]{2,1,0:T(8,128)(2,1)}, bf16[2,256,1024]{2,1,0:T(8,128)(2,1)}, u32[]{:S(2)}, u32[]{:S(2)}) collective-permute-start(bf16[2,256,1024]{2,1,0:T(8,128)(2,1)} %add_convert_fusion.1), channel_id=1, source_target_pairs={{0,16},{4,20},{8,24},{12,28},{16,0},{20,4},{24,8},{28,12},{1,17},{... | collective-permute-start | bytes 3145736 | tf_op jit(solution)/shard_map/ppermute | solution.py:845
  352.9 27.8 %collective-permute-start.64 = (bf16[2,256,1024]{2,1,0:T(8,128)(2,1)}, bf16[2,256,1024]{2,1,0:T(8,128)(2,1)}, u32[]{:S(2)}, u32[]{:S(2)}) collective-permute-start(bf16[2,256,1024]{2,1,0:T(8,128)(2,1)} %get-tuple-element.430), channel_id=1, source_target_pairs={{0,16},{4,20},{8,24},{12,28},{16,0},{20,4},{24,8},{28,12},{1,17},{... | collective-permute-start | bytes 3145736 | tf_op jit(solution)/shard_map/ppermute | solution.py:845
  353.4 27.3 %collective-permute-start.63 = (bf16[2,256,1024]{2,1,0:T(8,128)(2,1)}, bf16[2,256,1024]{2,1,0:T(8,128)(2,1)}, u32[]{:S(2)}, u32[]{:S(2)}) collective-permute-start(bf16[2,256,1024]{2,1,0:T(8,128)(2,1)} %get-tuple-element.429), channel_id=1, source_target_pairs={{0,8},{4,12},{8,0},{12,4},{16,24},{20,28},{24,16},{28,20},{1,9},{5... | collective-permute-start | bytes 3145736 | tf_op jit(solution)/shard_map/ppermute | solution.py:845
  380.7 24.3 %collective-permute-start.67 = (bf16[2,208,1024]{2,1,0:T(8,128)(2,1)}, bf16[2,208,1024]{2,1,0:T(8,128)(2,1)}, u32[]{:S(2)}, u32[]{:S(2)}) collective-permute-start(bf16[2,208,1024]{2,1,0:T(8,128)(2,1)} %get-tuple-element.443), channel_id=1, source_target_pairs={{0,16},{4,20},{8,24},{12,28},{16,0},{20,4},{24,8},{28,12},{1,17},{... | collective-permute-start | bytes 2555912 | tf_op jit(solution)/shard_map/ppermute | solution.py:845
  382.3 22.7 %collective-permute-start.66 = (bf16[2,208,1024]{2,1,0:T(8,128)(2,1)}, bf16[2,208,1024]{2,1,0:T(8,128)(2,1)}, u32[]{:S(2)}, u32[]{:S(2)}) collective-permute-start(bf16[2,208,1024]{2,1,0:T(8,128)(2,1)} %get-tuple-element.442), channel_id=1, source_target_pairs={{0,8},{4,12},{8,0},{12,4},{16,24},{20,28},{24,16},{28,20},{1,9},{5... | collective-permute-start | bytes 2555912 | tf_op jit(solution)/shard_map/ppermute | solution.py:845
  385.3 19.7 %collective-permute-start.65 = (bf16[256,1024]{1,0:T(8,128)(2,1)}, bf16[256,1024]{1,0:T(8,128)(2,1)}, u32[]{:S(2)}, u32[]{:S(2)}) collective-permute-start(bf16[256,1024]{1,0:T(8,128)(2,1)} %fusion.9), channel_id=1, source_target_pairs={{0,1},{1,2},{2,3},{3,0},{4,5},{5,6},{6,7},{7,4},{8,9},{9,10},{10,1... | collective-permute-start | bytes 1572872 | tf_op jit(solution)/shard_map/ppermute | solution.py:850
  410.2 21.5 %collective-permute-start.74 = (bf16[2,208,1024]{2,1,0:T(8,128)(2,1)S(1)}, bf16[2,208,1024]{2,1,0:T(8,128)(2,1)}, u32[]{:S(2)}, u32[]{:S(2)}) collective-permute-start(bf16[2,208,1024]{2,1,0:T(8,128)(2,1)S(1)} %add_convert_fusion.3), channel_id=1, source_target_pairs={{0,16},{4,20},{8,24},{12,28},{16,0},{20,4},{24,8},{28,12},{1,17},{... | collective-permute-start | bytes 2555912 | tf_op jit(solution)/shard_map/ppermute | solution.py:845
  410.7 21.3 %collective-permute-start.75 = (bf16[2,208,1024]{2,1,0:T(8,128)(2,1)}, bf16[2,208,1024]{2,1,0:T(8,128)(2,1)}, u32[]{:S(2)}, u32[]{:S(2)}) collective-permute-start(bf16[2,208,1024]{2,1,0:T(8,128)(2,1)} %add_convert_fusion.2), channel_id=1, source_target_pairs={{0,8},{4,12},{8,0},{12,4},{16,24},{20,28},{24,16},{28,20},{1,9},{5... | collective-permute-start | bytes 2555912 | tf_op jit(solution)/shard_map/ppermute | solution.py:845
  438.6 28.2 %collective-permute-start.76 = (bf16[2,208,1024]{2,1,0:T(8,128)(2,1)S(1)}, bf16[2,208,1024]{2,1,0:T(8,128)(2,1)S(1)}, u32[]{:S(2)}, u32[]{:S(2)}) collective-permute-start(bf16[2,208,1024]{2,1,0:T(8,128)(2,1)S(1)} %copy-done.93), channel_id=1, source_target_pairs={{0,8},{4,12},{8,0},{12,4},{16,24},{20,28},{24,16},{28,20},{1,9},{5... | collective-permute-start | bytes 2555912 | tf_op jit(solution)/shard_map/ppermute | solution.py:845
  439.1 28.7 %collective-permute-start.77 = (bf16[2,208,1024]{2,1,0:T(8,128)(2,1)S(1)}, bf16[2,208,1024]{2,1,0:T(8,128)(2,1)S(1)}, u32[]{:S(2)}, u32[]{:S(2)}) collective-permute-start(bf16[2,208,1024]{2,1,0:T(8,128)(2,1)S(1)} %copy-done.92), channel_id=1, source_target_pairs={{0,16},{4,20},{8,24},{12,28},{16,0},{20,4},{24,8},{28,12},{1,17},{... | collective-permute-start | bytes 2555912 | tf_op jit(solution)/shard_map/ppermute | solution.py:845
  451.3 29.2 %collective-permute-start.82 = (bf16[2,144,1024]{2,1,0:T(8,128)(2,1)S(1)}, bf16[2,144,1024]{2,1,0:T(8,128)(2,1)S(1)}, u32[]{:S(2)}, u32[]{:S(2)}) collective-permute-start(bf16[2,144,1024]{2,1,0:T(8,128)(2,1)S(1)} %add_convert_fusion.5), channel_id=1, source_target_pairs={{0,16},{4,20},{8,24},{12,28},{16,0},{20,4},{24,8},{28,12},{1,17},{... | collective-permute-start | bytes 1769480 | tf_op jit(solution)/shard_map/ppermute | solution.py:845
  452.1 28.4 %collective-permute-start.83 = (bf16[2,144,1024]{2,1,0:T(8,128)(2,1)S(1)}, bf16[2,144,1024]{2,1,0:T(8,128)(2,1)S(1)}, u32[]{:S(2)}, u32[]{:S(2)}) collective-permute-start(bf16[2,144,1024]{2,1,0:T(8,128)(2,1)S(1)} %add_convert_fusion.4), channel_id=1, source_target_pairs={{0,8},{4,12},{8,0},{12,4},{16,24},{20,28},{24,16},{28,20},{1,9},{5... | collective-permute-start | bytes 1769480 | tf_op jit(solution)/shard_map/ppermute | solution.py:845
  (191 other events, 1932.6 us)
